TPU v7x, 256 devices: a whole 4x4x8 slice. The times are simulated.
256 devices in a mesh: dp: 32 (over z, y), row: 2 (over core), col: 4 (over x).
Axes of the slice: x: 4, y: 4, z: 8, core: 2. Of those that a mesh axis runs over, the one named last changes fastest.
Arguments:
- x_input: bfloat16 [32, 32, 64, 640], P('dp', 'row', 'col'), may hold values from -6 to 6
- pre_act: bfloat16 [32, 32, 64, 640], P('dp', 'row', 'col'), may hold values from -6 to 6
- out_grad: bfloat16 [32, 32, 64, 640], P('dp', 'row', 'col'), may hold values from -0.15625 to 0.15625
- conv_weight: bfloat16 [3, 3, 640, 640], replicated, may hold values from -0.078125 to 0.078125
- q_prev: float32 [5760, 2, 64], replicated, may hold values from -6 to 6
Outputs:
- p_basis: float32 [640, 2, 64], P('dp')
- q_next: float32 [5760, 2, 64], P('dp')
All inputs are finite; a program needn't handle non-finite values.
Results may differ from a plain program's by a relative error of at most 0.0036.
Values may be sent and summed in bfloat16 or wider, within the bound.
A program may use at most 128 MiB of HBM per device.

v0:
```python
import functools
import math

import jax
import jax.numpy as jnp
from jax import lax
from jax.experimental import pallas as pl
from jax.experimental.pallas import tpu as pltpu
from jax.sharding import PartitionSpec as P


def member_coords(j, axes, sizes):
    coords = {}
    for axis in reversed(axes):
        coords[axis] = lax.rem(j, sizes[axis])
        j = j // sizes[axis]
    return coords


def exchange_kernel(x_ref, o_ref, send_sem, recv_sem, local_sem, *, axes, sizes, gather, chunks):
    n = math.prod(sizes[a] for a in axes)
    me = 0
    for axis in axes:
        me = me * sizes[axis] + lax.axis_index(axis)
    step = o_ref.shape[1] // chunks
    barrier = pltpu.get_barrier_semaphore()
    for s in range(1, n):
        peer = member_coords(lax.rem(me + s, n), axes, sizes)
        pl.semaphore_signal(barrier, inc=1, device_id=peer, device_id_type=pl.DeviceIdType.MESH)
    pl.semaphore_wait(barrier, n - 1)

    def source(index, part):
        rows = pl.ds(part * step, step)
        return x_ref.at[rows] if gather else x_ref.at[index, rows]

    copies = []
    for s in range(1, n):
        dst = lax.rem(me + s, n)
        for part in range(chunks):
            copy = pltpu.make_async_remote_copy(
                src_ref=source(dst, part),
                dst_ref=o_ref.at[me, pl.ds(part * step, step)],
                send_sem=send_sem.at[s - 1, part],
                recv_sem=recv_sem.at[s - 1, part],
                device_id=member_coords(dst, axes, sizes),
                device_id_type=pl.DeviceIdType.MESH,
            )
            copy.start()
            copies.append(copy)
    local = pltpu.make_async_copy(x_ref if gather else x_ref.at[me], o_ref.at[me], local_sem)
    local.start()
    for copy in copies:
        copy.wait_send()
        copy.wait_recv()
    local.wait()


def exchange(x, axes, sizes, cid, gather=False):
    n = math.prod(sizes[a] for a in axes)
    slab = x.shape if gather else x.shape[1:]
    slab_bytes = math.prod(slab) * x.dtype.itemsize
    chunks = 1
    while chunks < 8 and slab[0] % (chunks * 2) == 0 and slab_bytes // (chunks * 2) >= 96 * 1024:
        chunks *= 2
    return pl.pallas_call(
        functools.partial(exchange_kernel, axes=axes, sizes=sizes, gather=gather, chunks=chunks),
        out_shape=jax.ShapeDtypeStruct((n,) + slab, x.dtype),
        in_specs=[pl.BlockSpec(memory_space=pl.ANY)],
        out_specs=pl.BlockSpec(memory_space=pl.ANY),
        scratch_shapes=[
            pltpu.SemaphoreType.DMA((max(n - 1, 1), chunks)),
            pltpu.SemaphoreType.DMA((max(n - 1, 1), chunks)),
            pltpu.SemaphoreType.DMA,
        ],
        compiler_params=pltpu.CompilerParams(collective_id=cid, has_side_effects=True),
    )(x)


def padded_2(value, sides, width):
    for axis, dim in sides:
        size, length = (lax.axis_size(axis), value.shape[dim])
        up = [(i, (i + 1) % size) for i in range(size - 1)]
        down = [(j, i) for i, j in up]
        last = lax.slice_in_dim(value, length - width, length, axis=dim)
        leading = lax.slice_in_dim(value, 0, width, axis=dim)
        before = lax.ppermute(last, axis, up)
        after = lax.ppermute(leading, axis, down)
        value = jnp.concatenate([before, value, after], axis=dim)
    return value


def silu_slope(pre_float):
    sigma = jax.nn.sigmoid(pre_float)
    return sigma * (1.0 + pre_float * (1.0 - sigma))


def exact_dot(left, right, contract):
    return lax.dot_general(
        left.astype(jnp.float32),
        right.astype(jnp.float32),
        (contract, ((), ())),
        precision=lax.Precision.HIGHEST,
        preferred_element_type=jnp.float32,
    )


TAPS = [(a, b) for a in (-1, 0, 1) for b in (-1, 0, 1)]


def on_device(x_input, pre_act, out_grad, conv_weight, q_prev, sizes):
    height, breadth, channels = (x_input.shape[1], x_input.shape[2], x_input.shape[3])
    pixels = height * breadth
    rank = q_prev.shape[2]
    taps = len(TAPS)
    sides = (("row", 0), ("col", 1))
    pre_float = pre_act.reshape(pixels, channels).astype(jnp.float32)
    hidden = jax.nn.silu(pre_float).astype(jnp.bfloat16)
    grad_pad = padded_2(out_grad.reshape(height, breadth, channels), sides, 1)
    input_pad = padded_2(x_input.reshape(height, breadth, channels), sides, 1)
    back_grad = jnp.zeros((pixels, channels), jnp.float32)
    for a, b in TAPS:
        window = grad_pad[1 - a : 1 - a + height, 1 - b : 1 - b + breadth].reshape(pixels, channels)
        back_grad = back_grad + lax.dot_general(
            window, conv_weight[a + 1, b + 1], (((1,), (1,)), ((), ())), preferred_element_type=jnp.float32
        )
    pre_grad = (back_grad * silu_slope(pre_float)).astype(jnp.bfloat16)

    grid = (height + 2, breadth + 2)
    grad_flat = grad_pad.reshape(-1, channels)
    input_flat = input_pad.reshape(-1, channels)
    q_taps = q_prev.reshape(taps, channels, 2, rank).transpose(2, 1, 0, 3).reshape(2, channels, taps * rank)

    first_terms = exact_dot(input_flat, q_taps[0], ((1,), (0,))).reshape(grid + (taps, rank))
    first_sum = sum(
        first_terms[1 + a : 1 + a + height, 1 + b : 1 + b + breadth, k] for k, (a, b) in enumerate(TAPS)
    ).reshape(pixels, rank)
    first_raw = exact_dot(pre_grad, first_sum, ((0,), (0,)))
    second_terms = exact_dot(hidden, q_taps[1], ((1,), (0,))).reshape(height, breadth, taps, rank)
    second_sum = sum(
        jnp.pad(second_terms[:, :, k], ((1 - a, 1 + a), (1 - b, 1 + b), (0, 0))) for k, (a, b) in enumerate(TAPS)
    ).reshape(-1, rank)
    second_raw = exact_dot(grad_flat, second_sum, ((0,), (0,)))

    power_raw = all_sum_small(jnp.stack([first_raw, second_raw], axis=1), sizes)

    first_image = exact_dot(pre_grad, power_raw[:, 0], ((1,), (0,))).reshape(height, breadth, rank)
    first_spread = jnp.concatenate(
        [
            jnp.pad(first_image, ((1 + a, 1 - a), (1 + b, 1 - b), (0, 0))).reshape(-1, rank)
            for a, b in TAPS
        ],
        axis=1,
    )
    first_rows = exact_dot(input_flat, first_spread, ((0,), (0,)))
    second_image = exact_dot(grad_flat, power_raw[:, 1], ((1,), (0,))).reshape(grid + (rank,))
    second_spread = jnp.concatenate(
        [
            second_image[1 - a : 1 - a + height, 1 - b : 1 - b + breadth].reshape(pixels, rank)
            for a, b in TAPS
        ],
        axis=1,
    )
    second_rows = exact_dot(hidden, second_spread, ((0,), (0,)))
    rows = jnp.stack([first_rows, second_rows]).reshape(2, channels, taps, rank)
    rows = rows.transpose(2, 1, 0, 3).reshape(taps * channels, 2, rank)
    row_block = block_sum(rows, sizes)

    gram = jnp.einsum(
        "mqn,mqg->qng", power_raw, power_raw, precision=lax.Precision.HIGHEST, preferred_element_type=jnp.float32
    )
    lower = jnp.linalg.cholesky(gram)
    basis_count = channels // sizes["dp"]
    raw_part = lax.dynamic_slice_in_dim(power_raw, lax.axis_index("dp") * basis_count, basis_count, 0)
    basis_out = lax.linalg.triangular_solve(
        lower, raw_part.transpose(1, 0, 2), left_side=False, lower=True, transpose_a=True
    ).transpose(1, 0, 2)
    factor_out = lax.linalg.triangular_solve(
        lower, row_block.transpose(1, 0, 2), left_side=False, lower=True, transpose_a=True
    ).transpose(1, 0, 2)
    return (basis_out, factor_out)


def all_sum_small(value, sizes):
    shape = value.shape
    rows, group = shape[0], sizes["row"] * sizes["col"]
    flat = value.reshape(rows, -1)
    part = exchange(flat.reshape(group, rows // group, -1), ("row", "col"), sizes, 0).sum(0)
    piece = part.reshape(sizes["dp"], -1, 64)
    piece = exchange(piece, ("dp",), sizes, 1).sum(0)
    part = exchange(piece, ("dp",), sizes, 2, gather=True).reshape(part.shape)
    flat = exchange(part, ("row", "col"), sizes, 3, gather=True).reshape(flat.shape)
    return flat.reshape(shape)


def block_sum(value, sizes):
    shape = value.shape
    blocks, group = sizes["dp"], sizes["row"] * sizes["col"]
    block_rows = shape[0] // blocks
    piece_rows = -(-block_rows // (group * 8)) * 8
    lanes = math.prod(shape[1:])
    padded = jnp.pad(value.reshape(blocks, block_rows, lanes), ((0, 0), (0, piece_rows * group - block_rows), (0, 0)))
    pieces = padded.reshape(blocks, sizes["row"], sizes["col"], piece_rows, lanes).transpose(1, 2, 0, 3, 4)
    pieces = exchange(pieces, ("row",), sizes, 4).sum(0)
    pieces = exchange(pieces, ("col",), sizes, 5).sum(0)
    piece = exchange(pieces, ("dp",), sizes, 6).sum(0)
    block = exchange(piece, ("row", "col"), sizes, 7, gather=True)
    return block.reshape(group * piece_rows, lanes)[:block_rows].reshape((block_rows,) + shape[1:])


def solution(mesh):
    placed = (
        P("dp", "row", "col", None),
        P("dp", "row", "col", None),
        P("dp", "row", "col", None),
        P(),
        P(),
    )
    sizes = dict(mesh.shape)
    return jax.shard_map(
        functools.partial(on_device, sizes=sizes),
        mesh=mesh,
        in_specs=placed,
        out_specs=(P("dp", None, None), P("dp", None, None)),
        check_vma=False,
    )
```

profile of v0, /device:TPU:1, one launch (start us, length us, event | category | flops | bytes accessed | tf_op | source)
XLA Modules:
  0.0 260.0 jit_solution(5314771114429483606)
XLA Ops:
  2.0 5.1 %collective-permute-start.1 = (bf16[1,16,640]{2,1,0:T(8,128)(2,1)}, bf16[1,16,640]{2,1,0:T(8,128)(2,1)S(1)}, u32[]{:S(2)}, u32[]{:S(2)}) collective-permute-start(bf16[1,16,640]{2,1,0:T(8,128)(2,1)} %get-tuple-element.38), channel_id=1, source_target_pairs={{4,0},{5,1},{6,2},{7,3},{12,8},{13,9},{14,10},{15,11},{20,16},{21,... | collective-permute-start | bytes 61448 | tf_op jit(solution)/shard_map/ppermute | solution.py:87
  9.8 3.6 %collective-permute-start.5 = (bf16[1,16,640]{2,1,0:T(8,128)(2,1)}, bf16[1,16,640]{2,1,0:T(8,128)(2,1)}, u32[]{:S(2)}, u32[]{:S(2)}) collective-permute-start(bf16[1,16,640]{2,1,0:T(8,128)(2,1)} %get-tuple-element.34), channel_id=1, source_target_pairs={{4,0},{5,1},{6,2},{7,3},{12,8},{13,9},{14,10},{15,11},{20,16},{21,... | collective-permute-start | bytes 61448 | tf_op jit(solution)/shard_map/ppermute | solution.py:87
  14.7 2.1 fusion.37
  16.8 1.9 fusion.32
  18.7 4.7 %reshape.189 = f32[9,640,2,64]{1,0,3,2:T(8,128)} reshape(f32[5760,2,64]{0,2,1:T(8,128)} %param.9) | data formatting | bytes 5898240 | tf_op jit(solution)/shard_map/reshape | solution.py:131
  23.4 4.4 %fusion.67 = (f32[1,640,9,64]{1,2,3,0:T(8,128)}, f32[1,640,9,64]{1,2,3,0:T(8,128)S(1)}) fusion(f32[2,640,9,64]{1,2,3,0:T(8,128)} %bitcast.213), kind=kLoop, calls=%fused_computation.128 | loop fusion | bytes 5898240 | tf_op jit(solution)/shard_map/slice | solution.py:133
  27.9 2.0 fusion
  32.9 4.0 %collective-permute-start.3 = (bf16[18,1,640]{2,1,0:T(2,128)(2,1)S(1)}, bf16[18,1,640]{2,1,0:T(2,128)(2,1)S(1)}, u32[]{:S(2)}, u32[]{:S(2)}) collective-permute-start(bf16[18,1,640]{2,1,0:T(2,128)(2,1)S(1)} %get-tuple-element.31), channel_id=1, source_target_pairs={{0,1},{1,2},{2,3},{4,5},{5,6},{6,7},{8,9},{9,10},{10,11},{12,13},{... | collective-permute-start | bytes 69128 | tf_op jit(solution)/shard_map/ppermute | solution.py:86
  39.4 4.4 %collective-permute-start.6 = (bf16[18,1,640]{2,1,0:T(2,128)(2,1)S(1)}, bf16[18,1,640]{2,1,0:T(2,128)(2,1)S(1)}, u32[]{:S(2)}, u32[]{:S(2)}) collective-permute-start(bf16[18,1,640]{2,1,0:T(2,128)(2,1)S(1)} %get-tuple-element.27), channel_id=1, source_target_pairs={{0,1},{1,2},{2,3},{4,5},{5,6},{6,7},{8,9},{9,10},{10,11},{12,13},{... | collective-permute-start | bytes 69128 | tf_op jit(solution)/shard_map/ppermute | solution.py:86
  47.6 3.8 %fusion.2 = f32[18,18,9,64]{3,1,2,0:T(8,128)S(1)} fusion(f32[1,640,9,64]{1,2,3,0:T(8,128)S(1)} %copy-done.3, bf16[18,1,640]{2,1,0:T(2,128)(2,1)S(1)} %collective-permute-done.7, bf16[1,16,640]{2,1,0:T(8,128)(2,1)} %collective-permute-done.5, bf16[16,16,640]{2,1,0:T(8,128)(2,1)S(1)} %bitcast.230, bf16[1,16,640]{2,1,0:T(8,128)(2,1)} %collective-permute-done.4, ...), kind=kOutput, calls=%fused_computation.4 | convolution fusion | flops 1435345920 | bytes 2635776 | tf_op jit(solution)/shard_map/dot_general | solution.py:98
  58.2 10.2 %shard_map.68 = f32[8,80,128]{2,1,0:T(8,128)} custom-call(f32[8,80,128]{2,1,0:T(8,128)} %copy.82.x_ref), custom_call_target="tpu_custom_call" | custom-call | tf_op jit(solution)/shard_map/pallas_call | solution.py:65
  70.1 13.5 %shard_map.69 = f32[32,5,64]{2,1,0:T(8,128)} custom-call(f32[32,5,64]{2,1,0:T(8,128)} %reshape.190.x_ref), custom_call_target="tpu_custom_call" | custom-call | tf_op jit(solution)/shard_map/pallas_call | solution.py:65
  85.2 10.6 %shard_map.70 = f32[32,5,64]{2,1,0:T(8,128)} custom-call(f32[5,64]{1,0:T(8,128)} %reduce_sum.46.x_ref), custom_call_target="tpu_custom_call" | custom-call | tf_op jit(solution)/shard_map/pallas_call | solution.py:65
  97.4 10.1 %shard_map.71 = f32[8,80,128]{2,1,0:T(8,128)} custom-call(f32[80,128]{1,0:T(8,128)} %reshape.191.x_ref), custom_call_target="tpu_custom_call" | custom-call | tf_op jit(solution)/shard_map/pallas_call | solution.py:65
  109.6 12.0 %custom-call.9 = f32[2,64,64]{2,1,0:T(8,128)S(1)} custom-call(f32[2,64,64]{2,1,0:T(8,128)S(1)} %fusion.61), custom_call_target="Cholesky" | custom-call | tf_op jit(solution)/shard_map/jit(cholesky)/cholesky | solution.py:171
  121.8 9.8 %custom-call.10 = f32[2,1,64,64]{2,3,1,0:T(8,128)S(1)} custom-call(f32[2,1,64,64]{3,2,1,0:T(8,128)S(1)} %select_bitcast_fusion), custom_call_target="InvertDiagBlocksLowerTriangular" | custom-call | tf_op jit(solution)/shard_map/triangular_solve | solution.py:174
  143.5 5.5 %copy.89 = f32[9,640,2,64]{3,2,1,0:T(2,128)} copy(f32[9,640,2,64]{1,3,0,2:T(8,128)S(1)} %maximum_bitcast_fusion) | data formatting | bytes 5898240 | tf_op jit(solution)/shard_map/transpose | solution.py:165
  149.0 5.4 %reshape_reshape.15 = f32[32,180,128]{2,1,0:T(8,128)S(1)} reshape(f32[9,640,2,64]{3,2,1,0:T(2,128)} %copy.89) | data formatting | bytes 5898240 | tf_op jit(solution)/shard_map/reshape;reshape | solution.py:201
  156.7 50.0 %shard_map.72 = f32[2,4,32,24,128]{4,3,2,1,0:T(8,128)} custom-call(f32[2,4,32,24,128]{4,3,2,1,0:T(8,128)} %bitcast.215), custom_call_target="tpu_custom_call" | custom-call | tf_op jit(solution)/shard_map/pallas_call | solution.py:65
  206.8 3.4 %reduce_sum.47.x_ref = f32[4,32,24,128]{3,2,1,0:T(8,128)} reduce(f32[2,4,32,24,128]{4,3,2,1,0:T(8,128)} %shard_map.72, f32[]{:T(128)} %constant.56.clone.1), dimensions={0}, to_apply=%region_4.5 | reduce | flops 393216 | bytes 4718596 | tf_op jit(solution)/shard_map/reduce_sum | solution.py:203
  210.2 21.2 %shard_map.73 = f32[4,32,24,128]{3,2,1,0:T(8,128)} custom-call(f32[4,32,24,128]{3,2,1,0:T(8,128)} %reduce_sum.47.x_ref), custom_call_target="tpu_custom_call" | custom-call | tf_op jit(solution)/shard_map/pallas_call | solution.py:65
  231.4 2.3 reduce_sum.48.x_ref
  233.7 16.2 %shard_map.74 = f32[32,24,128]{2,1,0:T(8,128)} custom-call(f32[32,24,128]{2,1,0:T(8,128)} %reduce_sum.48.x_ref), custom_call_target="tpu_custom_call" | custom-call | tf_op jit(solution)/shard_map/pallas_call | solution.py:65
  251.6 6.4 %shard_map.75 = f32[8,24,128]{2,1,0:T(8,128)} custom-call(f32[24,128]{1,0:T(8,128)} %reduce_sum.49.x_ref), custom_call_target="tpu_custom_call" | custom-call | tf_op jit(solution)/shard_map/pallas_call | solution.py:65
  (144 shorter events, 45.8 us)
Async XLA Ops:
  2.0 29.5 %collective-permute-start.1 = (bf16[1,16,640]{2,1,0:T(8,128)(2,1)}, bf16[1,16,640]{2,1,0:T(8,128)(2,1)S(1)}, u32[]{:S(2)}, u32[]{:S(2)}) collective-permute-start(bf16[1,16,640]{2,1,0:T(8,128)(2,1)} %get-tuple-element.38), channel_id=1, source_target_pairs={{4,0},{5,1},{6,2},{7,3},{12,8},{13,9},{14,10},{15,11},{20,16},{21,... | collective-permute-start | bytes 61448 | tf_op jit(solution)/shard_map/ppermute | solution.py:87
  7.1 24.4 %collective-permute-start = (bf16[1,16,640]{2,1,0:T(8,128)(2,1)}, bf16[1,16,640]{2,1,0:T(8,128)(2,1)S(1)}, u32[]{:S(2)}, u32[]{:S(2)}) collective-permute-start(bf16[1,16,640]{2,1,0:T(8,128)(2,1)} %get-tuple-element.37), channel_id=1, source_target_pairs={{0,4},{1,5},{2,6},{3,7},{8,12},{9,13},{10,14},{11,15},{16,20},{17,... | collective-permute-start | bytes 61448 | tf_op jit(solution)/shard_map/ppermute | solution.py:86
  9.8 27.1 %collective-permute-start.5 = (bf16[1,16,640]{2,1,0:T(8,128)(2,1)}, bf16[1,16,640]{2,1,0:T(8,128)(2,1)}, u32[]{:S(2)}, u32[]{:S(2)}) collective-permute-start(bf16[1,16,640]{2,1,0:T(8,128)(2,1)} %get-tuple-element.34), channel_id=1, source_target_pairs={{4,0},{5,1},{6,2},{7,3},{12,8},{13,9},{14,10},{15,11},{20,16},{21,... | collective-permute-start | bytes 61448 | tf_op jit(solution)/shard_map/ppermute | solution.py:87
  13.4 23.5 %collective-permute-start.4 = (bf16[1,16,640]{2,1,0:T(8,128)(2,1)}, bf16[1,16,640]{2,1,0:T(8,128)(2,1)}, u32[]{:S(2)}, u32[]{:S(2)}) collective-permute-start(bf16[1,16,640]{2,1,0:T(8,128)(2,1)} %get-tuple-element.33), channel_id=1, source_target_pairs={{0,4},{1,5},{2,6},{3,7},{8,12},{9,13},{10,14},{11,15},{16,20},{17,... | collective-permute-start | bytes 61448 | tf_op jit(solution)/shard_map/ppermute | solution.py:86
  23.4 4.4 %copy-start.8 = (bf16[1,16,16,640]{3,2,1,0:T(8,128)(2,1)S(1)}, bf16[1,16,16,640]{3,2,1,0:T(8,128)(2,1)}, u32[]{:S(2)}) copy-start(bf16[1,16,16,640]{3,2,1,0:T(8,128)(2,1)} %param.6) | copy-start | bytes 983044
  27.9 18.1 %slice-start = ((s8[7372800]{0:T(1024)(128)(4,1)}), s8[3178496]{0:T(1024)(128)(4,1)S(1)}, s32[]{:S(2)}) async-start(s8[7372800]{0:T(1024)(128)(4,1)} %bitcast.216), calls=%async_computation | async-start | bytes 6356992
  29.9 1.6 copy-start
  31.6 13.9 %collective-permute-start.2 = (bf16[18,1,640]{2,1,0:T(2,128)(2,1)S(1)}, bf16[18,1,640]{2,1,0:T(2,128)(2,1)S(1)}, u32[]{:S(2)}, u32[]{:S(2)}) collective-permute-start(bf16[18,1,640]{2,1,0:T(2,128)(2,1)S(1)} %get-tuple-element.32), channel_id=1, source_target_pairs={{1,0},{2,1},{3,2},{5,4},{6,5},{7,6},{9,8},{10,9},{11,10},{13,12},{... | collective-permute-start | bytes 69128 | tf_op jit(solution)/shard_map/ppermute | solution.py:87
  32.9 12.6 %collective-permute-start.3 = (bf16[18,1,640]{2,1,0:T(2,128)(2,1)S(1)}, bf16[18,1,640]{2,1,0:T(2,128)(2,1)S(1)}, u32[]{:S(2)}, u32[]{:S(2)}) collective-permute-start(bf16[18,1,640]{2,1,0:T(2,128)(2,1)S(1)} %get-tuple-element.31), channel_id=1, source_target_pairs={{0,1},{1,2},{2,3},{4,5},{5,6},{6,7},{8,9},{9,10},{10,11},{12,13},{... | collective-permute-start | bytes 69128 | tf_op jit(solution)/shard_map/ppermute | solution.py:86
  38.0 8.4 %collective-permute-start.7 = (bf16[18,1,640]{2,1,0:T(2,128)(2,1)S(1)}, bf16[18,1,640]{2,1,0:T(2,128)(2,1)S(1)}, u32[]{:S(2)}, u32[]{:S(2)}) collective-permute-start(bf16[18,1,640]{2,1,0:T(2,128)(2,1)S(1)} %get-tuple-element.28), channel_id=1, source_target_pairs={{1,0},{2,1},{3,2},{5,4},{6,5},{7,6},{9,8},{10,9},{11,10},{13,12},{... | collective-permute-start | bytes 69128 | tf_op jit(solution)/shard_map/ppermute | solution.py:87
  39.3 6.7 %slice-start.1 = ((s8[7372800]{0:T(1024)(128)(4,1)}), s8[4194304]{0:T(1024)(128)(4,1)S(1)}, s32[]{:S(2)}) async-start(s8[7372800]{0:T(1024)(128)(4,1)} %bitcast.216), calls=%async_computation.1 | async-start | bytes 8388608
  39.4 7.2 %collective-permute-start.6 = (bf16[18,1,640]{2,1,0:T(2,128)(2,1)S(1)}, bf16[18,1,640]{2,1,0:T(2,128)(2,1)S(1)}, u32[]{:S(2)}, u32[]{:S(2)}) collective-permute-start(bf16[18,1,640]{2,1,0:T(2,128)(2,1)S(1)} %get-tuple-element.27), channel_id=1, source_target_pairs={{0,1},{1,2},{2,3},{4,5},{5,6},{6,7},{8,9},{9,10},{10,11},{12,13},{... | collective-permute-start | bytes 69128 | tf_op jit(solution)/shard_map/ppermute | solution.py:86
  45.5 10.4 %copy-start.20 = (bf16[18,1,640]{2,1,0:T(2,128)(2,1)}, bf16[18,1,640]{2,1,0:T(2,128)(2,1)S(1)}, u32[]{:S(2)}) copy-start(bf16[18,1,640]{2,1,0:T(2,128)(2,1)S(1)} %collective-permute-done.2) | copy-start | bytes 69124
  45.5 10.4 %copy-start.22 = (bf16[18,1,640]{2,1,0:T(2,128)(2,1)}, bf16[18,1,640]{2,1,0:T(2,128)(2,1)S(1)}, u32[]{:S(2)}) copy-start(bf16[18,1,640]{2,1,0:T(2,128)(2,1)S(1)} %collective-permute-done.3) | copy-start | bytes 69124
  45.8 1.8 copy-start.3
  46.0 1.6 copy-start.5
  46.5 4.9 %copy-start.24 = (bf16[18,1,640]{2,1,0:T(2,128)(2,1)}, bf16[18,1,640]{2,1,0:T(2,128)(2,1)S(1)}, u32[]{:S(2)}) copy-start(bf16[18,1,640]{2,1,0:T(2,128)(2,1)S(1)} %collective-permute-done.7) | copy-start | bytes 69124
  46.5 4.9 %copy-start.26 = (bf16[18,1,640]{2,1,0:T(2,128)(2,1)}, bf16[18,1,640]{2,1,0:T(2,128)(2,1)S(1)}, u32[]{:S(2)}) copy-start(bf16[18,1,640]{2,1,0:T(2,128)(2,1)S(1)} %collective-permute-done.6) | copy-start | bytes 69124
  107.5 14.2 %copy-start.28 = (pred[64,64]{1,0:T(8,128)(4,1)S(1)}, pred[64,64]{1,0:T(8,128)(4,1)}, u32[]{:S(2)}) copy-start(pred[64,64]{1,0:T(8,128)(4,1)} %iota_compare_fusion.1) | copy-start | bytes 12292
  107.5 25.1 %copy-start.21 = (bf16[18,1,640]{2,1,0:T(2,128)(2,1)S(1)}, bf16[18,1,640]{2,1,0:T(2,128)(2,1)}, u32[]{:S(2)}) copy-start(bf16[18,1,640]{2,1,0:T(2,128)(2,1)} %copy-done.20) | copy-start | bytes 69124
  107.5 25.1 %copy-start.23 = (bf16[18,1,640]{2,1,0:T(2,128)(2,1)S(1)}, bf16[18,1,640]{2,1,0:T(2,128)(2,1)}, u32[]{:S(2)}) copy-start(bf16[18,1,640]{2,1,0:T(2,128)(2,1)} %copy-done.22) | copy-start | bytes 69124
  133.7 1.8 copy-start.2
  138.9 2.0 copy-start.7
  231.4 27.6 %copy-start.10 = (f32[2,1,64,64]{2,3,1,0:T(8,128)S(1)}, f32[2,1,64,64]{2,3,1,0:T(8,128)}, u32[]{:S(2)}) copy-start(f32[2,1,64,64]{2,3,1,0:T(8,128)} %copy-done.9) | copy-start | bytes 98308
  (15 other events, 16.6 us)
where the time goes:
time: 261 us; the launch traced here: 260 us
  Pallas kernels  138 us (53%)
  local copies, waits for them, and re-layouts  41.3 us (16%)
  other arithmetic  39.4 us (15%)
  starting transfers between devices  22.3 us (9%)
  matrix products  17.2 us (7%)
    pallas_call x8, Pallas kernels, exchange(): pl.pallas_call(functools.partial(exchange_kernel, axes=axes, sizes=sizes,...  138 us
    another operation x4, other arithmetic, on_device(): lower = jnp.linalg.cholesky(gram)  12.1 us
    ppermute x4, starting transfers between devices, padded_2(): after = lax.ppermute(leading, axis, down)  11.3 us
    ppermute x4, starting transfers between devices, padded_2(): before = lax.ppermute(last, axis, up)  11 us
    another operation x3, other arithmetic, on_device(): lax.linalg.triangular_solve(lower, raw_part.transpose(1, 0, 2), left_side...  10.5 us
    dot_general x8, matrix products, exact_dot(): lax.dot_general(left.astype(jnp.float32), right.astype(jnp.float32), (con...  10.2 us
    transpose x1, local copies, waits for them, and re-layouts, on_device(): rows = rows.transpose(2, 1, 0, 3).reshape(taps * channels, 2, rank)  5.52 us
    another operation x1, local copies, waits for them, and re-layouts, block_sum(): value.reshape(blocks, block_rows, lanes)  5.45 us
  transfers between devices with their start and end apart: 8, of which 0 were waited for; matrix products, arithmetic and copies ran while one was open for 8% of the time, Pallas kernels for 0%

commit v1 on v0

--- a/solution.py
+++ b/solution.py
@@ -17,63 +17,74 @@
     return coords
 
 
-def exchange_kernel(x_ref, o_ref, send_sem, recv_sem, local_sem, *, axes, sizes, gather, chunks):
-    n = math.prod(sizes[a] for a in axes)
-    me = 0
-    for axis in axes:
-        me = me * sizes[axis] + lax.axis_index(axis)
-    step = o_ref.shape[1] // chunks
+def exchange_kernel(*refs, jobs, sizes):
+    count = len(jobs)
+    x_refs, o_refs = refs[:count], refs[count : 2 * count]
+    sems = refs[2 * count :]
     barrier = pltpu.get_barrier_semaphore()
-    for s in range(1, n):
-        peer = member_coords(lax.rem(me + s, n), axes, sizes)
-        pl.semaphore_signal(barrier, inc=1, device_id=peer, device_id_type=pl.DeviceIdType.MESH)
-    pl.semaphore_wait(barrier, n - 1)
-
-    def source(index, part):
-        rows = pl.ds(part * step, step)
-        return x_ref.at[rows] if gather else x_ref.at[index, rows]
-
-    copies = []
-    for s in range(1, n):
-        dst = lax.rem(me + s, n)
-        for part in range(chunks):
+    plans = []
+    total = 0
+    for axes, gather in jobs:
+        n = math.prod(sizes[a] for a in axes)
+        me = 0
+        for axis in axes:
+            me = me * sizes[axis] + lax.axis_index(axis)
+        for s in range(1, n):
+            peer = member_coords(lax.rem(me + s, n), axes, sizes)
+            pl.semaphore_signal(barrier, inc=1, device_id=peer, device_id_type=pl.DeviceIdType.MESH)
+        total += n - 1
+        plans.append((n, me))
+    pl.semaphore_wait(barrier, total)
+    copies, locals_ = [], []
+    for job, ((axes, gather), (n, me)) in enumerate(zip(jobs, plans)):
+        x_ref, o_ref = x_refs[job], o_refs[job]
+        send_sem, recv_sem, local_sem = sems[3 * job : 3 * job + 3]
+        for s in range(1, n):
+            dst = lax.rem(me + s, n)
             copy = pltpu.make_async_remote_copy(
-                src_ref=source(dst, part),
-                dst_ref=o_ref.at[me, pl.ds(part * step, step)],
-                send_sem=send_sem.at[s - 1, part],
-                recv_sem=recv_sem.at[s - 1, part],
+                src_ref=x_ref if gather else x_ref.at[dst],
+                dst_ref=o_ref.at[me],
+                send_sem=send_sem.at[s - 1],
+                recv_sem=recv_sem.at[s - 1],
                 device_id=member_coords(dst, axes, sizes),
                 device_id_type=pl.DeviceIdType.MESH,
             )
             copy.start()
             copies.append(copy)
-    local = pltpu.make_async_copy(x_ref if gather else x_ref.at[me], o_ref.at[me], local_sem)
-    local.start()
+        local = pltpu.make_async_copy(x_ref if gather else x_ref.at[me], o_ref.at[me], local_sem)
+        local.start()
+        locals_.append(local)
     for copy in copies:
         copy.wait_send()
         copy.wait_recv()
-    local.wait()
+    for local in locals_:
+        local.wait()
+
+
+def exchange_many(items, sizes, cid):
+    jobs, shapes, scratch = [], [], []
+    for x, axes, gather in items:
+        n = math.prod(sizes[a] for a in axes)
+        slab = x.shape if gather else x.shape[1:]
+        jobs.append((axes, gather))
+        shapes.append(jax.ShapeDtypeStruct((n,) + slab, x.dtype))
+        scratch += [
+            pltpu.SemaphoreType.DMA((max(n - 1, 1),)),
+            pltpu.SemaphoreType.DMA((max(n - 1, 1),)),
+            pltpu.SemaphoreType.DMA,
+        ]
+    return pl.pallas_call(
+        functools.partial(exchange_kernel, jobs=tuple(jobs), sizes=sizes),
+        out_shape=tuple(shapes),
+        in_specs=[pl.BlockSpec(memory_space=pl.ANY)] * len(items),
+        out_specs=tuple(pl.BlockSpec(memory_space=pl.ANY) for _ in items),
+        scratch_shapes=scratch,
+        compiler_params=pltpu.CompilerParams(collective_id=cid, has_side_effects=True),
+    )(*[x for x, _, _ in items])
 
 
 def exchange(x, axes, sizes, cid, gather=False):
-    n = math.prod(sizes[a] for a in axes)
-    slab = x.shape if gather else x.shape[1:]
-    slab_bytes = math.prod(slab) * x.dtype.itemsize
-    chunks = 1
-    while chunks < 8 and slab[0] % (chunks * 2) == 0 and slab_bytes // (chunks * 2) >= 96 * 1024:
-        chunks *= 2
-    return pl.pallas_call(
-        functools.partial(exchange_kernel, axes=axes, sizes=sizes, gather=gather, chunks=chunks),
-        out_shape=jax.ShapeDtypeStruct((n,) + slab, x.dtype),
-        in_specs=[pl.BlockSpec(memory_space=pl.ANY)],
-        out_specs=pl.BlockSpec(memory_space=pl.ANY),
-        scratch_shapes=[
-            pltpu.SemaphoreType.DMA((max(n - 1, 1), chunks)),
-            pltpu.SemaphoreType.DMA((max(n - 1, 1), chunks)),
-            pltpu.SemaphoreType.DMA,
-        ],
-        compiler_params=pltpu.CompilerParams(collective_id=cid, has_side_effects=True),
-    )(x)
+    return exchange_many([(x, axes, gather)], sizes, cid)[0]
 
 
 def padded_2(value, sides, width):
@@ -194,14 +205,21 @@
 
 def block_sum(value, sizes):
     shape = value.shape
-    blocks, group = sizes["dp"], sizes["row"] * sizes["col"]
+    blocks, rows_n, cols_n = sizes["dp"], sizes["row"], sizes["col"]
+    group = rows_n * cols_n
     block_rows = shape[0] // blocks
     piece_rows = -(-block_rows // (group * 8)) * 8
     lanes = math.prod(shape[1:])
     padded = jnp.pad(value.reshape(blocks, block_rows, lanes), ((0, 0), (0, piece_rows * group - block_rows), (0, 0)))
-    pieces = padded.reshape(blocks, sizes["row"], sizes["col"], piece_rows, lanes).transpose(1, 2, 0, 3, 4)
-    pieces = exchange(pieces, ("row",), sizes, 4).sum(0)
-    pieces = exchange(pieces, ("col",), sizes, 5).sum(0)
+    pieces = padded.reshape(blocks, rows_n, cols_n, piece_rows, lanes)
+    half = blocks // 2
+    first = pieces[:half].transpose(1, 2, 0, 3, 4)
+    second = pieces[half:].transpose(2, 1, 0, 3, 4)
+    first, second = exchange_many([(first, ("row",), False), (second, ("col",), False)], sizes, 4)
+    first, second = exchange_many(
+        [(first.sum(0), ("col",), False), (second.sum(0), ("row",), False)], sizes, 5
+    )
+    pieces = jnp.concatenate([first.sum(0), second.sum(0)])
     piece = exchange(pieces, ("dp",), sizes, 6).sum(0)
     block = exchange(piece, ("row", "col"), sizes, 7, gather=True)
     return block.reshape(group * piece_rows, lanes)[:block_rows].reshape((block_rows,) + shape[1:])

time: 261 us -> 245 us (0.939)
  Pallas kernels: 138 us -> 121 us
    pallas_call x8, Pallas kernels: 138 us -> 121 us  [exchange_many(): pl.pallas_call(functools.partial(exchange_kernel, jobs=tuple(jobs), sizes...]
    slice x0 -> x3, local copies, waits for them, and re-layouts: none -> 2.97 us  [the longest x2 1.68 us: block_sum(): second = pieces[half:].transpose(2, 1, 0, 3, 4)]
    reduce_sum x2 -> x4, other arithmetic: 5.74 us -> 5.68 us  [the longest x1 2.58 us: block_sum(): first.sum(0)]
  transfers between devices with their start and end apart: 8 -> 8, of which waited for: 0 -> 0; matrix products, arithmetic and copies ran while one was open for 8% -> 9% of each run, Pallas kernels for 0% -> 0%
where the time goes in v1:
time: 245 us; the launch traced here: 244 us
  Pallas kernels  121 us (49%)
  local copies, waits for them, and re-layouts  42.1 us (17%)
  other arithmetic  40.1 us (16%)
  starting transfers between devices  22.3 us (9%)
  matrix products  17.2 us (7%)
    pallas_call x8, Pallas kernels, exchange_many(): pl.pallas_call(functools.partial(exchange_kernel, jobs=tuple(jobs), sizes...  121 us
    another operation x4, other arithmetic, on_device(): lower = jnp.linalg.cholesky(gram)  12.1 us
    ppermute x4, starting transfers between devices, padded_2(): after = lax.ppermute(leading, axis, down)  11.3 us
    ppermute x4, starting transfers between devices, padded_2(): before = lax.ppermute(last, axis, up)  11 us
    another operation x3, other arithmetic, on_device(): lax.linalg.triangular_solve(lower, raw_part.transpose(1, 0, 2), left_side...  10.5 us
    dot_general x8, matrix products, exact_dot(): lax.dot_general(left.astype(jnp.float32), right.astype(jnp.float32), (con...  10.2 us
    transpose x1, local copies, waits for them, and re-layouts, on_device(): rows = rows.transpose(2, 1, 0, 3).reshape(taps * channels, 2, rank)  5.53 us
    another operation x1, local copies, waits for them, and re-layouts, block_sum(): value.reshape(blocks, block_rows, lanes)  5.45 us
  transfers between devices with their start and end apart: 8, of which 0 were waited for; matrix products, arithmetic and copies ran while one was open for 9% of the time, Pallas kernels for 0%

profile of v1, /device:TPU:1, one launch (start us, length us, event | category | flops | bytes accessed | tf_op | source)
XLA Modules:
  0.0 244.1 jit_solution(11676962884203407890)
XLA Ops:
  2.0 5.1 %collective-permute-start.1 = (bf16[1,16,640]{2,1,0:T(8,128)(2,1)}, bf16[1,16,640]{2,1,0:T(8,128)(2,1)S(1)}, u32[]{:S(2)}, u32[]{:S(2)}) collective-permute-start(bf16[1,16,640]{2,1,0:T(8,128)(2,1)} %get-tuple-element.48), channel_id=1, source_target_pairs={{4,0},{5,1},{6,2},{7,3},{12,8},{13,9},{14,10},{15,11},{20,16},{21,... | collective-permute-start | bytes 61448 | tf_op jit(solution)/shard_map/ppermute | solution.py:98
  9.8 3.6 %collective-permute-start.5 = (bf16[1,16,640]{2,1,0:T(8,128)(2,1)}, bf16[1,16,640]{2,1,0:T(8,128)(2,1)}, u32[]{:S(2)}, u32[]{:S(2)}) collective-permute-start(bf16[1,16,640]{2,1,0:T(8,128)(2,1)} %get-tuple-element.44), channel_id=1, source_target_pairs={{4,0},{5,1},{6,2},{7,3},{12,8},{13,9},{14,10},{15,11},{20,16},{21,... | collective-permute-start | bytes 61448 | tf_op jit(solution)/shard_map/ppermute | solution.py:98
  14.7 2.1 fusion.37
  16.8 1.9 fusion.32
  18.7 4.7 %reshape.189 = f32[9,640,2,64]{1,0,3,2:T(8,128)} reshape(f32[5760,2,64]{0,2,1:T(8,128)} %param.9) | data formatting | bytes 5898240 | tf_op jit(solution)/shard_map/reshape | solution.py:142
  23.5 4.4 %fusion.67 = (f32[1,640,9,64]{1,2,3,0:T(8,128)}, f32[1,640,9,64]{1,2,3,0:T(8,128)S(1)}) fusion(f32[2,640,9,64]{1,2,3,0:T(8,128)} %bitcast.217), kind=kLoop, calls=%fused_computation.132 | loop fusion | bytes 5898240 | tf_op jit(solution)/shard_map/slice | solution.py:144
  27.9 2.0 fusion
  32.9 4.0 %collective-permute-start.3 = (bf16[18,1,640]{2,1,0:T(2,128)(2,1)S(1)}, bf16[18,1,640]{2,1,0:T(2,128)(2,1)S(1)}, u32[]{:S(2)}, u32[]{:S(2)}) collective-permute-start(bf16[18,1,640]{2,1,0:T(2,128)(2,1)S(1)} %get-tuple-element.41), channel_id=1, source_target_pairs={{0,1},{1,2},{2,3},{4,5},{5,6},{6,7},{8,9},{9,10},{10,11},{12,13},{... | collective-permute-start | bytes 69128 | tf_op jit(solution)/shard_map/ppermute | solution.py:97
  39.4 4.4 %collective-permute-start.6 = (bf16[18,1,640]{2,1,0:T(2,128)(2,1)S(1)}, bf16[18,1,640]{2,1,0:T(2,128)(2,1)S(1)}, u32[]{:S(2)}, u32[]{:S(2)}) collective-permute-start(bf16[18,1,640]{2,1,0:T(2,128)(2,1)S(1)} %get-tuple-element.37), channel_id=1, source_target_pairs={{0,1},{1,2},{2,3},{4,5},{5,6},{6,7},{8,9},{9,10},{10,11},{12,13},{... | collective-permute-start | bytes 69128 | tf_op jit(solution)/shard_map/ppermute | solution.py:97
  47.6 3.8 %fusion.2 = f32[18,18,9,64]{3,1,2,0:T(8,128)S(1)} fusion(f32[1,640,9,64]{1,2,3,0:T(8,128)S(1)} %copy-done.3, bf16[18,1,640]{2,1,0:T(2,128)(2,1)S(1)} %collective-permute-done.7, bf16[1,16,640]{2,1,0:T(8,128)(2,1)} %collective-permute-done.5, bf16[16,16,640]{2,1,0:T(8,128)(2,1)S(1)} %bitcast.236, bf16[1,16,640]{2,1,0:T(8,128)(2,1)} %collective-permute-done.4, ...), kind=kOutput, calls=%fused_computation.7 | convolution fusion | flops 1435345920 | bytes 2635776 | tf_op jit(solution)/shard_map/dot_general | solution.py:109
  58.2 10.2 %shard_map.68 = f32[8,80,128]{2,1,0:T(8,128)} custom-call(f32[8,80,128]{2,1,0:T(8,128)} %copy.84.refs_0_), custom_call_target="tpu_custom_call" | custom-call | tf_op jit(solution)/shard_map/pallas_call | solution.py:76
  70.1 13.5 %shard_map.69 = f32[32,5,64]{2,1,0:T(8,128)} custom-call(f32[32,5,64]{2,1,0:T(8,128)} %reshape.190.refs_0_), custom_call_target="tpu_custom_call" | custom-call | tf_op jit(solution)/shard_map/pallas_call | solution.py:76
  85.2 10.6 %shard_map.70 = f32[32,5,64]{2,1,0:T(8,128)} custom-call(f32[5,64]{1,0:T(8,128)} %reduce_sum.64.refs_0_), custom_call_target="tpu_custom_call" | custom-call | tf_op jit(solution)/shard_map/pallas_call | solution.py:76
  97.4 10.1 %shard_map.71 = f32[8,80,128]{2,1,0:T(8,128)} custom-call(f32[80,128]{1,0:T(8,128)} %reshape.191.refs_0_), custom_call_target="tpu_custom_call" | custom-call | tf_op jit(solution)/shard_map/pallas_call | solution.py:76
  109.6 12.0 %custom-call.9 = f32[2,64,64]{2,1,0:T(8,128)S(1)} custom-call(f32[2,64,64]{2,1,0:T(8,128)S(1)} %fusion.61), custom_call_target="Cholesky" | custom-call | tf_op jit(solution)/shard_map/jit(cholesky)/cholesky | solution.py:182
  121.8 9.8 %custom-call.10 = f32[2,1,64,64]{2,3,1,0:T(8,128)S(1)} custom-call(f32[2,1,64,64]{3,2,1,0:T(8,128)S(1)} %select_bitcast_fusion), custom_call_target="InvertDiagBlocksLowerTriangular" | custom-call | tf_op jit(solution)/shard_map/triangular_solve | solution.py:185
  138.9 1.7 concatenate.46
  143.5 5.5 %copy.91 = f32[9,640,2,64]{3,2,1,0:T(2,128)} copy(f32[9,640,2,64]{1,3,0,2:T(8,128)S(1)} %maximum_bitcast_fusion) | data formatting | bytes 5898240 | tf_op jit(solution)/shard_map/transpose | solution.py:176
  149.0 5.4 %reshape_reshape.15 = f32[32,180,128]{2,1,0:T(8,128)S(1)} reshape(f32[9,640,2,64]{3,2,1,0:T(2,128)} %copy.91) | data formatting | bytes 5898240 | tf_op jit(solution)/shard_map/reshape;reshape | solution.py:213
  157.5 39.3 %shard_map.72 = (f32[2,4,16,24,128]{4,3,2,1,0:T(8,128)}, f32[4,2,16,24,128]{4,3,2,1,0:T(8,128)}) custom-call(f32[2,4,16,24,128]{4,3,2,1,0:T(8,128)} %bitcast.220, f32[4,2,16,24,128]{4,3,2,1,0:T(8,128)} %bitcast.221), custom_call_target="tpu_custom_call" | custom-call | tf_op jit(solution)/shard_map/pallas_call | solution.py:76
  196.8 2.6 %reduce_sum.65.refs_0_ = f32[4,16,24,128]{3,2,1,0:T(8,128)} reduce(f32[2,4,16,24,128]{4,3,2,1,0:T(8,128)} %get-tuple-element.6, f32[]{:T(128)} %constant.56.clone.1), dimensions={0}, to_apply=%region_4.5 | reduce | flops 196608 | bytes 2359300 | tf_op jit(solution)/shard_map/reduce_sum | solution.py:220
  200.2 13.8 %shard_map.73 = (f32[4,16,24,128]{3,2,1,0:T(8,128)}, f32[2,16,24,128]{3,2,1,0:T(8,128)}) custom-call(f32[4,16,24,128]{3,2,1,0:T(8,128)} %reduce_sum.65.refs_0_, f32[2,16,24,128]{3,2,1,0:T(8,128)} %reduce_sum.66.refs_1_), custom_call_target="tpu_custom_call" | custom-call | tf_op jit(solution)/shard_map/pallas_call | solution.py:76
  217.1 15.3 %shard_map.74 = f32[32,24,128]{2,1,0:T(8,128)} custom-call(f32[32,24,128]{2,1,0:T(8,128)} %pad_maximum_fusion.3.refs_0_), custom_call_target="tpu_custom_call" | custom-call | tf_op jit(solution)/shard_map/pallas_call | solution.py:76
  234.0 8.0 %shard_map.75 = f32[8,24,128]{2,1,0:T(8,128)} custom-call(f32[24,128]{1,0:T(8,128)} %reduce_sum.69.refs_0_), custom_call_target="tpu_custom_call" | custom-call | tf_op jit(solution)/shard_map/pallas_call | solution.py:76
  (150 shorter events, 48.6 us)
Async XLA Ops:
  2.0 29.5 %collective-permute-start.1 = (bf16[1,16,640]{2,1,0:T(8,128)(2,1)}, bf16[1,16,640]{2,1,0:T(8,128)(2,1)S(1)}, u32[]{:S(2)}, u32[]{:S(2)}) collective-permute-start(bf16[1,16,640]{2,1,0:T(8,128)(2,1)} %get-tuple-element.48), channel_id=1, source_target_pairs={{4,0},{5,1},{6,2},{7,3},{12,8},{13,9},{14,10},{15,11},{20,16},{21,... | collective-permute-start | bytes 61448 | tf_op jit(solution)/shard_map/ppermute | solution.py:98
  7.1 24.4 %collective-permute-start = (bf16[1,16,640]{2,1,0:T(8,128)(2,1)}, bf16[1,16,640]{2,1,0:T(8,128)(2,1)S(1)}, u32[]{:S(2)}, u32[]{:S(2)}) collective-permute-start(bf16[1,16,640]{2,1,0:T(8,128)(2,1)} %get-tuple-element.47), channel_id=1, source_target_pairs={{0,4},{1,5},{2,6},{3,7},{8,12},{9,13},{10,14},{11,15},{16,20},{17,... | collective-permute-start | bytes 61448 | tf_op jit(solution)/shard_map/ppermute | solution.py:97
  9.8 27.1 %collective-permute-start.5 = (bf16[1,16,640]{2,1,0:T(8,128)(2,1)}, bf16[1,16,640]{2,1,0:T(8,128)(2,1)}, u32[]{:S(2)}, u32[]{:S(2)}) collective-permute-start(bf16[1,16,640]{2,1,0:T(8,128)(2,1)} %get-tuple-element.44), channel_id=1, source_target_pairs={{4,0},{5,1},{6,2},{7,3},{12,8},{13,9},{14,10},{15,11},{20,16},{21,... | collective-permute-start | bytes 61448 | tf_op jit(solution)/shard_map/ppermute | solution.py:98
  13.4 23.5 %collective-permute-start.4 = (bf16[1,16,640]{2,1,0:T(8,128)(2,1)}, bf16[1,16,640]{2,1,0:T(8,128)(2,1)}, u32[]{:S(2)}, u32[]{:S(2)}) collective-permute-start(bf16[1,16,640]{2,1,0:T(8,128)(2,1)} %get-tuple-element.43), channel_id=1, source_target_pairs={{0,4},{1,5},{2,6},{3,7},{8,12},{9,13},{10,14},{11,15},{16,20},{17,... | collective-permute-start | bytes 61448 | tf_op jit(solution)/shard_map/ppermute | solution.py:97
  23.5 4.4 %copy-start.9 = (bf16[1,16,16,640]{3,2,1,0:T(8,128)(2,1)S(1)}, bf16[1,16,16,640]{3,2,1,0:T(8,128)(2,1)}, u32[]{:S(2)}) copy-start(bf16[1,16,16,640]{3,2,1,0:T(8,128)(2,1)} %param.6) | copy-start | bytes 983044
  27.9 18.1 %slice-start = ((s8[7372800]{0:T(1024)(128)(4,1)}), s8[3178496]{0:T(1024)(128)(4,1)S(1)}, s32[]{:S(2)}) async-start(s8[7372800]{0:T(1024)(128)(4,1)} %bitcast.218), calls=%async_computation | async-start | bytes 6356992
  31.6 13.9 %collective-permute-start.2 = (bf16[18,1,640]{2,1,0:T(2,128)(2,1)S(1)}, bf16[18,1,640]{2,1,0:T(2,128)(2,1)S(1)}, u32[]{:S(2)}, u32[]{:S(2)}) collective-permute-start(bf16[18,1,640]{2,1,0:T(2,128)(2,1)S(1)} %get-tuple-element.42), channel_id=1, source_target_pairs={{1,0},{2,1},{3,2},{5,4},{6,5},{7,6},{9,8},{10,9},{11,10},{13,12},{... | collective-permute-start | bytes 69128 | tf_op jit(solution)/shard_map/ppermute | solution.py:98
  32.9 12.6 %collective-permute-start.3 = (bf16[18,1,640]{2,1,0:T(2,128)(2,1)S(1)}, bf16[18,1,640]{2,1,0:T(2,128)(2,1)S(1)}, u32[]{:S(2)}, u32[]{:S(2)}) collective-permute-start(bf16[18,1,640]{2,1,0:T(2,128)(2,1)S(1)} %get-tuple-element.41), channel_id=1, source_target_pairs={{0,1},{1,2},{2,3},{4,5},{5,6},{6,7},{8,9},{9,10},{10,11},{12,13},{... | collective-permute-start | bytes 69128 | tf_op jit(solution)/shard_map/ppermute | solution.py:97
  38.0 8.4 %collective-permute-start.7 = (bf16[18,1,640]{2,1,0:T(2,128)(2,1)S(1)}, bf16[18,1,640]{2,1,0:T(2,128)(2,1)S(1)}, u32[]{:S(2)}, u32[]{:S(2)}) collective-permute-start(bf16[18,1,640]{2,1,0:T(2,128)(2,1)S(1)} %get-tuple-element.38), channel_id=1, source_target_pairs={{1,0},{2,1},{3,2},{5,4},{6,5},{7,6},{9,8},{10,9},{11,10},{13,12},{... | collective-permute-start | bytes 69128 | tf_op jit(solution)/shard_map/ppermute | solution.py:98
  39.3 6.6 %slice-start.1 = ((s8[7372800]{0:T(1024)(128)(4,1)}), s8[4194304]{0:T(1024)(128)(4,1)S(1)}, s32[]{:S(2)}) async-start(s8[7372800]{0:T(1024)(128)(4,1)} %bitcast.218), calls=%async_computation.1 | async-start | bytes 8388608
  39.4 7.1 %collective-permute-start.6 = (bf16[18,1,640]{2,1,0:T(2,128)(2,1)S(1)}, bf16[18,1,640]{2,1,0:T(2,128)(2,1)S(1)}, u32[]{:S(2)}, u32[]{:S(2)}) collective-permute-start(bf16[18,1,640]{2,1,0:T(2,128)(2,1)S(1)} %get-tuple-element.37), channel_id=1, source_target_pairs={{0,1},{1,2},{2,3},{4,5},{5,6},{6,7},{8,9},{9,10},{10,11},{12,13},{... | collective-permute-start | bytes 69128 | tf_op jit(solution)/shard_map/ppermute | solution.py:97
  45.5 10.4 %copy-start.21 = (bf16[18,1,640]{2,1,0:T(2,128)(2,1)}, bf16[18,1,640]{2,1,0:T(2,128)(2,1)S(1)}, u32[]{:S(2)}) copy-start(bf16[18,1,640]{2,1,0:T(2,128)(2,1)S(1)} %collective-permute-done.2) | copy-start | bytes 69124
  45.5 10.4 %copy-start.23 = (bf16[18,1,640]{2,1,0:T(2,128)(2,1)}, bf16[18,1,640]{2,1,0:T(2,128)(2,1)S(1)}, u32[]{:S(2)}) copy-start(bf16[18,1,640]{2,1,0:T(2,128)(2,1)S(1)} %collective-permute-done.3) | copy-start | bytes 69124
  45.8 1.8 copy-start.3
  46.0 1.6 copy-start.6
  46.5 4.9 %copy-start.25 = (bf16[18,1,640]{2,1,0:T(2,128)(2,1)}, bf16[18,1,640]{2,1,0:T(2,128)(2,1)S(1)}, u32[]{:S(2)}) copy-start(bf16[18,1,640]{2,1,0:T(2,128)(2,1)S(1)} %collective-permute-done.7) | copy-start | bytes 69124
  46.5 4.9 %copy-start.27 = (bf16[18,1,640]{2,1,0:T(2,128)(2,1)}, bf16[18,1,640]{2,1,0:T(2,128)(2,1)S(1)}, u32[]{:S(2)}) copy-start(bf16[18,1,640]{2,1,0:T(2,128)(2,1)S(1)} %collective-permute-done.6) | copy-start | bytes 69124
  107.5 14.2 %copy-start.29 = (pred[64,64]{1,0:T(8,128)(4,1)S(1)}, pred[64,64]{1,0:T(8,128)(4,1)}, u32[]{:S(2)}) copy-start(pred[64,64]{1,0:T(8,128)(4,1)} %iota_compare_fusion.1) | copy-start | bytes 12292
  107.5 25.1 %copy-start.22 = (bf16[18,1,640]{2,1,0:T(2,128)(2,1)S(1)}, bf16[18,1,640]{2,1,0:T(2,128)(2,1)}, u32[]{:S(2)}) copy-start(bf16[18,1,640]{2,1,0:T(2,128)(2,1)} %copy-done.21) | copy-start | bytes 69124
  107.5 25.1 %copy-start.24 = (bf16[18,1,640]{2,1,0:T(2,128)(2,1)S(1)}, bf16[18,1,640]{2,1,0:T(2,128)(2,1)}, u32[]{:S(2)}) copy-start(bf16[18,1,640]{2,1,0:T(2,128)(2,1)} %copy-done.23) | copy-start | bytes 69124
  133.7 1.8 copy-start.2
  138.9 2.0 copy-start.8
  196.8 2.6 %copy-start.5 = (f32[4,2,16,24,128]{4,3,2,1,0:T(8,128)S(1)}, f32[4,2,16,24,128]{4,3,2,1,0:T(8,128)}, u32[]{:S(2)}) copy-start(f32[4,2,16,24,128]{4,3,2,1,0:T(8,128)} %get-tuple-element.7) | copy-start | bytes 4718596
  216.3 26.8 %copy-start.11 = (f32[2,1,64,64]{2,3,1,0:T(8,128)S(1)}, f32[2,1,64,64]{2,3,1,0:T(8,128)}, u32[]{:S(2)}) copy-start(f32[2,1,64,64]{2,3,1,0:T(8,128)} %copy-done.10) | copy-start | bytes 98308
  (16 other events, 18.2 us)

commit v2 on v1

--- a/solution.py
+++ b/solution.py
@@ -76,10 +76,12 @@
     return pl.pallas_call(
         functools.partial(exchange_kernel, jobs=tuple(jobs), sizes=sizes),
         out_shape=tuple(shapes),
-        in_specs=[pl.BlockSpec(memory_space=pl.ANY)] * len(items),
-        out_specs=tuple(pl.BlockSpec(memory_space=pl.ANY) for _ in items),
+        in_specs=[pl.BlockSpec(memory_space=pltpu.VMEM)] * len(items),
+        out_specs=tuple(pl.BlockSpec(memory_space=pltpu.VMEM) for _ in items),
         scratch_shapes=scratch,
-        compiler_params=pltpu.CompilerParams(collective_id=cid, has_side_effects=True),
+        compiler_params=pltpu.CompilerParams(
+            collective_id=cid, has_side_effects=True, vmem_limit_bytes=48 * 1024 * 1024
+        ),
     )(*[x for x, _, _ in items])
 
 

time: 245 us -> 213 us (0.87)
  Pallas kernels: 121 us -> 102 us
  other arithmetic: 40.1 us -> 31.2 us
  local copies, waits for them, and re-layouts: 42.1 us -> 37.5 us
    pallas_call x8, Pallas kernels: 121 us -> 102 us  [exchange_many(): pl.pallas_call(functools.partial(exchange_kernel, jobs=tuple(jobs), sizes...]
  transfers between devices with their start and end apart: 8 -> 8, of which waited for: 0 -> 0; matrix products, arithmetic and copies ran while one was open for 9% -> 10% of each run, Pallas kernels for 0% -> 0%
where the time goes in v2:
time: 213 us; the launch traced here: 212 us
  Pallas kernels  102 us (48%)
  local copies, waits for them, and re-layouts  37.5 us (18%)
  other arithmetic  31.2 us (15%)
  starting transfers between devices  22.3 us (10%)
  matrix products  17.2 us (8%)
    pallas_call x8, Pallas kernels, exchange_many(): pl.pallas_call(functools.partial(exchange_kernel, jobs=tuple(jobs), sizes...  102 us
    another operation x4, other arithmetic, on_device(): lower = jnp.linalg.cholesky(gram)  11.9 us
    ppermute x4, starting transfers between devices, padded_2(): after = lax.ppermute(leading, axis, down)  11.3 us
    ppermute x4, starting transfers between devices, padded_2(): before = lax.ppermute(last, axis, up)  11 us
    another operation x3, other arithmetic, on_device(): lax.linalg.triangular_solve(lower, raw_part.transpose(1, 0, 2), left_side...  10.5 us
    dot_general x8, matrix products, exact_dot(): lax.dot_general(left.astype(jnp.float32), right.astype(jnp.float32), (con...  10.2 us
    another operation x1, local copies, waits for them, and re-layouts, block_sum(): value.reshape(blocks, block_rows, lanes)  5.71 us
    transpose x1, local copies, waits for them, and re-layouts, on_device(): rows = rows.transpose(2, 1, 0, 3).reshape(taps * channels, 2, rank)  5.53 us
  transfers between devices with their start and end apart: 8, of which 0 were waited for; matrix products, arithmetic and copies ran while one was open for 10% of the time, Pallas kernels for 0%

profile of v2, /device:TPU:1, one launch (start us, length us, event | category | flops | bytes accessed | tf_op | source)
XLA Modules:
  0.0 211.6 jit_solution(1046905665019134329)
XLA Ops:
  2.0 5.1 %collective-permute-start.1 = (bf16[1,16,640]{2,1,0:T(8,128)(2,1)}, bf16[1,16,640]{2,1,0:T(8,128)(2,1)S(1)}, u32[]{:S(2)}, u32[]{:S(2)}) collective-permute-start(bf16[1,16,640]{2,1,0:T(8,128)(2,1)} %get-tuple-element.48), channel_id=1, source_target_pairs={{4,0},{5,1},{6,2},{7,3},{12,8},{13,9},{14,10},{15,11},{20,16},{21,... | collective-permute-start | bytes 61448 | tf_op jit(solution)/shard_map/ppermute | solution.py:100
  9.8 3.6 %collective-permute-start.5 = (bf16[1,16,640]{2,1,0:T(8,128)(2,1)}, bf16[1,16,640]{2,1,0:T(8,128)(2,1)}, u32[]{:S(2)}, u32[]{:S(2)}) collective-permute-start(bf16[1,16,640]{2,1,0:T(8,128)(2,1)} %get-tuple-element.44), channel_id=1, source_target_pairs={{4,0},{5,1},{6,2},{7,3},{12,8},{13,9},{14,10},{15,11},{20,16},{21,... | collective-permute-start | bytes 61448 | tf_op jit(solution)/shard_map/ppermute | solution.py:100
  14.7 2.1 fusion.37
  16.8 1.9 fusion.32
  18.7 4.7 %reshape.189 = f32[9,640,2,64]{1,0,3,2:T(8,128)} reshape(f32[5760,2,64]{0,2,1:T(8,128)} %param.9) | data formatting | bytes 5898240 | tf_op jit(solution)/shard_map/reshape | solution.py:144
  23.5 4.4 %fusion.67 = (f32[1,640,9,64]{1,2,3,0:T(8,128)}, f32[1,640,9,64]{1,2,3,0:T(8,128)S(1)}) fusion(f32[2,640,9,64]{1,2,3,0:T(8,128)} %bitcast.219), kind=kLoop, calls=%fused_computation.132 | loop fusion | bytes 5898240 | tf_op jit(solution)/shard_map/slice | solution.py:146
  27.9 2.0 fusion
  32.9 4.0 %collective-permute-start.3 = (bf16[18,1,640]{2,1,0:T(2,128)(2,1)S(1)}, bf16[18,1,640]{2,1,0:T(2,128)(2,1)S(1)}, u32[]{:S(2)}, u32[]{:S(2)}) collective-permute-start(bf16[18,1,640]{2,1,0:T(2,128)(2,1)S(1)} %get-tuple-element.41), channel_id=1, source_target_pairs={{0,1},{1,2},{2,3},{4,5},{5,6},{6,7},{8,9},{9,10},{10,11},{12,13},{... | collective-permute-start | bytes 69128 | tf_op jit(solution)/shard_map/ppermute | solution.py:99
  39.4 4.4 %collective-permute-start.6 = (bf16[18,1,640]{2,1,0:T(2,128)(2,1)S(1)}, bf16[18,1,640]{2,1,0:T(2,128)(2,1)S(1)}, u32[]{:S(2)}, u32[]{:S(2)}) collective-permute-start(bf16[18,1,640]{2,1,0:T(2,128)(2,1)S(1)} %get-tuple-element.37), channel_id=1, source_target_pairs={{0,1},{1,2},{2,3},{4,5},{5,6},{6,7},{8,9},{9,10},{10,11},{12,13},{... | collective-permute-start | bytes 69128 | tf_op jit(solution)/shard_map/ppermute | solution.py:99
  43.9 1.6 fusion.17
  47.6 3.8 %fusion.2 = f32[18,18,9,64]{3,1,2,0:T(8,128)S(1)} fusion(f32[1,640,9,64]{1,2,3,0:T(8,128)S(1)} %copy-done.4, bf16[18,1,640]{2,1,0:T(2,128)(2,1)S(1)} %collective-permute-done.7, bf16[1,16,640]{2,1,0:T(8,128)(2,1)} %collective-permute-done.5, bf16[16,16,640]{2,1,0:T(8,128)(2,1)S(1)} %bitcast.237, bf16[1,16,640]{2,1,0:T(8,128)(2,1)} %collective-permute-done.4, ...), kind=kOutput, calls=%fused_computation.7 | convolution fusion | flops 1435345920 | bytes 2635776 | tf_op jit(solution)/shard_map/dot_general | solution.py:111
  57.5 10.4 %shard_map.68 = f32[8,80,128]{2,1,0:T(8,128)S(1)} custom-call(f32[8,80,128]{2,1,0:T(8,128)S(1)} %copy.84.refs_0_), custom_call_target="tpu_custom_call" | custom-call | tf_op jit(solution)/shard_map/pallas_call | solution.py:76
  68.0 13.3 %shard_map.69 = f32[32,5,64]{2,1,0:T(8,128)S(1)} custom-call(f32[32,5,64]{2,1,0:T(8,128)S(1)} %reshape.190.refs_0_), custom_call_target="tpu_custom_call" | custom-call | tf_op jit(solution)/shard_map/pallas_call | solution.py:76
  81.4 10.5 %shard_map.70 = f32[32,5,64]{2,1,0:T(8,128)S(1)} custom-call(f32[5,64]{1,0:T(8,128)S(1)} %reduce_sum.64.refs_0_), custom_call_target="tpu_custom_call" | custom-call | tf_op jit(solution)/shard_map/pallas_call | solution.py:76
  91.9 10.2 %shard_map.71 = f32[8,80,128]{2,1,0:T(8,128)S(1)} custom-call(f32[80,128]{1,0:T(8,128)S(1)} %reshape.191.refs_0_), custom_call_target="tpu_custom_call" | custom-call | tf_op jit(solution)/shard_map/pallas_call | solution.py:76
  103.1 11.7 %custom-call.9 = f32[2,64,64]{2,1,0:T(8,128)S(1)} custom-call(f32[2,64,64]{2,1,0:T(8,128)S(1)} %fusion.61), custom_call_target="Cholesky" | custom-call | tf_op jit(solution)/shard_map/jit(cholesky)/cholesky | solution.py:184
  115.1 9.8 %custom-call.10 = f32[2,1,64,64]{2,3,1,0:T(8,128)S(1)} custom-call(f32[2,1,64,64]{3,2,1,0:T(8,128)S(1)} %select_bitcast_fusion), custom_call_target="InvertDiagBlocksLowerTriangular" | custom-call | tf_op jit(solution)/shard_map/triangular_solve | solution.py:187
  132.2 1.7 concatenate.46
  136.8 5.5 %copy.91 = f32[9,640,2,64]{3,2,1,0:T(2,128)} copy(f32[9,640,2,64]{1,3,0,2:T(8,128)S(1)} %maximum_bitcast_fusion) | data formatting | bytes 5898240 | tf_op jit(solution)/shard_map/transpose | solution.py:178
  142.4 5.7 %reshape_reshape.15 = f32[32,180,128]{2,1,0:T(8,128)S(1)} reshape(f32[9,640,2,64]{3,2,1,0:T(2,128)} %copy.91) | data formatting | bytes 5898240 | tf_op jit(solution)/shard_map/reshape;reshape | solution.py:215
  149.9 21.3 %shard_map.72 = (f32[2,4,16,24,128]{4,3,2,1,0:T(8,128)S(1)}, f32[4,2,16,24,128]{4,3,2,1,0:T(8,128)S(1)}) custom-call(f32[2,4,16,24,128]{4,3,2,1,0:T(8,128)S(1)} %bitcast.217, f32[4,2,16,24,128]{4,3,2,1,0:T(8,128)} %bitcast.222), custom_call_target="tpu_custom_call" | custom-call | tf_op jit(solution)/shard_map/pallas_call | solution.py:76
  174.1 12.4 %shard_map.73 = (f32[4,16,24,128]{3,2,1,0:T(8,128)S(1)}, f32[2,16,24,128]{3,2,1,0:T(8,128)S(1)}) custom-call(f32[4,16,24,128]{3,2,1,0:T(8,128)S(1)} %reduce_sum.65.refs_0_, f32[2,16,24,128]{3,2,1,0:T(8,128)S(1)} %reduce_sum.66.refs_1_), custom_call_target="tpu_custom_call" | custom-call | tf_op jit(solution)/shard_map/pallas_call | solution.py:76
  186.6 15.2 %shard_map.74 = f32[32,24,128]{2,1,0:T(8,128)S(1)} custom-call(f32[32,24,128]{2,1,0:T(8,128)S(1)} %pad_maximum_fusion.3.refs_0_), custom_call_target="tpu_custom_call" | custom-call | tf_op jit(solution)/shard_map/pallas_call | solution.py:76
  201.8 8.7 %shard_map.75 = f32[8,24,128]{2,1,0:T(8,128)S(1)} custom-call(f32[24,128]{1,0:T(8,128)S(1)} %reduce_sum.69.refs_0_), custom_call_target="tpu_custom_call" | custom-call | tf_op jit(solution)/shard_map/pallas_call | solution.py:76
  (150 shorter events, 36.1 us)
Async XLA Ops:
  2.0 29.5 %collective-permute-start.1 = (bf16[1,16,640]{2,1,0:T(8,128)(2,1)}, bf16[1,16,640]{2,1,0:T(8,128)(2,1)S(1)}, u32[]{:S(2)}, u32[]{:S(2)}) collective-permute-start(bf16[1,16,640]{2,1,0:T(8,128)(2,1)} %get-tuple-element.48), channel_id=1, source_target_pairs={{4,0},{5,1},{6,2},{7,3},{12,8},{13,9},{14,10},{15,11},{20,16},{21,... | collective-permute-start | bytes 61448 | tf_op jit(solution)/shard_map/ppermute | solution.py:100
  7.1 24.4 %collective-permute-start = (bf16[1,16,640]{2,1,0:T(8,128)(2,1)}, bf16[1,16,640]{2,1,0:T(8,128)(2,1)S(1)}, u32[]{:S(2)}, u32[]{:S(2)}) collective-permute-start(bf16[1,16,640]{2,1,0:T(8,128)(2,1)} %get-tuple-element.47), channel_id=1, source_target_pairs={{0,4},{1,5},{2,6},{3,7},{8,12},{9,13},{10,14},{11,15},{16,20},{17,... | collective-permute-start | bytes 61448 | tf_op jit(solution)/shard_map/ppermute | solution.py:99
  9.8 27.1 %collective-permute-start.5 = (bf16[1,16,640]{2,1,0:T(8,128)(2,1)}, bf16[1,16,640]{2,1,0:T(8,128)(2,1)}, u32[]{:S(2)}, u32[]{:S(2)}) collective-permute-start(bf16[1,16,640]{2,1,0:T(8,128)(2,1)} %get-tuple-element.44), channel_id=1, source_target_pairs={{4,0},{5,1},{6,2},{7,3},{12,8},{13,9},{14,10},{15,11},{20,16},{21,... | collective-permute-start | bytes 61448 | tf_op jit(solution)/shard_map/ppermute | solution.py:100
  13.4 23.5 %collective-permute-start.4 = (bf16[1,16,640]{2,1,0:T(8,128)(2,1)}, bf16[1,16,640]{2,1,0:T(8,128)(2,1)}, u32[]{:S(2)}, u32[]{:S(2)}) collective-permute-start(bf16[1,16,640]{2,1,0:T(8,128)(2,1)} %get-tuple-element.43), channel_id=1, source_target_pairs={{0,4},{1,5},{2,6},{3,7},{8,12},{9,13},{10,14},{11,15},{16,20},{17,... | collective-permute-start | bytes 61448 | tf_op jit(solution)/shard_map/ppermute | solution.py:99
  23.5 4.4 %copy-start.9 = (bf16[1,16,16,640]{3,2,1,0:T(8,128)(2,1)S(1)}, bf16[1,16,16,640]{3,2,1,0:T(8,128)(2,1)}, u32[]{:S(2)}) copy-start(bf16[1,16,16,640]{3,2,1,0:T(8,128)(2,1)} %param.6) | copy-start | bytes 983044
  27.9 18.1 %slice-start = ((s8[7372800]{0:T(1024)(128)(4,1)}), s8[3178496]{0:T(1024)(128)(4,1)S(1)}, s32[]{:S(2)}) async-start(s8[7372800]{0:T(1024)(128)(4,1)} %bitcast.220), calls=%async_computation | async-start | bytes 6356992
  29.9 1.6 copy-start.1
  31.6 13.9 %collective-permute-start.2 = (bf16[18,1,640]{2,1,0:T(2,128)(2,1)S(1)}, bf16[18,1,640]{2,1,0:T(2,128)(2,1)S(1)}, u32[]{:S(2)}, u32[]{:S(2)}) collective-permute-start(bf16[18,1,640]{2,1,0:T(2,128)(2,1)S(1)} %get-tuple-element.42), channel_id=1, source_target_pairs={{1,0},{2,1},{3,2},{5,4},{6,5},{7,6},{9,8},{10,9},{11,10},{13,12},{... | collective-permute-start | bytes 69128 | tf_op jit(solution)/shard_map/ppermute | solution.py:100
  32.9 12.6 %collective-permute-start.3 = (bf16[18,1,640]{2,1,0:T(2,128)(2,1)S(1)}, bf16[18,1,640]{2,1,0:T(2,128)(2,1)S(1)}, u32[]{:S(2)}, u32[]{:S(2)}) collective-permute-start(bf16[18,1,640]{2,1,0:T(2,128)(2,1)S(1)} %get-tuple-element.41), channel_id=1, source_target_pairs={{0,1},{1,2},{2,3},{4,5},{5,6},{6,7},{8,9},{9,10},{10,11},{12,13},{... | collective-permute-start | bytes 69128 | tf_op jit(solution)/shard_map/ppermute | solution.py:99
  38.0 8.4 %collective-permute-start.7 = (bf16[18,1,640]{2,1,0:T(2,128)(2,1)S(1)}, bf16[18,1,640]{2,1,0:T(2,128)(2,1)S(1)}, u32[]{:S(2)}, u32[]{:S(2)}) collective-permute-start(bf16[18,1,640]{2,1,0:T(2,128)(2,1)S(1)} %get-tuple-element.38), channel_id=1, source_target_pairs={{1,0},{2,1},{3,2},{5,4},{6,5},{7,6},{9,8},{10,9},{11,10},{13,12},{... | collective-permute-start | bytes 69128 | tf_op jit(solution)/shard_map/ppermute | solution.py:100
  39.3 6.6 %slice-start.1 = ((s8[7372800]{0:T(1024)(128)(4,1)}), s8[4194304]{0:T(1024)(128)(4,1)S(1)}, s32[]{:S(2)}) async-start(s8[7372800]{0:T(1024)(128)(4,1)} %bitcast.220), calls=%async_computation.1 | async-start | bytes 8388608
  39.4 7.1 %collective-permute-start.6 = (bf16[18,1,640]{2,1,0:T(2,128)(2,1)S(1)}, bf16[18,1,640]{2,1,0:T(2,128)(2,1)S(1)}, u32[]{:S(2)}, u32[]{:S(2)}) collective-permute-start(bf16[18,1,640]{2,1,0:T(2,128)(2,1)S(1)} %get-tuple-element.37), channel_id=1, source_target_pairs={{0,1},{1,2},{2,3},{4,5},{5,6},{6,7},{8,9},{9,10},{10,11},{12,13},{... | collective-permute-start | bytes 69128 | tf_op jit(solution)/shard_map/ppermute | solution.py:99
  45.5 10.4 %copy-start.21 = (bf16[18,1,640]{2,1,0:T(2,128)(2,1)}, bf16[18,1,640]{2,1,0:T(2,128)(2,1)S(1)}, u32[]{:S(2)}) copy-start(bf16[18,1,640]{2,1,0:T(2,128)(2,1)S(1)} %collective-permute-done.2) | copy-start | bytes 69124
  45.5 10.4 %copy-start.23 = (bf16[18,1,640]{2,1,0:T(2,128)(2,1)}, bf16[18,1,640]{2,1,0:T(2,128)(2,1)S(1)}, u32[]{:S(2)}) copy-start(bf16[18,1,640]{2,1,0:T(2,128)(2,1)S(1)} %collective-permute-done.3) | copy-start | bytes 69124
  45.8 1.8 copy-start.4
  46.0 1.6 copy-start.6
  46.5 4.9 %copy-start.25 = (bf16[18,1,640]{2,1,0:T(2,128)(2,1)}, bf16[18,1,640]{2,1,0:T(2,128)(2,1)S(1)}, u32[]{:S(2)}) copy-start(bf16[18,1,640]{2,1,0:T(2,128)(2,1)S(1)} %collective-permute-done.7) | copy-start | bytes 69124
  46.5 4.9 %copy-start.27 = (bf16[18,1,640]{2,1,0:T(2,128)(2,1)}, bf16[18,1,640]{2,1,0:T(2,128)(2,1)S(1)}, u32[]{:S(2)}) copy-start(bf16[18,1,640]{2,1,0:T(2,128)(2,1)S(1)} %collective-permute-done.6) | copy-start | bytes 69124
  102.1 12.9 %copy-start.29 = (pred[64,64]{1,0:T(8,128)(4,1)S(1)}, pred[64,64]{1,0:T(8,128)(4,1)}, u32[]{:S(2)}) copy-start(pred[64,64]{1,0:T(8,128)(4,1)} %iota_compare_fusion.1) | copy-start | bytes 12292
  102.1 23.9 %copy-start.22 = (bf16[18,1,640]{2,1,0:T(2,128)(2,1)S(1)}, bf16[18,1,640]{2,1,0:T(2,128)(2,1)}, u32[]{:S(2)}) copy-start(bf16[18,1,640]{2,1,0:T(2,128)(2,1)} %copy-done.21) | copy-start | bytes 69124
  102.1 23.9 %copy-start.24 = (bf16[18,1,640]{2,1,0:T(2,128)(2,1)S(1)}, bf16[18,1,640]{2,1,0:T(2,128)(2,1)}, u32[]{:S(2)}) copy-start(bf16[18,1,640]{2,1,0:T(2,128)(2,1)} %copy-done.23) | copy-start | bytes 69124
  127.0 1.8 copy-start.3
  132.2 2.0 copy-start.8
  186.6 24.1 %copy-start.11 = (f32[2,1,64,64]{2,3,1,0:T(8,128)S(1)}, f32[2,1,64,64]{2,3,1,0:T(8,128)}, u32[]{:S(2)}) copy-start(f32[2,1,64,64]{2,3,1,0:T(8,128)} %copy-done.10) | copy-start | bytes 98308
  (16 other events, 17.7 us)

commit v3 on v2

--- a/solution.py
+++ b/solution.py
@@ -89,17 +89,69 @@
     return exchange_many([(x, axes, gather)], sizes, cid)[0]
 
 
-def padded_2(value, sides, width):
-    for axis, dim in sides:
-        size, length = (lax.axis_size(axis), value.shape[dim])
-        up = [(i, (i + 1) % size) for i in range(size - 1)]
-        down = [(j, i) for i, j in up]
-        last = lax.slice_in_dim(value, length - width, length, axis=dim)
-        leading = lax.slice_in_dim(value, 0, width, axis=dim)
-        before = lax.ppermute(last, axis, up)
-        after = lax.ppermute(leading, axis, down)
-        value = jnp.concatenate([before, value, after], axis=dim)
-    return value
+HALO_MOVES = ((1, 0), (-1, 0), (0, 1), (0, -1), (1, 1), (1, -1), (-1, 1), (-1, -1))
+
+
+def halo_kernel(*refs, sizes):
+    sends, recvs = refs[:3], refs[3:6]
+    send_sem, recv_sem = refs[6:8]
+    row, col = lax.axis_index("row"), lax.axis_index("col")
+
+    def target(dr, dc):
+        return {"row": lax.rem(row + dr + sizes["row"], sizes["row"]), "col": lax.rem(col + dc + sizes["col"], sizes["col"])}
+
+    barrier = pltpu.get_barrier_semaphore()
+    for dr, dc in HALO_MOVES:
+        pl.semaphore_signal(barrier, inc=1, device_id=target(dr, dc), device_id_type=pl.DeviceIdType.MESH)
+    pl.semaphore_wait(barrier, len(HALO_MOVES))
+    copies = []
+    for k, (dr, dc) in enumerate(HALO_MOVES):
+        kind, slot = (0, k) if k < 2 else ((1, k - 2) if k < 4 else (2, k - 4))
+        copy = pltpu.make_async_remote_copy(
+            src_ref=sends[kind].at[slot],
+            dst_ref=recvs[kind].at[slot],
+            send_sem=send_sem.at[k],
+            recv_sem=recv_sem.at[k],
+            device_id=target(dr, dc),
+            device_id_type=pl.DeviceIdType.MESH,
+        )
+        copy.start()
+        copies.append(copy)
+    for copy in copies:
+        copy.wait_send()
+        copy.wait_recv()
+
+
+def padded_pair(tiles, sizes):
+    rows_out = jnp.stack([tiles[:, -1], tiles[:, 0]])
+    cols_out = jnp.stack([tiles[:, :, -1], tiles[:, :, 0]])
+    corners_out = jnp.stack([tiles[:, -1, -1], tiles[:, -1, 0], tiles[:, 0, -1], tiles[:, 0, 0]])
+    sends = (rows_out, cols_out, corners_out)
+    recvs = pl.pallas_call(
+        functools.partial(halo_kernel, sizes=sizes),
+        out_shape=tuple(jax.ShapeDtypeStruct(x.shape, x.dtype) for x in sends),
+        in_specs=[pl.BlockSpec(memory_space=pltpu.VMEM)] * 3,
+        out_specs=tuple(pl.BlockSpec(memory_space=pltpu.VMEM) for _ in sends),
+        scratch_shapes=[pltpu.SemaphoreType.DMA((len(HALO_MOVES),)), pltpu.SemaphoreType.DMA((len(HALO_MOVES),))],
+        compiler_params=pltpu.CompilerParams(collective_id=8, has_side_effects=True),
+    )(*sends)
+    rows_in, cols_in, corners_in = recvs
+    row, col = lax.axis_index("row"), lax.axis_index("col")
+    up, down = row > 0, row < sizes["row"] - 1
+    left, right = col > 0, col < sizes["col"] - 1
+    zero = jnp.zeros((), tiles.dtype)
+    top = jnp.where(up, rows_in[0], zero)
+    bottom = jnp.where(down, rows_in[1], zero)
+    west = jnp.where(left, cols_in[0], zero)
+    east = jnp.where(right, cols_in[1], zero)
+    top_left = jnp.where(up & left, corners_in[0], zero)
+    top_right = jnp.where(up & right, corners_in[1], zero)
+    bottom_left = jnp.where(down & left, corners_in[2], zero)
+    bottom_right = jnp.where(down & right, corners_in[3], zero)
+    first = jnp.concatenate([top_left[:, None], top, top_right[:, None]], axis=1)
+    middle = jnp.concatenate([west[:, :, None], tiles, east[:, :, None]], axis=2)
+    last = jnp.concatenate([bottom_left[:, None], bottom, bottom_right[:, None]], axis=1)
+    return jnp.concatenate([first[:, None], middle, last[:, None]], axis=1)
 
 
 def silu_slope(pre_float):
@@ -125,11 +177,12 @@
     pixels = height * breadth
     rank = q_prev.shape[2]
     taps = len(TAPS)
-    sides = (("row", 0), ("col", 1))
     pre_float = pre_act.reshape(pixels, channels).astype(jnp.float32)
     hidden = jax.nn.silu(pre_float).astype(jnp.bfloat16)
-    grad_pad = padded_2(out_grad.reshape(height, breadth, channels), sides, 1)
-    input_pad = padded_2(x_input.reshape(height, breadth, channels), sides, 1)
+    both_pad = padded_pair(
+        jnp.stack([out_grad.reshape(height, breadth, channels), x_input.reshape(height, breadth, channels)]), sizes
+    )
+    grad_pad, input_pad = both_pad[0], both_pad[1]
     back_grad = jnp.zeros((pixels, channels), jnp.float32)
     for a, b in TAPS:
         window = grad_pad[1 - a : 1 - a + height, 1 - b : 1 - b + breadth].reshape(pixels, channels)

time: 213 us -> 202 us (0.948)
  starting transfers between devices: 22.3 us -> 0 us
  Pallas kernels: 102 us -> 109 us
  local copies, waits for them, and re-layouts: 37.5 us -> 40.6 us
  matrix products: 17.2 us -> 19.5 us
    ppermute x8 -> x0, starting transfers between devices: 22.3 us -> none  [the longest x4 11.3 us: padded_2(): after = lax.ppermute(leading, axis, down)]
    pallas_call x0 -> x1, Pallas kernels: none -> 9.81 us  [padded_pair(): pl.pallas_call(functools.partial(halo_kernel, sizes=sizes), out_shape=tup...]
    pallas_call x8, Pallas kernels: 102 us -> 99.1 us  [exchange_many(): pl.pallas_call(functools.partial(exchange_kernel, jobs=tuple(jobs), sizes...]
    reshape x9, local copies, waits for them, and re-layouts: 2.8 us -> 0.15 us  [on_device(): jnp.pad(first_image, ((1 + a, 1 - a), (1 + b, 1 - b), (0, 0)))]
    slice x2 -> x1, local copies, waits for them, and re-layouts: 2.72 us -> 5.31 us  [on_device(): grad_pad, input_pad = (both_pad[0], both_pad[1])]
    another operation x0 -> x4, local copies, waits for them, and re-layouts: none -> 2.28 us  [the longest x1 0.87 us: on_device(): grad_flat = grad_pad.reshape(-1, channels)]
    reshape x1, local copies, waits for them, and re-layouts: 4.71 us -> 2.56 us  [on_device(): q_prev.reshape(taps, channels, 2, rank).transpose(2, 1, 0, 3)]
    unnamed x66 -> x27, local copies, waits for them, and re-layouts: 4.54 us -> 6.3 us
  transfers between devices with their start and end apart: 8 -> 0, of which waited for: 0 -> 0; matrix products, arithmetic and copies ran while one was open for 10% -> 0% of each run, Pallas kernels for 0% -> 0%
where the time goes in v3:
time: 202 us
  Pallas kernels  109 us (54%)
  local copies, waits for them, and re-layouts  40.6 us (20%)
  other arithmetic  31.4 us (16%)
  matrix products  19.5 us (10%)
    pallas_call x8, Pallas kernels, exchange_many(): pl.pallas_call(functools.partial(exchange_kernel, jobs=tuple(jobs), sizes...  99.1 us
    another operation x4, other arithmetic, on_device(): lower = jnp.linalg.cholesky(gram)  11.9 us
    dot_general x8, matrix products, exact_dot(): lax.dot_general(left.astype(jnp.float32), right.astype(jnp.float32), (con...  11.2 us
    another operation x3, other arithmetic, on_device(): lax.linalg.triangular_solve(lower, raw_part.transpose(1, 0, 2), left_side...  9.91 us
    pallas_call x1, Pallas kernels, padded_pair(): pl.pallas_call(functools.partial(halo_kernel, sizes=sizes), out_shape=tup...  9.81 us
    dot_general x9, matrix products, on_device(): lax.dot_general(window, conv_weight[a + 1, b + 1], (((1,), (1,)), ((), ()...  6.63 us
    unnamed x27, local copies, waits for them, and re-layouts  6.3 us
    another operation x1, local copies, waits for them, and re-layouts, block_sum(): value.reshape(blocks, block_rows, lanes)  5.71 us

profile of v3, /device:TPU:1, one launch (start us, length us, event | category | flops | bytes accessed | tf_op | source)
XLA Modules:
  0.0 201.7 jit_solution(7529312374534349829)
XLA Ops:
  6.2 9.8 %shard_map.68 = (bf16[2,2,16,640]{3,2,1,0:T(8,128)(2,1)}, bf16[2,2,16,640]{3,2,1,0:T(8,128)(2,1)}, bf16[4,2,640]{2,1,0:T(2,128)(2,1)}) custom-call(bf16[2,2,16,640]{3,2,1,0:T(8,128)(2,1)} %copy.110.refs_0_, bf16[2,2,16,640]{3,2,1,0:T(8,128)(2,1)} %copy.111.refs_1_, bf16[4,2,640]{2,1,0:T(2,128)(2,1)} %pad_maximum_fusion.5.refs_2_), custom_call_target="tpu_custom_call" | custom-call | tf_op jit(solution)/shard_map/pallas_call | solution.py:130
  18.9 2.5 %pad_maximum_fusion = bf16[2,18,18,640]{3,0,2,1:T(2,128)(2,1)S(1)} fusion(bf16[2,1,18,640]{3,0,2,1:T(2,128)(2,1)S(1)} %get-tuple-element.85, bf16[2,16,1,640]{3,0,2,1:T(2,128)(2,1)S(1)} %get-tuple-element.79, bf16[1,16,16,640]{3,0,2,1:T(2,128)(2,1)S(1)} %copy.108, bf16[1,16,16,640]{3,0,2,1:T(2,128)(2,1)S(1)} %copy.107, ...), kind=kLoop, calls=%fused_computation.27 | loop fusion | flops 4976640 | bytes 1658880 | tf_op jit(solution)/shard_map/concatenate | solution.py:154
  21.4 5.3 %slice_reduce_fusion = (bf16[18,18,640]{2,1,0:T(8,128)(2,1)}, bf16[18,18,640]{2,1,0:T(8,128)(2,1)S(1)}, bf16[1,18,18,640]{3,0,2,1:T(2,128)(2,1)}, bf16[1,18,18,640]{3,0,2,1:T(2,128)(2,1)}) fusion(bf16[2,18,18,640]{3,0,2,1:T(2,128)(2,1)S(1)} %pad_maximum_fusion), kind=kLoop, calls=%fused_computation.129 | loop fusion | bytes 2488320 | tf_op jit(solution)/shard_map/slice | solution.py:185
  27.6 2.6 %reshape.263 = f32[9,640,2,64]{1,0,3,2:T(8,128)} reshape(f32[5760,2,64]{0,2,1:T(8,128)S(1)} %copy-done.1) | data formatting | bytes 5898240 | tf_op jit(solution)/shard_map/reshape | solution.py:197
  30.2 2.9 %fusion.55 = (f32[1,640,9,64]{1,2,3,0:T(8,128)S(1)}, f32[1,640,9,64]{1,2,3,0:T(8,128)S(1)}) fusion(f32[2,640,9,64]{1,2,3,0:T(8,128)} %bitcast.258), kind=kLoop, calls=%fused_computation.131 | loop fusion | bytes 5898240 | tf_op jit(solution)/shard_map/slice | solution.py:199
  33.1 2.0 %fusion = f32[16,16,9,64]{3,1,2,0:T(8,128)S(1)} fusion(f32[1,640,9,64]{1,2,3,0:T(8,128)S(1)} %get-tuple-element.27, bf16[1,16,16,640]{3,2,1,0:T(8,128)(2,1)S(1)} %copy-done.5), kind=kOutput, calls=%fused_computation.5 | convolution fusion | flops 1133445120 | bytes 2392064 | tf_op jit(solution)/shard_map/dot_general | solution.py:163
  36.1 1.6 reshape.264
  41.0 1.8 fusion.16
  42.7 1.6 convolution_add_fusion.7
  47.9 2.9 %fusion.2 = f32[18,18,9,64]{3,1,2,0:T(8,128)S(1)} fusion(f32[1,640,9,64]{1,2,3,0:T(8,128)S(1)} %get-tuple-element.26, bf16[1,18,18,640]{3,0,2,1:T(2,128)(2,1)S(1)} %copy-done.2), kind=kOutput, calls=%fused_computation.7 | convolution fusion | flops 1433272320 | bytes 2635776 | tf_op jit(solution)/shard_map/dot_general | solution.py:163
  51.7 8.0 %shard_map.69 = f32[8,80,128]{2,1,0:T(8,128)S(1)} custom-call(f32[8,80,128]{2,1,0:T(8,128)S(1)} %copy.128.refs_0_), custom_call_target="tpu_custom_call" | custom-call | tf_op jit(solution)/shard_map/pallas_call | solution.py:76
  59.9 12.7 %shard_map.70 = f32[32,5,64]{2,1,0:T(8,128)S(1)} custom-call(f32[32,5,64]{2,1,0:T(8,128)S(1)} %reshape.265.refs_0_), custom_call_target="tpu_custom_call" | custom-call | tf_op jit(solution)/shard_map/pallas_call | solution.py:76
  72.6 10.5 %shard_map.71 = f32[32,5,64]{2,1,0:T(8,128)S(1)} custom-call(f32[5,64]{1,0:T(8,128)S(1)} %reduce_sum.64.refs_0_), custom_call_target="tpu_custom_call" | custom-call | tf_op jit(solution)/shard_map/pallas_call | solution.py:76
  83.2 10.9 %shard_map.72 = f32[8,80,128]{2,1,0:T(8,128)S(1)} custom-call(f32[80,128]{1,0:T(8,128)S(1)} %reshape.266.refs_0_), custom_call_target="tpu_custom_call" | custom-call | tf_op jit(solution)/shard_map/pallas_call | solution.py:76
  95.0 11.7 %custom-call.9 = f32[2,64,64]{2,1,0:T(8,128)S(1)} custom-call(f32[2,64,64]{2,1,0:T(8,128)S(1)} %fusion.43), custom_call_target="Cholesky" | custom-call | tf_op jit(solution)/shard_map/jit(cholesky)/cholesky | solution.py:237
  107.0 9.8 %custom-call.10 = f32[2,1,64,64]{2,3,1,0:T(8,128)S(1)} custom-call(f32[2,1,64,64]{3,2,1,0:T(8,128)S(1)} %select_bitcast_fusion), custom_call_target="InvertDiagBlocksLowerTriangular" | custom-call | tf_op jit(solution)/shard_map/triangular_solve | solution.py:240
  119.3 2.0 convolution_bitcast_fusion
  122.2 1.9 concatenate.26
  127.4 5.6 %copy.135 = f32[9,640,2,64]{3,2,1,0:T(2,128)} copy(f32[9,640,2,64]{1,3,0,2:T(8,128)S(1)} %maximum_bitcast_fusion) | data formatting | bytes 5898240 | tf_op jit(solution)/shard_map/transpose | solution.py:231
  133.0 5.7 %reshape_reshape.11 = f32[32,180,128]{2,1,0:T(8,128)S(1)} reshape(f32[9,640,2,64]{3,2,1,0:T(2,128)} %copy.135) | data formatting | bytes 5898240 | tf_op jit(solution)/shard_map/reshape;reshape | solution.py:268
  140.5 21.3 %shard_map.73 = (f32[2,4,16,24,128]{4,3,2,1,0:T(8,128)S(1)}, f32[4,2,16,24,128]{4,3,2,1,0:T(8,128)S(1)}) custom-call(f32[2,4,16,24,128]{4,3,2,1,0:T(8,128)S(1)} %bitcast.254, f32[4,2,16,24,128]{4,3,2,1,0:T(8,128)} %bitcast.261), custom_call_target="tpu_custom_call" | custom-call | tf_op jit(solution)/shard_map/pallas_call | solution.py:76
  164.6 12.1 %shard_map.74 = (f32[4,16,24,128]{3,2,1,0:T(8,128)S(1)}, f32[2,16,24,128]{3,2,1,0:T(8,128)S(1)}) custom-call(f32[4,16,24,128]{3,2,1,0:T(8,128)S(1)} %reduce_sum.65.refs_0_, f32[2,16,24,128]{3,2,1,0:T(8,128)S(1)} %reduce_sum.66.refs_1_), custom_call_target="tpu_custom_call" | custom-call | tf_op jit(solution)/shard_map/pallas_call | solution.py:76
  176.9 14.1 %shard_map.75 = f32[32,24,128]{2,1,0:T(8,128)S(1)} custom-call(f32[32,24,128]{2,1,0:T(8,128)S(1)} %pad_maximum_fusion.1.refs_0_), custom_call_target="tpu_custom_call" | custom-call | tf_op jit(solution)/shard_map/pallas_call | solution.py:76
  191.0 9.5 %shard_map.76 = f32[8,24,128]{2,1,0:T(8,128)S(1)} custom-call(f32[24,128]{1,0:T(8,128)S(1)} %reduce_sum.69.refs_0_), custom_call_target="tpu_custom_call" | custom-call | tf_op jit(solution)/shard_map/pallas_call | solution.py:76
  (108 shorter events, 31.5 us)
Async XLA Ops:
  21.4 6.2 %copy-start.1 = (f32[5760,2,64]{0,2,1:T(8,128)S(1)}, f32[5760,2,64]{0,2,1:T(8,128)}, u32[]{:S(2)}) copy-start(f32[5760,2,64]{0,2,1:T(8,128)} %param.9) | copy-start | bytes 8847364
  30.2 2.9 %copy-start.5 = (bf16[1,16,16,640]{3,2,1,0:T(8,128)(2,1)S(1)}, bf16[1,16,16,640]{3,2,1,0:T(8,128)(2,1)}, u32[]{:S(2)}) copy-start(bf16[1,16,16,640]{3,2,1,0:T(8,128)(2,1)} %param.6) | copy-start | bytes 983044
  35.2 2.6 %copy-start.4 = (bf16[324,640]{1,0:T(8,128)(2,1)S(1)}, bf16[324,640]{1,0:T(8,128)(2,1)}, u32[]{:S(2)}) copy-start(bf16[324,640]{1,0:T(8,128)(2,1)} %reshape_squeeze.6) | copy-start | bytes 1244164
  37.7 6.6 %slice-start = ((s8[7372800]{0:T(1024)(128)(4,1)}), s8[4194304]{0:T(1024)(128)(4,1)S(1)}, s32[]{:S(2)}) async-start(s8[7372800]{0:T(1024)(128)(4,1)} %bitcast.259), calls=%async_computation | async-start | bytes 8388608
  40.7 3.7 %slice-start.1 = ((s8[7372800]{0:T(1024)(128)(4,1)}), s8[3178496]{0:T(1024)(128)(4,1)S(1)}, s32[]{:S(2)}) async-start(s8[7372800]{0:T(1024)(128)(4,1)} %bitcast.259), calls=%async_computation.1 | async-start | bytes 6356992
  46.7 1.1 copy-start.2
  59.7 58.2 %copy-start.6 = (bf16[1,16,16,640]{3,2,1,0:T(8,128)(2,1)S(1)}, bf16[1,16,16,640]{3,2,1,0:T(8,128)(2,1)}, u32[]{:S(2)}) copy-start(bf16[1,16,16,640]{3,2,1,0:T(8,128)(2,1)} %param.6) | copy-start | bytes 983044
  116.9 1.9 copy-start.7
  118.8 2.5 %copy-start.3 = (bf16[18,18,640]{2,1,0:T(8,128)(2,1)S(1)}, bf16[18,18,640]{2,1,0:T(8,128)(2,1)}, u32[]{:S(2)}) copy-start(bf16[18,18,640]{2,1,0:T(8,128)(2,1)} %get-tuple-element.24) | copy-start | bytes 1244164
  161.8 1.2 copy-start
  164.6 36.1 %copy-start.8 = (f32[2,1,64,64]{2,3,1,0:T(8,128)S(1)}, f32[2,1,64,64]{2,3,1,0:T(8,128)}, u32[]{:S(2)}) copy-start(f32[2,1,64,64]{2,3,1,0:T(8,128)} %copy-done.7) | copy-start | bytes 98308

commit v4 on v3

--- a/solution.py
+++ b/solution.py
@@ -246,16 +246,84 @@
     return (basis_out, factor_out)
 
 
+def allsum_kernel(p_ref, o_ref, recv1, send2, recv2, piece, recv3, chunk, *sems, sizes):
+    group_axes, ring_axes = ("row", "col"), ("dp",)
+    n_group = sizes["row"] * sizes["col"]
+    n_ring = sizes["dp"]
+    me_group = lax.axis_index("row") * sizes["col"] + lax.axis_index("col")
+    me_ring = lax.axis_index("dp")
+    barrier = pltpu.get_barrier_semaphore()
+    for s in range(1, n_group):
+        peer = member_coords(lax.rem(me_group + s, n_group), group_axes, sizes)
+        pl.semaphore_signal(barrier, inc=1, device_id=peer, device_id_type=pl.DeviceIdType.MESH)
+    for s in range(1, n_ring):
+        peer = member_coords(lax.rem(me_ring + s, n_ring), ring_axes, sizes)
+        pl.semaphore_signal(barrier, inc=1, device_id=peer, device_id_type=pl.DeviceIdType.MESH)
+    pl.semaphore_wait(barrier, n_group - 1 + n_ring - 1)
+
+    def phase(source, target, me, n, axes, send_sem, recv_sem, local_sem, gather):
+        copies = []
+        for s in range(1, n):
+            dst = lax.rem(me + s, n)
+            copy = pltpu.make_async_remote_copy(
+                src_ref=source if gather else source.at[dst],
+                dst_ref=target.at[me],
+                send_sem=send_sem.at[s - 1],
+                recv_sem=recv_sem.at[s - 1],
+                device_id=member_coords(dst, axes, sizes),
+                device_id_type=pl.DeviceIdType.MESH,
+            )
+            copy.start()
+            copies.append(copy)
+        local = pltpu.make_async_copy(source if gather else source.at[me], target.at[me], local_sem)
+        local.start()
+        for copy in copies:
+            copy.wait_send()
+            copy.wait_recv()
+        local.wait()
+
+    phase(p_ref, recv1, me_group, n_group, group_axes, sems[0], sems[1], sems[8], False)
+    total = recv1[0]
+    for j in range(1, n_group):
+        total = total + recv1[j]
+    for j in range(n_ring):
+        send2[j] = total[j : j + 1]
+    phase(send2, recv2, me_ring, n_ring, ring_axes, sems[2], sems[3], sems[9], False)
+    reduced = recv2[0]
+    for j in range(1, n_ring):
+        reduced = reduced + recv2[j]
+    piece[...] = reduced
+    phase(piece, recv3, me_ring, n_ring, ring_axes, sems[4], sems[5], sems[10], True)
+    for j in range(n_ring):
+        chunk[j : j + 1] = recv3[j]
+    phase(chunk, o_ref, me_group, n_group, group_axes, sems[6], sems[7], sems[11], True)
+
+
 def all_sum_small(value, sizes):
     shape = value.shape
-    rows, group = shape[0], sizes["row"] * sizes["col"]
-    flat = value.reshape(rows, -1)
-    part = exchange(flat.reshape(group, rows // group, -1), ("row", "col"), sizes, 0).sum(0)
-    piece = part.reshape(sizes["dp"], -1, 64)
-    piece = exchange(piece, ("dp",), sizes, 1).sum(0)
-    part = exchange(piece, ("dp",), sizes, 2, gather=True).reshape(part.shape)
-    flat = exchange(part, ("row", "col"), sizes, 3, gather=True).reshape(flat.shape)
-    return flat.reshape(shape)
+    n_group = sizes["row"] * sizes["col"]
+    n_ring = sizes["dp"]
+    width = value.size // (n_group * n_ring)
+    parts = value.reshape(n_group, n_ring, width)
+    vmem = pl.BlockSpec(memory_space=pltpu.VMEM)
+    out = pl.pallas_call(
+        functools.partial(allsum_kernel, sizes=sizes),
+        out_shape=jax.ShapeDtypeStruct(parts.shape, parts.dtype),
+        in_specs=[vmem],
+        out_specs=vmem,
+        scratch_shapes=[
+            pltpu.VMEM((n_group, n_ring, width), jnp.float32),
+            pltpu.VMEM((n_ring, 1, width), jnp.float32),
+            pltpu.VMEM((n_ring, 1, width), jnp.float32),
+            pltpu.VMEM((1, width), jnp.float32),
+            pltpu.VMEM((n_ring, 1, width), jnp.float32),
+            pltpu.VMEM((n_ring, width), jnp.float32),
+        ]
+        + [pltpu.SemaphoreType.DMA((n - 1,)) for n in (n_group, n_group, n_ring, n_ring, n_ring, n_ring, n_group, n_group)]
+        + [pltpu.SemaphoreType.DMA] * 4,
+        compiler_params=pltpu.CompilerParams(collective_id=0, has_side_effects=True),
+    )(parts)
+    return out.reshape(shape)
 
 
 def block_sum(value, sizes):

time: 202 us -> 199 us (0.985)
  Pallas kernels: 109 us -> 103 us
    pallas_call x8 -> x4, Pallas kernels: 99.1 us -> 58.5 us  [exchange_many(): pl.pallas_call(functools.partial(exchange_kernel, jobs=tuple(jobs), sizes...]
    pallas_call x0 -> x1, Pallas kernels: none -> 35.2 us  [all_sum_small(): pl.pallas_call(functools.partial(allsum_kernel, sizes=sizes), out_shape=j...]
    reshape x2 -> x3, local copies, waits for them, and re-layouts: 0.16 us -> 2.93 us  [the longest x2 1.65 us: all_sum_small(): return out.reshape(shape)]
    unnamed x27 -> x26, local copies, waits for them, and re-layouts: 6.3 us -> 6.23 us
where the time goes in v4:
time: 199 us; the launch traced here: 198 us
  Pallas kernels  103 us (52%)
  local copies, waits for them, and re-layouts  42.3 us (21%)
  other arithmetic  31.3 us (16%)
  matrix products  19.5 us (10%)
    pallas_call x4, Pallas kernels, exchange_many(): pl.pallas_call(functools.partial(exchange_kernel, jobs=tuple(jobs), sizes...  58.5 us
    pallas_call x1, Pallas kernels, all_sum_small(): pl.pallas_call(functools.partial(allsum_kernel, sizes=sizes), out_shape=j...  35.2 us
    another operation x4, other arithmetic, on_device(): lower = jnp.linalg.cholesky(gram)  11.9 us
    dot_general x8, matrix products, exact_dot(): lax.dot_general(left.astype(jnp.float32), right.astype(jnp.float32), (con...  11.2 us
    another operation x3, other arithmetic, on_device(): lax.linalg.triangular_solve(lower, raw_part.transpose(1, 0, 2), left_side...  9.91 us
    pallas_call x1, Pallas kernels, padded_pair(): pl.pallas_call(functools.partial(halo_kernel, sizes=sizes), out_shape=tup...  9.8 us
    dot_general x9, matrix products, on_device(): lax.dot_general(window, conv_weight[a + 1, b + 1], (((1,), (1,)), ((), ()...  6.63 us
    unnamed x26, local copies, waits for them, and re-layouts  6.23 us

profile of v4, /device:TPU:1, one launch (start us, length us, event | category | flops | bytes accessed | tf_op | source)
XLA Modules:
  0.0 197.9 jit_solution(9589875757463770873)
XLA Ops:
  2.1 1.5 copy.113
  6.2 9.8 %shard_map.68 = (bf16[2,2,16,640]{3,2,1,0:T(8,128)(2,1)}, bf16[2,2,16,640]{3,2,1,0:T(8,128)(2,1)}, bf16[4,2,640]{2,1,0:T(2,128)(2,1)}) custom-call(bf16[2,2,16,640]{3,2,1,0:T(8,128)(2,1)} %copy.116.refs_0_, bf16[2,2,16,640]{3,2,1,0:T(8,128)(2,1)} %copy.117.refs_1_, bf16[4,2,640]{2,1,0:T(2,128)(2,1)} %pad_maximum_fusion.5.refs_2_), custom_call_target="tpu_custom_call" | custom-call | tf_op jit(solution)/shard_map/pallas_call | solution.py:130
  18.9 2.5 %pad_maximum_fusion = bf16[2,18,18,640]{3,0,2,1:T(2,128)(2,1)S(1)} fusion(bf16[2,1,18,640]{3,0,2,1:T(2,128)(2,1)S(1)} %get-tuple-element.85, bf16[2,16,1,640]{3,0,2,1:T(2,128)(2,1)S(1)} %get-tuple-element.79, bf16[1,16,16,640]{3,0,2,1:T(2,128)(2,1)S(1)} %copy.114, bf16[1,16,16,640]{3,0,2,1:T(2,128)(2,1)S(1)} %copy.113, ...), kind=kLoop, calls=%fused_computation.27 | loop fusion | flops 4976640 | bytes 1658880 | tf_op jit(solution)/shard_map/concatenate | solution.py:154
  21.4 5.3 %slice_reduce_fusion = (bf16[18,18,640]{2,1,0:T(8,128)(2,1)}, bf16[18,18,640]{2,1,0:T(8,128)(2,1)S(1)}, bf16[1,18,18,640]{3,0,2,1:T(2,128)(2,1)}, bf16[1,18,18,640]{3,0,2,1:T(2,128)(2,1)}) fusion(bf16[2,18,18,640]{3,0,2,1:T(2,128)(2,1)S(1)} %pad_maximum_fusion), kind=kLoop, calls=%fused_computation.129 | loop fusion | bytes 2488320 | tf_op jit(solution)/shard_map/slice | solution.py:185
  27.6 2.5 %reshape.263 = f32[9,640,2,64]{1,0,3,2:T(8,128)} reshape(f32[5760,2,64]{0,2,1:T(8,128)S(1)} %copy-done.1) | data formatting | bytes 5898240 | tf_op jit(solution)/shard_map/reshape | solution.py:197
  30.1 2.9 %fusion.54 = (f32[1,640,9,64]{1,2,3,0:T(8,128)S(1)}, f32[1,640,9,64]{1,2,3,0:T(8,128)S(1)}) fusion(f32[2,640,9,64]{1,2,3,0:T(8,128)} %bitcast.254), kind=kLoop, calls=%fused_computation.131 | loop fusion | bytes 5898240 | tf_op jit(solution)/shard_map/slice | solution.py:199
  33.1 2.0 %fusion = f32[16,16,9,64]{3,1,2,0:T(8,128)S(1)} fusion(f32[1,640,9,64]{1,2,3,0:T(8,128)S(1)} %get-tuple-element.27, bf16[1,16,16,640]{3,2,1,0:T(8,128)(2,1)S(1)} %copy-done.5), kind=kOutput, calls=%fused_computation.5 | convolution fusion | flops 1133445120 | bytes 2392064 | tf_op jit(solution)/shard_map/dot_general | solution.py:163
  36.1 1.6 reshape.264
  40.9 1.8 fusion.16
  42.7 1.6 convolution_add_fusion.7
  47.9 2.9 %fusion.2 = f32[18,18,9,64]{3,1,2,0:T(8,128)S(1)} fusion(f32[1,640,9,64]{1,2,3,0:T(8,128)S(1)} %get-tuple-element.26, bf16[1,18,18,640]{3,0,2,1:T(2,128)(2,1)S(1)} %copy-done.2), kind=kOutput, calls=%fused_computation.7 | convolution fusion | flops 1433272320 | bytes 2635776 | tf_op jit(solution)/shard_map/dot_general | solution.py:163
  52.8 35.2 %shard_map.69 = f32[8,32,320]{2,1,0:T(8,128)} custom-call(f32[8,32,320]{2,1,0:T(8,128)} %reshape.265.p_ref), custom_call_target="tpu_custom_call" | custom-call | tf_op jit(solution)/shard_map/pallas_call | solution.py:309
  90.2 11.7 %custom-call.9 = f32[2,64,64]{2,1,0:T(8,128)S(1)} custom-call(f32[2,64,64]{2,1,0:T(8,128)S(1)} %fusion.43), custom_call_target="Cholesky" | custom-call | tf_op jit(solution)/shard_map/jit(cholesky)/cholesky | solution.py:237
  102.2 9.8 %custom-call.10 = f32[2,1,64,64]{2,3,1,0:T(8,128)S(1)} custom-call(f32[2,1,64,64]{3,2,1,0:T(8,128)S(1)} %select_bitcast_fusion), custom_call_target="InvertDiagBlocksLowerTriangular" | custom-call | tf_op jit(solution)/shard_map/triangular_solve | solution.py:240
  114.3 2.0 %convolution_bitcast_fusion = f32[1,640,9,64]{1,3,2,0:T(8,128)} fusion(bf16[256,640,1]{1,0,2:T(8,128)(2,1)S(1)} %bitcast.274, f32[9,64,256]{2,1,0:T(8,128)S(1)} %bitcast.264), kind=kOutput, calls=%fused_computation.11 | convolution fusion | flops 1132462080 | bytes 2392064 | tf_op jit(solution)/shard_map/dot_general | solution.py:163
  117.2 1.9 concatenate.26
  120.9 1.6 maximum_bitcast_fusion
  122.4 5.6 %copy.144 = f32[9,640,2,64]{3,2,1,0:T(2,128)} copy(f32[9,640,2,64]{1,3,0,2:T(8,128)S(1)} %maximum_bitcast_fusion) | data formatting | bytes 5898240 | tf_op jit(solution)/shard_map/transpose | solution.py:231
  128.0 5.4 %reshape_reshape.3 = f32[32,180,128]{2,1,0:T(8,128)S(1)} reshape(f32[9,640,2,64]{3,2,1,0:T(2,128)} %copy.144) | data formatting | bytes 5898240 | tf_op jit(solution)/shard_map/reshape;reshape | solution.py:336
  135.2 21.6 %shard_map.70 = (f32[2,4,16,24,128]{4,3,2,1,0:T(8,128)S(1)}, f32[4,2,16,24,128]{4,3,2,1,0:T(8,128)S(1)}) custom-call(f32[2,4,16,24,128]{4,3,2,1,0:T(8,128)S(1)} %bitcast.250, f32[4,2,16,24,128]{4,3,2,1,0:T(8,128)} %bitcast.257), custom_call_target="tpu_custom_call" | custom-call | tf_op jit(solution)/shard_map/pallas_call | solution.py:76
  158.2 1.5 reduce_sum.46.refs_1_
  159.7 13.5 %shard_map.71 = (f32[4,16,24,128]{3,2,1,0:T(8,128)S(1)}, f32[2,16,24,128]{3,2,1,0:T(8,128)S(1)}) custom-call(f32[4,16,24,128]{3,2,1,0:T(8,128)S(1)} %reduce_sum.45.refs_0_, f32[2,16,24,128]{3,2,1,0:T(8,128)S(1)} %reduce_sum.46.refs_1_), custom_call_target="tpu_custom_call" | custom-call | tf_op jit(solution)/shard_map/pallas_call | solution.py:76
  173.3 12.9 %shard_map.72 = f32[32,24,128]{2,1,0:T(8,128)S(1)} custom-call(f32[32,24,128]{2,1,0:T(8,128)S(1)} %pad_maximum_fusion.1.refs_0_), custom_call_target="tpu_custom_call" | custom-call | tf_op jit(solution)/shard_map/pallas_call | solution.py:76
  186.2 10.6 %shard_map.73 = f32[8,24,128]{2,1,0:T(8,128)S(1)} custom-call(f32[24,128]{1,0:T(8,128)S(1)} %reduce_sum.49.refs_0_), custom_call_target="tpu_custom_call" | custom-call | tf_op jit(solution)/shard_map/pallas_call | solution.py:76
  (100 shorter events, 28.9 us)
Async XLA Ops:
  21.4 6.2 %copy-start.1 = (f32[5760,2,64]{0,2,1:T(8,128)S(1)}, f32[5760,2,64]{0,2,1:T(8,128)}, u32[]{:S(2)}) copy-start(f32[5760,2,64]{0,2,1:T(8,128)} %param.9) | copy-start | bytes 8847364
  30.1 2.9 %copy-start.5 = (bf16[1,16,16,640]{3,2,1,0:T(8,128)(2,1)S(1)}, bf16[1,16,16,640]{3,2,1,0:T(8,128)(2,1)}, u32[]{:S(2)}) copy-start(bf16[1,16,16,640]{3,2,1,0:T(8,128)(2,1)} %param.6) | copy-start | bytes 983044
  35.1 2.6 %copy-start.4 = (bf16[324,640]{1,0:T(8,128)(2,1)S(1)}, bf16[324,640]{1,0:T(8,128)(2,1)}, u32[]{:S(2)}) copy-start(bf16[324,640]{1,0:T(8,128)(2,1)} %reshape_squeeze.6) | copy-start | bytes 1244164
  37.7 6.6 %slice-start = ((s8[7372800]{0:T(1024)(128)(4,1)}), s8[4194304]{0:T(1024)(128)(4,1)S(1)}, s32[]{:S(2)}) async-start(s8[7372800]{0:T(1024)(128)(4,1)} %bitcast.255), calls=%async_computation | async-start | bytes 8388608
  40.6 3.7 %slice-start.1 = ((s8[7372800]{0:T(1024)(128)(4,1)}), s8[3178496]{0:T(1024)(128)(4,1)S(1)}, s32[]{:S(2)}) async-start(s8[7372800]{0:T(1024)(128)(4,1)} %bitcast.255), calls=%async_computation.1 | async-start | bytes 6356992
  46.7 1.1 copy-start.2
  51.5 61.4 %copy-start.6 = (bf16[1,16,16,640]{3,2,1,0:T(8,128)(2,1)S(1)}, bf16[1,16,16,640]{3,2,1,0:T(8,128)(2,1)}, u32[]{:S(2)}) copy-start(bf16[1,16,16,640]{3,2,1,0:T(8,128)(2,1)} %param.6) | copy-start | bytes 983044
  112.0 1.1 copy-start.7
  113.8 2.5 %copy-start.3 = (bf16[18,18,640]{2,1,0:T(8,128)(2,1)S(1)}, bf16[18,18,640]{2,1,0:T(8,128)(2,1)}, u32[]{:S(2)}) copy-start(bf16[18,18,640]{2,1,0:T(8,128)(2,1)} %get-tuple-element.24) | copy-start | bytes 1244164
  156.8 1.2 copy-start
  159.7 37.2 %copy-start.8 = (f32[2,1,64,64]{2,3,1,0:T(8,128)S(1)}, f32[2,1,64,64]{2,3,1,0:T(8,128)}, u32[]{:S(2)}) copy-start(f32[2,1,64,64]{2,3,1,0:T(8,128)} %copy-done.7) | copy-start | bytes 98308

commit v5 on v3

--- a/solution.py
+++ b/solution.py
@@ -9,11 +9,37 @@
 from jax.sharding import PartitionSpec as P
 
 
+def split_of(sizes):
+    return 4 if sizes["dp"] % 4 == 0 else 1
+
+
+def member_index(axis, sizes):
+    if axis == "dp_y":
+        return lax.rem(lax.axis_index("dp"), split_of(sizes))
+    if axis == "dp_z":
+        return lax.axis_index("dp") // split_of(sizes)
+    return lax.axis_index(axis)
+
+
+def axis_length(axis, sizes):
+    if axis == "dp_y":
+        return split_of(sizes)
+    if axis == "dp_z":
+        return sizes["dp"] // split_of(sizes)
+    return sizes[axis]
+
+
 def member_coords(j, axes, sizes):
     coords = {}
     for axis in reversed(axes):
-        coords[axis] = lax.rem(j, sizes[axis])
-        j = j // sizes[axis]
+        index = lax.rem(j, axis_length(axis, sizes))
+        j = j // axis_length(axis, sizes)
+        if axis == "dp_y":
+            coords["dp"] = lax.axis_index("dp") // split_of(sizes) * split_of(sizes) + index
+        elif axis == "dp_z":
+            coords["dp"] = index * split_of(sizes) + lax.rem(lax.axis_index("dp"), split_of(sizes))
+        else:
+            coords[axis] = index
     return coords
 
 
@@ -246,16 +272,107 @@
     return (basis_out, factor_out)
 
 
+def allsum_kernel(p_ref, o_ref, *scratch, sizes):
+    recv1, send_y, recv_y, send_z, recv_z, piece, recv_z2, zrows, recv_y2, chunk = scratch[:10]
+    sems = scratch[10:]
+    groups = (("row", "col"), ("dp_y",), ("dp_z",))
+    count = {g: math.prod(axis_length(a, sizes) for a in g) for g in groups}
+    me = {}
+    for g in groups:
+        index = 0
+        for axis in g:
+            index = index * axis_length(axis, sizes) + member_index(axis, sizes)
+        me[g] = index
+    barrier = pltpu.get_barrier_semaphore()
+    for g in groups:
+        for s in range(1, count[g]):
+            peer = member_coords(lax.rem(me[g] + s, count[g]), g, sizes)
+            pl.semaphore_signal(barrier, inc=1, device_id=peer, device_id_type=pl.DeviceIdType.MESH)
+    pl.semaphore_wait(barrier, sum(count[g] - 1 for g in groups))
+
+    def phase(k, source, target, g, gather):
+        send_sem, recv_sem, local_sem = sems[3 * k : 3 * k + 3]
+        n, mine = count[g], me[g]
+        copies = []
+        for s in range(1, n):
+            dst = lax.rem(mine + s, n)
+            copy = pltpu.make_async_remote_copy(
+                src_ref=source if gather else source.at[dst],
+                dst_ref=target.at[mine],
+                send_sem=send_sem.at[s - 1],
+                recv_sem=recv_sem.at[s - 1],
+                device_id=member_coords(dst, g, sizes),
+                device_id_type=pl.DeviceIdType.MESH,
+            )
+            copy.start()
+            copies.append(copy)
+        local = pltpu.make_async_copy(source if gather else source.at[mine], target.at[mine], local_sem)
+        local.start()
+        for copy in copies:
+            copy.wait_send()
+            copy.wait_recv()
+        local.wait()
+
+    def summed(ref):
+        total = ref[0]
+        for j in range(1, ref.shape[0]):
+            total = total + ref[j]
+        return total
+
+    group, along_y, along_z = groups
+    ny, nz = count[along_y], count[along_z]
+    phase(0, p_ref, recv1, group, False)
+    total = summed(recv1)
+    for j in range(ny):
+        send_y[j] = total[j * nz : (j + 1) * nz]
+    phase(1, send_y, recv_y, along_y, False)
+    part = summed(recv_y)
+    for j in range(nz):
+        send_z[j] = part[j : j + 1]
+    phase(2, send_z, recv_z, along_z, False)
+    piece[...] = summed(recv_z)
+    phase(3, piece, recv_z2, along_z, True)
+    for j in range(nz):
+        zrows[j : j + 1] = recv_z2[j]
+    phase(4, zrows, recv_y2, along_y, True)
+    for j in range(ny):
+        chunk[j * nz : (j + 1) * nz] = recv_y2[j]
+    phase(5, chunk, o_ref, group, True)
+
+
 def all_sum_small(value, sizes):
     shape = value.shape
-    rows, group = shape[0], sizes["row"] * sizes["col"]
-    flat = value.reshape(rows, -1)
-    part = exchange(flat.reshape(group, rows // group, -1), ("row", "col"), sizes, 0).sum(0)
-    piece = part.reshape(sizes["dp"], -1, 64)
-    piece = exchange(piece, ("dp",), sizes, 1).sum(0)
-    part = exchange(piece, ("dp",), sizes, 2, gather=True).reshape(part.shape)
-    flat = exchange(part, ("row", "col"), sizes, 3, gather=True).reshape(flat.shape)
-    return flat.reshape(shape)
+    n_group = sizes["row"] * sizes["col"]
+    ny = split_of(sizes)
+    nz = sizes["dp"] // ny
+    width = value.size // (n_group * ny * nz)
+    parts = value.reshape(n_group, ny * nz, width)
+    vmem = pl.BlockSpec(memory_space=pltpu.VMEM)
+    f32 = jnp.float32
+    sems = []
+    for n in (n_group, ny, nz, nz, ny, n_group):
+        sems += [pltpu.SemaphoreType.DMA((max(n - 1, 1),)), pltpu.SemaphoreType.DMA((max(n - 1, 1),)), pltpu.SemaphoreType.DMA]
+    out = pl.pallas_call(
+        functools.partial(allsum_kernel, sizes=sizes),
+        out_shape=jax.ShapeDtypeStruct(parts.shape, parts.dtype),
+        in_specs=[vmem],
+        out_specs=vmem,
+        scratch_shapes=[
+            pltpu.VMEM((n_group, ny * nz, width), f32),
+            pltpu.VMEM((ny, nz, width), f32),
+            pltpu.VMEM((ny, nz, width), f32),
+            pltpu.VMEM((nz, 1, width), f32),
+            pltpu.VMEM((nz, 1, width), f32),
+            pltpu.VMEM((1, width), f32),
+            pltpu.VMEM((nz, 1, width), f32),
+            pltpu.VMEM((nz, width), f32),
+            pltpu.VMEM((ny, nz, width), f32),
+            pltpu.VMEM((ny * nz, width), f32),
+        ]
+        + sems,
+        compiler_params=pltpu.CompilerParams(collective_id=0, has_side_effects=True),
+    )(parts)
+    return out.reshape(shape)
 
 
 def block_sum(value, sizes):

time: 202 us -> 199 us (0.985)
  Pallas kernels: 109 us -> 104 us
    pallas_call x8 -> x4, Pallas kernels: 99.1 us -> 58 us  [exchange_many(): pl.pallas_call(functools.partial(exchange_kernel, jobs=tuple(jobs), sizes...]
    pallas_call x0 -> x1, Pallas kernels: none -> 36.6 us  [all_sum_small(): pl.pallas_call(functools.partial(allsum_kernel, sizes=sizes), out_shape=j...]
    reshape x2 -> x3, local copies, waits for them, and re-layouts: 0.16 us -> 2.93 us  [the longest x2 1.65 us: all_sum_small(): return out.reshape(shape)]
    unnamed x27 -> x26, local copies, waits for them, and re-layouts: 6.3 us -> 6.23 us
where the time goes in v5:
time: 199 us
  Pallas kernels  104 us (52%)
  local copies, waits for them, and re-layouts  42.3 us (21%)
  other arithmetic  31.3 us (16%)
  matrix products  19.5 us (10%)
    pallas_call x4, Pallas kernels, exchange_many(): pl.pallas_call(functools.partial(exchange_kernel, jobs=tuple(jobs), sizes...  58 us
    pallas_call x1, Pallas kernels, all_sum_small(): pl.pallas_call(functools.partial(allsum_kernel, sizes=sizes), out_shape=j...  36.6 us
    another operation x4, other arithmetic, on_device(): lower = jnp.linalg.cholesky(gram)  11.9 us
    dot_general x8, matrix products, exact_dot(): lax.dot_general(left.astype(jnp.float32), right.astype(jnp.float32), (con...  11.2 us
    another operation x3, other arithmetic, on_device(): lax.linalg.triangular_solve(lower, raw_part.transpose(1, 0, 2), left_side...  9.91 us
    pallas_call x1, Pallas kernels, padded_pair(): pl.pallas_call(functools.partial(halo_kernel, sizes=sizes), out_shape=tup...  9.8 us
    dot_general x9, matrix products, on_device(): lax.dot_general(window, conv_weight[a + 1, b + 1], (((1,), (1,)), ((), ()...  6.63 us
    unnamed x26, local copies, waits for them, and re-layouts  6.23 us

profile of v5, /device:TPU:1, one launch (start us, length us, event | category | flops | bytes accessed | tf_op | source)
XLA Modules:
  0.0 198.8 jit_solution(12417569137739948693)
XLA Ops:
  2.1 1.5 copy.113
  6.2 9.8 %shard_map.68 = (bf16[2,2,16,640]{3,2,1,0:T(8,128)(2,1)}, bf16[2,2,16,640]{3,2,1,0:T(8,128)(2,1)}, bf16[4,2,640]{2,1,0:T(2,128)(2,1)}) custom-call(bf16[2,2,16,640]{3,2,1,0:T(8,128)(2,1)} %copy.116.refs_0_, bf16[2,2,16,640]{3,2,1,0:T(8,128)(2,1)} %copy.117.refs_1_, bf16[4,2,640]{2,1,0:T(2,128)(2,1)} %pad_maximum_fusion.5.refs_2_), custom_call_target="tpu_custom_call" | custom-call | tf_op jit(solution)/shard_map/pallas_call | solution.py:156
  18.9 2.5 %pad_maximum_fusion = bf16[2,18,18,640]{3,0,2,1:T(2,128)(2,1)S(1)} fusion(bf16[2,1,18,640]{3,0,2,1:T(2,128)(2,1)S(1)} %get-tuple-element.85, bf16[2,16,1,640]{3,0,2,1:T(2,128)(2,1)S(1)} %get-tuple-element.79, bf16[1,16,16,640]{3,0,2,1:T(2,128)(2,1)S(1)} %copy.114, bf16[1,16,16,640]{3,0,2,1:T(2,128)(2,1)S(1)} %copy.113, ...), kind=kLoop, calls=%fused_computation.27 | loop fusion | flops 4976640 | bytes 1658880 | tf_op jit(solution)/shard_map/concatenate | solution.py:180
  21.4 5.3 %slice_reduce_fusion = (bf16[18,18,640]{2,1,0:T(8,128)(2,1)}, bf16[18,18,640]{2,1,0:T(8,128)(2,1)S(1)}, bf16[1,18,18,640]{3,0,2,1:T(2,128)(2,1)}, bf16[1,18,18,640]{3,0,2,1:T(2,128)(2,1)}) fusion(bf16[2,18,18,640]{3,0,2,1:T(2,128)(2,1)S(1)} %pad_maximum_fusion), kind=kLoop, calls=%fused_computation.129 | loop fusion | bytes 2488320 | tf_op jit(solution)/shard_map/slice | solution.py:211
  27.6 2.5 %reshape.263 = f32[9,640,2,64]{1,0,3,2:T(8,128)} reshape(f32[5760,2,64]{0,2,1:T(8,128)S(1)} %copy-done.1) | data formatting | bytes 5898240 | tf_op jit(solution)/shard_map/reshape | solution.py:223
  30.1 2.9 %fusion.54 = (f32[1,640,9,64]{1,2,3,0:T(8,128)S(1)}, f32[1,640,9,64]{1,2,3,0:T(8,128)S(1)}) fusion(f32[2,640,9,64]{1,2,3,0:T(8,128)} %bitcast.254), kind=kLoop, calls=%fused_computation.131 | loop fusion | bytes 5898240 | tf_op jit(solution)/shard_map/slice | solution.py:225
  33.1 2.0 %fusion = f32[16,16,9,64]{3,1,2,0:T(8,128)S(1)} fusion(f32[1,640,9,64]{1,2,3,0:T(8,128)S(1)} %get-tuple-element.27, bf16[1,16,16,640]{3,2,1,0:T(8,128)(2,1)S(1)} %copy-done.5), kind=kOutput, calls=%fused_computation.5 | convolution fusion | flops 1133445120 | bytes 2392064 | tf_op jit(solution)/shard_map/dot_general | solution.py:189
  36.1 1.6 reshape.264
  40.9 1.8 fusion.16
  42.7 1.6 convolution_add_fusion.7
  47.9 2.9 %fusion.2 = f32[18,18,9,64]{3,1,2,0:T(8,128)S(1)} fusion(f32[1,640,9,64]{1,2,3,0:T(8,128)S(1)} %get-tuple-element.26, bf16[1,18,18,640]{3,0,2,1:T(2,128)(2,1)S(1)} %copy-done.2), kind=kOutput, calls=%fused_computation.7 | convolution fusion | flops 1433272320 | bytes 2635776 | tf_op jit(solution)/shard_map/dot_general | solution.py:189
  52.8 36.6 %shard_map.69 = f32[8,32,320]{2,1,0:T(8,128)} custom-call(f32[8,32,320]{2,1,0:T(8,128)} %reshape.265.p_ref), custom_call_target="tpu_custom_call" | custom-call | tf_op jit(solution)/shard_map/pallas_call | solution.py:355
  91.6 11.7 %custom-call.9 = f32[2,64,64]{2,1,0:T(8,128)S(1)} custom-call(f32[2,64,64]{2,1,0:T(8,128)S(1)} %fusion.43), custom_call_target="Cholesky" | custom-call | tf_op jit(solution)/shard_map/jit(cholesky)/cholesky | solution.py:263
  103.6 9.8 %custom-call.10 = f32[2,1,64,64]{2,3,1,0:T(8,128)S(1)} custom-call(f32[2,1,64,64]{3,2,1,0:T(8,128)S(1)} %select_bitcast_fusion), custom_call_target="InvertDiagBlocksLowerTriangular" | custom-call | tf_op jit(solution)/shard_map/triangular_solve | solution.py:266
  115.7 2.0 %convolution_bitcast_fusion = f32[1,640,9,64]{1,3,2,0:T(8,128)} fusion(bf16[256,640,1]{1,0,2:T(8,128)(2,1)S(1)} %bitcast.274, f32[9,64,256]{2,1,0:T(8,128)S(1)} %bitcast.264), kind=kOutput, calls=%fused_computation.11 | convolution fusion | flops 1132462080 | bytes 2392064 | tf_op jit(solution)/shard_map/dot_general | solution.py:189
  118.6 1.9 concatenate.26
  122.3 1.6 maximum_bitcast_fusion
  123.9 5.6 %copy.144 = f32[9,640,2,64]{3,2,1,0:T(2,128)} copy(f32[9,640,2,64]{1,3,0,2:T(8,128)S(1)} %maximum_bitcast_fusion) | data formatting | bytes 5898240 | tf_op jit(solution)/shard_map/transpose | solution.py:257
  129.4 5.4 %reshape_reshape.3 = f32[32,180,128]{2,1,0:T(8,128)S(1)} reshape(f32[9,640,2,64]{3,2,1,0:T(2,128)} %copy.144) | data formatting | bytes 5898240 | tf_op jit(solution)/shard_map/reshape;reshape | solution.py:385
  136.7 21.6 %shard_map.70 = (f32[2,4,16,24,128]{4,3,2,1,0:T(8,128)S(1)}, f32[4,2,16,24,128]{4,3,2,1,0:T(8,128)S(1)}) custom-call(f32[2,4,16,24,128]{4,3,2,1,0:T(8,128)S(1)} %bitcast.250, f32[4,2,16,24,128]{4,3,2,1,0:T(8,128)} %bitcast.257), custom_call_target="tpu_custom_call" | custom-call | tf_op jit(solution)/shard_map/pallas_call | solution.py:102
  159.6 1.5 reduce_sum.46.refs_1_
  161.1 13.5 %shard_map.71 = (f32[4,16,24,128]{3,2,1,0:T(8,128)S(1)}, f32[2,16,24,128]{3,2,1,0:T(8,128)S(1)}) custom-call(f32[4,16,24,128]{3,2,1,0:T(8,128)S(1)} %reduce_sum.45.refs_0_, f32[2,16,24,128]{3,2,1,0:T(8,128)S(1)} %reduce_sum.46.refs_1_), custom_call_target="tpu_custom_call" | custom-call | tf_op jit(solution)/shard_map/pallas_call | solution.py:102
  174.8 13.6 %shard_map.72 = f32[32,24,128]{2,1,0:T(8,128)S(1)} custom-call(f32[32,24,128]{2,1,0:T(8,128)S(1)} %pad_maximum_fusion.1.refs_0_), custom_call_target="tpu_custom_call" | custom-call | tf_op jit(solution)/shard_map/pallas_call | solution.py:102
  188.4 9.3 %shard_map.73 = f32[8,24,128]{2,1,0:T(8,128)S(1)} custom-call(f32[24,128]{1,0:T(8,128)S(1)} %reduce_sum.49.refs_0_), custom_call_target="tpu_custom_call" | custom-call | tf_op jit(solution)/shard_map/pallas_call | solution.py:102
  (100 shorter events, 28.9 us)
Async XLA Ops:
  21.4 6.2 %copy-start.1 = (f32[5760,2,64]{0,2,1:T(8,128)S(1)}, f32[5760,2,64]{0,2,1:T(8,128)}, u32[]{:S(2)}) copy-start(f32[5760,2,64]{0,2,1:T(8,128)} %param.9) | copy-start | bytes 8847364
  30.1 2.9 %copy-start.5 = (bf16[1,16,16,640]{3,2,1,0:T(8,128)(2,1)S(1)}, bf16[1,16,16,640]{3,2,1,0:T(8,128)(2,1)}, u32[]{:S(2)}) copy-start(bf16[1,16,16,640]{3,2,1,0:T(8,128)(2,1)} %param.6) | copy-start | bytes 983044
  35.1 2.6 %copy-start.4 = (bf16[324,640]{1,0:T(8,128)(2,1)S(1)}, bf16[324,640]{1,0:T(8,128)(2,1)}, u32[]{:S(2)}) copy-start(bf16[324,640]{1,0:T(8,128)(2,1)} %reshape_squeeze.6) | copy-start | bytes 1244164
  37.7 6.6 %slice-start = ((s8[7372800]{0:T(1024)(128)(4,1)}), s8[4194304]{0:T(1024)(128)(4,1)S(1)}, s32[]{:S(2)}) async-start(s8[7372800]{0:T(1024)(128)(4,1)} %bitcast.255), calls=%async_computation | async-start | bytes 8388608
  40.6 3.7 %slice-start.1 = ((s8[7372800]{0:T(1024)(128)(4,1)}), s8[3178496]{0:T(1024)(128)(4,1)S(1)}, s32[]{:S(2)}) async-start(s8[7372800]{0:T(1024)(128)(4,1)} %bitcast.255), calls=%async_computation.1 | async-start | bytes 6356992
  46.7 1.1 copy-start.2
  51.5 62.8 %copy-start.6 = (bf16[1,16,16,640]{3,2,1,0:T(8,128)(2,1)S(1)}, bf16[1,16,16,640]{3,2,1,0:T(8,128)(2,1)}, u32[]{:S(2)}) copy-start(bf16[1,16,16,640]{3,2,1,0:T(8,128)(2,1)} %param.6) | copy-start | bytes 983044
  113.5 1.1 copy-start.7
  115.2 2.5 %copy-start.3 = (bf16[18,18,640]{2,1,0:T(8,128)(2,1)S(1)}, bf16[18,18,640]{2,1,0:T(8,128)(2,1)}, u32[]{:S(2)}) copy-start(bf16[18,18,640]{2,1,0:T(8,128)(2,1)} %get-tuple-element.24) | copy-start | bytes 1244164
  158.2 1.2 copy-start
  161.1 36.7 %copy-start.8 = (f32[2,1,64,64]{2,3,1,0:T(8,128)S(1)}, f32[2,1,64,64]{2,3,1,0:T(8,128)}, u32[]{:S(2)}) copy-start(f32[2,1,64,64]{2,3,1,0:T(8,128)} %copy-done.7) | copy-start | bytes 98308

commit v6 on v5

--- a/solution.py
+++ b/solution.py
@@ -375,6 +375,58 @@
     return out.reshape(shape)
 
 
+def tail_kernel(first_ref, second_ref, o_ref, send, recv, piece, *sems, sizes):
+    ring, group = ("dp",), ("row", "col")
+    n_ring, n_group = sizes["dp"], sizes["row"] * sizes["col"]
+    me_ring = lax.axis_index("dp")
+    me_group = lax.axis_index("row") * sizes["col"] + lax.axis_index("col")
+    barrier = pltpu.get_barrier_semaphore()
+    for g, n, mine in ((ring, n_ring, me_ring), (group, n_group, me_group)):
+        for s in range(1, n):
+            peer = member_coords(lax.rem(mine + s, n), g, sizes)
+            pl.semaphore_signal(barrier, inc=1, device_id=peer, device_id_type=pl.DeviceIdType.MESH)
+    pl.semaphore_wait(barrier, n_ring - 1 + n_group - 1)
+
+    def phase(k, source, target, g, n, mine, gather):
+        send_sem, recv_sem, local_sem = sems[3 * k : 3 * k + 3]
+        copies = []
+        for s in range(1, n):
+            dst = lax.rem(mine + s, n)
+            copy = pltpu.make_async_remote_copy(
+                src_ref=source if gather else source.at[dst],
+                dst_ref=target.at[mine],
+                send_sem=send_sem.at[s - 1],
+                recv_sem=recv_sem.at[s - 1],
+                device_id=member_coords(dst, g, sizes),
+                device_id_type=pl.DeviceIdType.MESH,
+            )
+            copy.start()
+            copies.append(copy)
+        local = pltpu.make_async_copy(source if gather else source.at[mine], target.at[mine], local_sem)
+        local.start()
+        for copy in copies:
+            copy.wait_send()
+            copy.wait_recv()
+        local.wait()
+
+    half = first_ref.shape[1]
+    for b in range(half):
+        total = first_ref[0, b]
+        for j in range(1, first_ref.shape[0]):
+            total = total + first_ref[j, b]
+        send[b] = total
+        total = second_ref[0, b]
+        for j in range(1, second_ref.shape[0]):
+            total = total + second_ref[j, b]
+        send[half + b] = total
+    phase(0, send, recv, ring, n_ring, me_ring, False)
+    total = recv[0]
+    for j in range(1, n_ring):
+        total = total + recv[j]
+    piece[...] = total
+    phase(1, piece, o_ref, group, n_group, me_group, True)
+
+
 def block_sum(value, sizes):
     shape = value.shape
     blocks, rows_n, cols_n = sizes["dp"], sizes["row"], sizes["col"]
@@ -391,9 +443,23 @@
     first, second = exchange_many(
         [(first.sum(0), ("col",), False), (second.sum(0), ("row",), False)], sizes, 5
     )
-    pieces = jnp.concatenate([first.sum(0), second.sum(0)])
-    piece = exchange(pieces, ("dp",), sizes, 6).sum(0)
-    block = exchange(piece, ("row", "col"), sizes, 7, gather=True)
+    vmem = pl.BlockSpec(memory_space=pltpu.VMEM)
+    sems = []
+    for n in (blocks, group):
+        sems += [pltpu.SemaphoreType.DMA((n - 1,)), pltpu.SemaphoreType.DMA((n - 1,)), pltpu.SemaphoreType.DMA]
+    block = pl.pallas_call(
+        functools.partial(tail_kernel, sizes=sizes),
+        out_shape=jax.ShapeDtypeStruct((group, piece_rows, lanes), value.dtype),
+        in_specs=[vmem, vmem],
+        out_specs=vmem,
+        scratch_shapes=[
+            pltpu.VMEM((blocks, piece_rows, lanes), jnp.float32),
+            pltpu.VMEM((blocks, piece_rows, lanes), jnp.float32),
+            pltpu.VMEM((piece_rows, lanes), jnp.float32),
+        ]
+        + sems,
+        compiler_params=pltpu.CompilerParams(collective_id=6, has_side_effects=True),
+    )(first, second)
     return block.reshape(group * piece_rows, lanes)[:block_rows].reshape((block_rows,) + shape[1:])
 
 

time: 199 us -> 202 us (1.015)
  local copies, waits for them, and re-layouts: 42.3 us -> 44.9 us
    pallas_call x0 -> x1, Pallas kernels: none -> 22.9 us  [block_sum(): pl.pallas_call(functools.partial(tail_kernel, sizes=sizes), out_shape=jax...]
    pallas_call x4 -> x2, Pallas kernels: 58 us -> 35.1 us  [exchange_many(): pl.pallas_call(functools.partial(exchange_kernel, jobs=tuple(jobs), sizes...]
    unnamed x26 -> x30, local copies, waits for them, and re-layouts: 6.23 us -> 7.88 us
where the time goes in v6:
time: 202 us; the launch traced here: 201 us
  Pallas kernels  104 us (51%)
  local copies, waits for them, and re-layouts  44.9 us (22%)
  other arithmetic  31.2 us (15%)
  matrix products  19.4 us (10%)
    pallas_call x1, Pallas kernels, all_sum_small(): pl.pallas_call(functools.partial(allsum_kernel, sizes=sizes), out_shape=j...  36.6 us
    pallas_call x2, Pallas kernels, exchange_many(): pl.pallas_call(functools.partial(exchange_kernel, jobs=tuple(jobs), sizes...  35.1 us
    pallas_call x1, Pallas kernels, block_sum(): pl.pallas_call(functools.partial(tail_kernel, sizes=sizes), out_shape=jax...  22.9 us
    another operation x4, other arithmetic, on_device(): lower = jnp.linalg.cholesky(gram)  11.9 us
    dot_general x8, matrix products, exact_dot(): lax.dot_general(left.astype(jnp.float32), right.astype(jnp.float32), (con...  11.2 us
    another operation x3, other arithmetic, on_device(): lax.linalg.triangular_solve(lower, raw_part.transpose(1, 0, 2), left_side...  9.91 us
    pallas_call x1, Pallas kernels, padded_pair(): pl.pallas_call(functools.partial(halo_kernel, sizes=sizes), out_shape=tup...  9.82 us
    unnamed x30, local copies, waits for them, and re-layouts  7.88 us

profile of v6, /device:TPU:1, one launch (start us, length us, event | category | flops | bytes accessed | tf_op | source)
XLA Modules:
  0.0 201.3 jit_solution(14422983072102517811)
XLA Ops:
  0.6 1.5 copy.114
  2.1 1.5 copy.113
  6.2 9.8 %shard_map.68 = (bf16[2,2,16,640]{3,2,1,0:T(8,128)(2,1)}, bf16[2,2,16,640]{3,2,1,0:T(8,128)(2,1)}, bf16[4,2,640]{2,1,0:T(2,128)(2,1)}) custom-call(bf16[2,2,16,640]{3,2,1,0:T(8,128)(2,1)} %copy.116.refs_0_, bf16[2,2,16,640]{3,2,1,0:T(8,128)(2,1)} %copy.117.refs_1_, bf16[4,2,640]{2,1,0:T(2,128)(2,1)} %pad_maximum_fusion.4.refs_2_), custom_call_target="tpu_custom_call" | custom-call | tf_op jit(solution)/shard_map/pallas_call | solution.py:156
  18.9 2.5 %pad_maximum_fusion = bf16[2,18,18,640]{3,0,2,1:T(2,128)(2,1)S(1)} fusion(bf16[2,1,18,640]{3,0,2,1:T(2,128)(2,1)S(1)} %get-tuple-element.85, bf16[2,16,1,640]{3,0,2,1:T(2,128)(2,1)S(1)} %get-tuple-element.79, bf16[1,16,16,640]{3,0,2,1:T(2,128)(2,1)S(1)} %copy.114, bf16[1,16,16,640]{3,0,2,1:T(2,128)(2,1)S(1)} %copy.113, ...), kind=kLoop, calls=%fused_computation.27 | loop fusion | flops 4976640 | bytes 1658880 | tf_op jit(solution)/shard_map/concatenate | solution.py:180
  21.4 5.3 %slice_reduce_fusion = (bf16[18,18,640]{2,1,0:T(8,128)(2,1)}, bf16[18,18,640]{2,1,0:T(8,128)(2,1)S(1)}, bf16[1,18,18,640]{3,0,2,1:T(2,128)(2,1)}, bf16[1,18,18,640]{3,0,2,1:T(2,128)(2,1)}) fusion(bf16[2,18,18,640]{3,0,2,1:T(2,128)(2,1)S(1)} %pad_maximum_fusion), kind=kLoop, calls=%fused_computation.128 | loop fusion | bytes 2488320 | tf_op jit(solution)/shard_map/slice | solution.py:211
  27.6 2.6 %reshape.263 = f32[9,640,2,64]{1,0,3,2:T(8,128)} reshape(f32[5760,2,64]{0,2,1:T(8,128)S(1)} %copy-done.3) | data formatting | bytes 5898240 | tf_op jit(solution)/shard_map/reshape | solution.py:223
  30.2 2.9 %fusion.54 = (f32[1,640,9,64]{1,2,3,0:T(8,128)S(1)}, f32[1,640,9,64]{1,2,3,0:T(8,128)S(1)}) fusion(f32[2,640,9,64]{1,2,3,0:T(8,128)} %bitcast.253), kind=kLoop, calls=%fused_computation.130 | loop fusion | bytes 5898240 | tf_op jit(solution)/shard_map/slice | solution.py:225
  33.1 2.0 %fusion = f32[16,16,9,64]{3,1,2,0:T(8,128)S(1)} fusion(f32[1,640,9,64]{1,2,3,0:T(8,128)S(1)} %get-tuple-element.27, bf16[1,16,16,640]{3,2,1,0:T(8,128)(2,1)S(1)} %copy-done.7), kind=kOutput, calls=%fused_computation.5 | convolution fusion | flops 1133445120 | bytes 2392064 | tf_op jit(solution)/shard_map/dot_general | solution.py:189
  36.1 1.6 reshape.264
  41.0 1.8 fusion.16
  42.7 1.6 convolution_add_fusion.7
  47.9 2.9 %fusion.2 = f32[18,18,9,64]{3,1,2,0:T(8,128)S(1)} fusion(f32[1,640,9,64]{1,2,3,0:T(8,128)S(1)} %get-tuple-element.26, bf16[1,18,18,640]{3,0,2,1:T(2,128)(2,1)S(1)} %copy-done.4), kind=kOutput, calls=%fused_computation.7 | convolution fusion | flops 1433272320 | bytes 2635776 | tf_op jit(solution)/shard_map/dot_general | solution.py:189
  52.9 36.6 %shard_map.69 = f32[8,32,320]{2,1,0:T(8,128)} custom-call(f32[8,32,320]{2,1,0:T(8,128)} %reshape.265.p_ref), custom_call_target="tpu_custom_call" | custom-call | tf_op jit(solution)/shard_map/pallas_call | solution.py:355
  91.7 11.7 %custom-call.9 = f32[2,64,64]{2,1,0:T(8,128)S(1)} custom-call(f32[2,64,64]{2,1,0:T(8,128)S(1)} %fusion.43), custom_call_target="Cholesky" | custom-call | tf_op jit(solution)/shard_map/jit(cholesky)/cholesky | solution.py:263
  103.7 9.8 %custom-call.10 = f32[2,1,64,64]{2,3,1,0:T(8,128)S(1)} custom-call(f32[2,1,64,64]{3,2,1,0:T(8,128)S(1)} %select_bitcast_fusion), custom_call_target="InvertDiagBlocksLowerTriangular" | custom-call | tf_op jit(solution)/shard_map/triangular_solve | solution.py:266
  115.8 2.0 convolution_bitcast_fusion
  118.7 1.9 concatenate.23
  122.3 1.6 maximum_bitcast_fusion
  123.9 5.6 %copy.144 = f32[9,640,2,64]{3,2,1,0:T(2,128)} copy(f32[9,640,2,64]{1,3,0,2:T(8,128)S(1)} %maximum_bitcast_fusion) | data formatting | bytes 5898240 | tf_op jit(solution)/shard_map/transpose | solution.py:257
  129.5 5.4 %reshape_reshape.3 = f32[32,180,128]{2,1,0:T(8,128)S(1)} reshape(f32[9,640,2,64]{3,2,1,0:T(2,128)} %copy.144) | data formatting | bytes 5898240 | tf_op jit(solution)/shard_map/reshape;reshape | solution.py:437
  136.7 21.6 %shard_map.70 = (f32[2,4,16,24,128]{4,3,2,1,0:T(8,128)S(1)}, f32[4,2,16,24,128]{4,3,2,1,0:T(8,128)S(1)}) custom-call(f32[2,4,16,24,128]{4,3,2,1,0:T(8,128)S(1)} %bitcast.250, f32[4,2,16,24,128]{4,3,2,1,0:T(8,128)} %bitcast.256), custom_call_target="tpu_custom_call" | custom-call | tf_op jit(solution)/shard_map/pallas_call | solution.py:102
  159.6 1.5 reduce_sum.19.refs_1_
  161.2 13.5 %shard_map.71 = (f32[4,16,24,128]{3,2,1,0:T(8,128)S(1)}, f32[2,16,24,128]{3,2,1,0:T(8,128)S(1)}) custom-call(f32[4,16,24,128]{3,2,1,0:T(8,128)S(1)} %reduce_sum.18.refs_0_, f32[2,16,24,128]{3,2,1,0:T(8,128)S(1)} %reduce_sum.19.refs_1_), custom_call_target="tpu_custom_call" | custom-call | tf_op jit(solution)/shard_map/pallas_call | solution.py:102
  176.4 22.9 %shard_map.72 = f32[8,24,128]{2,1,0:T(8,128)} custom-call(f32[4,16,24,128]{3,2,1,0:T(8,128)} %copy-done.1, f32[2,16,24,128]{3,2,1,0:T(8,128)} %copy-done.2), custom_call_target="tpu_custom_call" | custom-call | tf_op jit(solution)/shard_map/pallas_call | solution.py:450
  (99 shorter events, 29.9 us)
Async XLA Ops:
  21.4 6.2 %copy-start.3 = (f32[5760,2,64]{0,2,1:T(8,128)S(1)}, f32[5760,2,64]{0,2,1:T(8,128)}, u32[]{:S(2)}) copy-start(f32[5760,2,64]{0,2,1:T(8,128)} %param.9) | copy-start | bytes 8847364
  30.2 2.9 %copy-start.7 = (bf16[1,16,16,640]{3,2,1,0:T(8,128)(2,1)S(1)}, bf16[1,16,16,640]{3,2,1,0:T(8,128)(2,1)}, u32[]{:S(2)}) copy-start(bf16[1,16,16,640]{3,2,1,0:T(8,128)(2,1)} %param.6) | copy-start | bytes 983044
  35.2 2.6 %copy-start.6 = (bf16[324,640]{1,0:T(8,128)(2,1)S(1)}, bf16[324,640]{1,0:T(8,128)(2,1)}, u32[]{:S(2)}) copy-start(bf16[324,640]{1,0:T(8,128)(2,1)} %reshape_squeeze.6) | copy-start | bytes 1244164
  37.7 6.6 %slice-start = ((s8[7372800]{0:T(1024)(128)(4,1)}), s8[4194304]{0:T(1024)(128)(4,1)S(1)}, s32[]{:S(2)}) async-start(s8[7372800]{0:T(1024)(128)(4,1)} %bitcast.254), calls=%async_computation | async-start | bytes 8388608
  40.7 3.7 %slice-start.1 = ((s8[7372800]{0:T(1024)(128)(4,1)}), s8[3178496]{0:T(1024)(128)(4,1)S(1)}, s32[]{:S(2)}) async-start(s8[7372800]{0:T(1024)(128)(4,1)} %bitcast.254), calls=%async_computation.1 | async-start | bytes 6356992
  46.8 1.1 copy-start.4
  51.6 62.8 %copy-start.8 = (bf16[1,16,16,640]{3,2,1,0:T(8,128)(2,1)S(1)}, bf16[1,16,16,640]{3,2,1,0:T(8,128)(2,1)}, u32[]{:S(2)}) copy-start(bf16[1,16,16,640]{3,2,1,0:T(8,128)(2,1)} %param.6) | copy-start | bytes 983044
  113.5 1.1 copy-start.9
  115.3 2.5 %copy-start.5 = (bf16[18,18,640]{2,1,0:T(8,128)(2,1)S(1)}, bf16[18,18,640]{2,1,0:T(8,128)(2,1)}, u32[]{:S(2)}) copy-start(bf16[18,18,640]{2,1,0:T(8,128)(2,1)} %get-tuple-element.24) | copy-start | bytes 1244164
  158.3 1.2 copy-start
  159.6 40.7 %copy-start.10 = (f32[2,1,64,64]{2,3,1,0:T(8,128)S(1)}, f32[2,1,64,64]{2,3,1,0:T(8,128)}, u32[]{:S(2)}) copy-start(f32[2,1,64,64]{2,3,1,0:T(8,128)} %copy-done.9) | copy-start | bytes 98308
  174.7 0.9 copy-start.1
  175.6 0.8 copy-start.2

commit v7 on v4

--- a/solution.py
+++ b/solution.py
@@ -326,6 +326,16 @@
     return out.reshape(shape)
 
 
+def permute_sum(value, axis, sizes):
+    n = sizes[axis]
+    me = lax.axis_index(axis)
+    total = lax.dynamic_index_in_dim(value, me, 0, keepdims=False)
+    for shift in range(1, n):
+        slab = lax.dynamic_index_in_dim(value, lax.rem(me + shift, n), 0, keepdims=False)
+        total = total + lax.ppermute(slab, axis, [(i, (i + shift) % n) for i in range(n)])
+    return total
+
+
 def block_sum(value, sizes):
     shape = value.shape
     blocks, rows_n, cols_n = sizes["dp"], sizes["row"], sizes["col"]
@@ -338,10 +348,8 @@
     half = blocks // 2
     first = pieces[:half].transpose(1, 2, 0, 3, 4)
     second = pieces[half:].transpose(2, 1, 0, 3, 4)
-    first, second = exchange_many([(first, ("row",), False), (second, ("col",), False)], sizes, 4)
-    first, second = exchange_many(
-        [(first.sum(0), ("col",), False), (second.sum(0), ("row",), False)], sizes, 5
-    )
+    first, second = permute_sum(first, "row", sizes), permute_sum(second, "col", sizes)
+    first, second = exchange_many([(first, ("col",), False), (second, ("row",), False)], sizes, 5)
     pieces = jnp.concatenate([first.sum(0), second.sum(0)])
     piece = exchange(pieces, ("dp",), sizes, 6).sum(0)
     block = exchange(piece, ("row", "col"), sizes, 7, gather=True)

time: 199 us -> 185 us (0.930)
  Pallas kernels: 103 us -> 81.8 us
  local copies, waits for them, and re-layouts: 42.3 us -> 50.8 us
  matrix products: 19.5 us -> 14.8 us
  starting transfers between devices: 0 us -> 3.58 us
    pallas_call x4 -> x3, Pallas kernels: 58.5 us -> 36.8 us  [exchange_many(): pl.pallas_call(functools.partial(exchange_kernel, jobs=tuple(jobs), sizes...]
    reshape x9, local copies, waits for them, and re-layouts: 0.15 us -> 4.11 us  [on_device(): jnp.pad(first_image, ((1 + a, 1 - a), (1 + b, 1 - b), (0, 0)))]
    ppermute x0 -> x4, starting transfers between devices: none -> 3.58 us  [permute_sum(): lax.ppermute(slab, axis, [(i, (i + shift) % n) for i in range(n)])]
    dot_general x9, matrix products: 6.63 us -> 4.16 us  [on_device(): lax.dot_general(window, conv_weight[a + 1, b + 1], (((1,), (1,)), ((), ()...]
    add x0 -> x2, other arithmetic: none -> 2.4 us  [permute_sum(): total + lax.ppermute(slab, axis, [(i, (i + shift) % n) for i in range(n)])]
    dot_general x8, matrix products: 11.2 us -> 9.07 us  [exact_dot(): lax.dot_general(left.astype(jnp.float32), right.astype(jnp.float32), (con...]
    unnamed x26 -> x32, local copies, waits for them, and re-layouts: 6.23 us -> 6.21 us
  transfers between devices with their start and end apart: 0 -> 4, of which waited for: 0 -> 0; matrix products, arithmetic and copies ran while one was open for 0% -> 14% of each run, Pallas kernels for 0% -> 0%
where the time goes in v7:
time: 185 us; the launch traced here: 184 us
  Pallas kernels  81.8 us (44%)
  local copies, waits for them, and re-layouts  50.8 us (27%)
  other arithmetic  31.8 us (17%)
  matrix products  14.8 us (8%)
  starting transfers between devices  3.58 us (2%)
    pallas_call x3, Pallas kernels, exchange_many(): pl.pallas_call(functools.partial(exchange_kernel, jobs=tuple(jobs), sizes...  36.8 us
    pallas_call x1, Pallas kernels, all_sum_small(): pl.pallas_call(functools.partial(allsum_kernel, sizes=sizes), out_shape=j...  35.2 us
    another operation x4, other arithmetic, on_device(): lower = jnp.linalg.cholesky(gram)  12.1 us
    another operation x3, other arithmetic, on_device(): lax.linalg.triangular_solve(lower, raw_part.transpose(1, 0, 2), left_side...  9.92 us
    pallas_call x1, Pallas kernels, padded_pair(): pl.pallas_call(functools.partial(halo_kernel, sizes=sizes), out_shape=tup...  9.81 us
    dot_general x8, matrix products, exact_dot(): lax.dot_general(left.astype(jnp.float32), right.astype(jnp.float32), (con...  9.07 us
    unnamed x32, local copies, waits for them, and re-layouts  6.21 us
    transpose x1, local copies, waits for them, and re-layouts, on_device(): rows = rows.transpose(2, 1, 0, 3).reshape(taps * channels, 2, rank)  5.57 us
  transfers between devices with their start and end apart: 4, of which 0 were waited for; matrix products, arithmetic and copies ran while one was open for 14% of the time, Pallas kernels for 0%

profile of v7, /device:TPU:1, one launch (start us, length us, event | category | flops | bytes accessed | tf_op | source)
XLA Modules:
  0.0 184.2 jit_solution(18101525237596685223)
XLA Ops:
  0.6 1.5 copy.122
  2.1 1.5 copy.121
  8.3 9.8 %shard_map.68 = (bf16[2,2,16,640]{3,2,1,0:T(8,128)(2,1)}, bf16[2,2,16,640]{3,2,1,0:T(8,128)(2,1)}, bf16[4,2,640]{2,1,0:T(2,128)(2,1)}) custom-call(bf16[2,2,16,640]{3,2,1,0:T(8,128)(2,1)} %copy.124.refs_0_, bf16[2,2,16,640]{3,2,1,0:T(8,128)(2,1)} %copy.125.refs_1_, bf16[4,2,640]{2,1,0:T(2,128)(2,1)} %pad_maximum_fusion.5.refs_2_), custom_call_target="tpu_custom_call" | custom-call | tf_op jit(solution)/shard_map/pallas_call | solution.py:130
  21.0 2.5 %pad_maximum_fusion = bf16[2,18,18,640]{3,0,2,1:T(2,128)(2,1)S(1)} fusion(bf16[2,1,18,640]{3,0,2,1:T(2,128)(2,1)S(1)} %get-tuple-element.87, bf16[2,16,1,640]{3,0,2,1:T(2,128)(2,1)S(1)} %get-tuple-element.81, bf16[1,16,16,640]{3,0,2,1:T(2,128)(2,1)S(1)} %copy.122, bf16[1,16,16,640]{3,0,2,1:T(2,128)(2,1)S(1)} %copy.121, ...), kind=kLoop, calls=%fused_computation.25 | loop fusion | flops 4976640 | bytes 1658880 | tf_op jit(solution)/shard_map/concatenate | solution.py:154
  23.5 5.5 %slice_reduce_fusion = (bf16[18,18,640]{2,1,0:T(8,128)(2,1)}, bf16[18,18,640]{2,1,0:T(8,128)(2,1)}, bf16[1,18,18,640]{3,0,2,1:T(2,128)(2,1)}, bf16[1,18,18,640]{3,0,2,1:T(2,128)(2,1)}) fusion(bf16[2,18,18,640]{3,0,2,1:T(2,128)(2,1)S(1)} %pad_maximum_fusion), kind=kLoop, calls=%fused_computation.143 | loop fusion | bytes 2488320 | tf_op jit(solution)/shard_map/slice | solution.py:185
  29.0 2.0 %reshape_squeeze.6 = bf16[324,640]{1,0:T(8,128)(2,1)} reshape(bf16[18,18,640]{2,1,0:T(8,128)(2,1)} %get-tuple-element.21) | data formatting | bytes 829440 | tf_op jit(solution)/shard_map/reshape;squeeze | solution.py:195
  31.0 2.6 %reshape.263 = f32[9,640,2,64]{1,0,3,2:T(8,128)} reshape(f32[5760,2,64]{0,2,1:T(8,128)S(1)} %copy-done.1) | data formatting | bytes 5898240 | tf_op jit(solution)/shard_map/reshape | solution.py:197
  33.6 2.9 %fusion.58 = (f32[1,640,9,64]{1,2,3,0:T(8,128)S(1)}, f32[1,640,9,64]{1,2,3,0:T(8,128)S(1)}) fusion(f32[2,640,9,64]{1,2,3,0:T(8,128)} %bitcast.283), kind=kLoop, calls=%fused_computation.145 | loop fusion | bytes 5898240 | tf_op jit(solution)/shard_map/slice | solution.py:199
  36.4 2.0 %fusion = f32[16,16,9,64]{3,1,2,0:T(8,128)S(1)} fusion(f32[1,640,9,64]{1,2,3,0:T(8,128)S(1)} %get-tuple-element.23, bf16[1,16,16,640]{3,2,1,0:T(8,128)(2,1)S(1)} %copy-done.8), kind=kOutput, calls=%fused_computation.3 | convolution fusion | flops 1133445120 | bytes 2392064 | tf_op jit(solution)/shard_map/dot_general | solution.py:163
  41.1 2.9 %fusion.2 = f32[18,18,9,64]{3,1,2,0:T(8,128)S(1)} fusion(f32[1,640,9,64]{1,2,3,0:T(8,128)S(1)} %get-tuple-element.22, bf16[1,18,18,640]{3,0,2,1:T(2,128)(2,1)S(1)} %copy-done.4), kind=kOutput, calls=%fused_computation.5 | convolution fusion | flops 1433272320 | bytes 2635776 | tf_op jit(solution)/shard_map/dot_general | solution.py:163
  50.9 35.2 %shard_map.69 = f32[8,32,320]{2,1,0:T(8,128)} custom-call(f32[8,32,320]{2,1,0:T(8,128)} %reshape.265.p_ref), custom_call_target="tpu_custom_call" | custom-call | tf_op jit(solution)/shard_map/pallas_call | solution.py:309
  86.1 1.4 reshape.266
  95.5 1.6 concatenate.26
  98.4 1.5 convolution_bitcast_fusion.1
  100.0 5.6 %copy.152 = f32[9,640,2,64]{3,2,1,0:T(2,128)} copy(f32[9,640,2,64]{1,3,0,2:T(8,128)S(1)} %maximum_bitcast_fusion) | data formatting | bytes 5898240 | tf_op jit(solution)/shard_map/transpose | solution.py:231
  105.6 5.4 %reshape_reshape.3 = f32[32,180,128]{2,1,0:T(8,128)S(1)} reshape(f32[9,640,2,64]{3,2,1,0:T(2,128)} %copy.152) | data formatting | bytes 5898240 | tf_op jit(solution)/shard_map/reshape;reshape | solution.py:346
  111.1 2.0 %pad_slice_fusion = (f32[16,192,128]{2,1,0:T(8,128)}, f32[16,192,128]{2,1,0:T(8,128)}) fusion(f32[32,180,128]{2,1,0:T(8,128)S(1)} %reshape_reshape.3), kind=kLoop, calls=%fused_computation | loop fusion | bytes 6094848 | tf_op jit(solution)/shard_map/slice | solution.py:350
  113.1 1.6 constant_dynamic-slice_fusion.5
  115.6 1.7 collective-permute-start
  120.1 12.0 %custom-call.9 = f32[2,64,64]{2,1,0:T(8,128)S(1)} custom-call(f32[2,64,64]{2,1,0:T(8,128)S(1)} %fusion.47), custom_call_target="Cholesky" | custom-call | tf_op jit(solution)/shard_map/jit(cholesky)/cholesky | solution.py:237
  132.3 9.8 %custom-call.10 = f32[2,1,64,64]{2,3,1,0:T(8,128)S(1)} custom-call(f32[2,1,64,64]{3,2,1,0:T(8,128)S(1)} %select_bitcast_fusion), custom_call_target="InvertDiagBlocksLowerTriangular" | custom-call | tf_op jit(solution)/shard_map/triangular_solve | solution.py:240
  146.1 13.5 %shard_map.70 = (f32[4,16,24,128]{3,2,1,0:T(8,128)S(1)}, f32[2,16,24,128]{3,2,1,0:T(8,128)S(1)}) custom-call(f32[4,16,24,128]{3,2,1,0:T(8,128)S(1)} %fusion.27.refs_0_, f32[2,16,24,128]{3,2,1,0:T(8,128)S(1)} %fusion.41.refs_1_), custom_call_target="tpu_custom_call" | custom-call | tf_op jit(solution)/shard_map/pallas_call | solution.py:76
  159.8 13.4 %shard_map.71 = f32[32,24,128]{2,1,0:T(8,128)S(1)} custom-call(f32[32,24,128]{2,1,0:T(8,128)S(1)} %pad_maximum_fusion.1.refs_0_), custom_call_target="tpu_custom_call" | custom-call | tf_op jit(solution)/shard_map/pallas_call | solution.py:76
  173.2 9.9 %shard_map.72 = f32[8,24,128]{2,1,0:T(8,128)S(1)} custom-call(f32[24,128]{1,0:T(8,128)S(1)} %reduce_sum.29.refs_0_), custom_call_target="tpu_custom_call" | custom-call | tf_op jit(solution)/shard_map/pallas_call | solution.py:76
  (113 shorter events, 35.1 us)
Async XLA Ops:
  2.1 2.0 %copy-start.8 = (bf16[1,16,16,640]{3,2,1,0:T(8,128)(2,1)S(1)}, bf16[1,16,16,640]{3,2,1,0:T(8,128)(2,1)}, u32[]{:S(2)}) copy-start(bf16[1,16,16,640]{3,2,1,0:T(8,128)(2,1)} %param.6) | copy-start | bytes 983044
  23.5 7.5 %copy-start.1 = (f32[5760,2,64]{0,2,1:T(8,128)S(1)}, f32[5760,2,64]{0,2,1:T(8,128)}, u32[]{:S(2)}) copy-start(f32[5760,2,64]{0,2,1:T(8,128)} %param.9) | copy-start | bytes 8847364
  39.5 1.7 copy-start.4
  39.5 5.2 %slice-start = ((s8[7372800]{0:T(1024)(128)(4,1)}), s8[4194304]{0:T(1024)(128)(4,1)S(1)}, s32[]{:S(2)}) async-start(s8[7372800]{0:T(1024)(128)(4,1)} %bitcast.284), calls=%async_computation | async-start | bytes 8388608
  40.8 3.8 %slice-start.1 = ((s8[7372800]{0:T(1024)(128)(4,1)}), s8[3178496]{0:T(1024)(128)(4,1)S(1)}, s32[]{:S(2)}) async-start(s8[7372800]{0:T(1024)(128)(4,1)} %bitcast.284), calls=%async_computation.1 | async-start | bytes 6356992
  41.1 3.0 %copy-start.6 = (bf16[324,640]{1,0:T(8,128)(2,1)S(1)}, bf16[324,640]{1,0:T(8,128)(2,1)}, u32[]{:S(2)}) copy-start(bf16[324,640]{1,0:T(8,128)(2,1)} %reshape_squeeze.6) | copy-start | bytes 1244164
  41.1 3.0 %copy-start.9 = (f32[324,64]{1,0:T(8,128)S(1)}, f32[324,64]{1,0:T(8,128)}, u32[]{:S(2)}) copy-start(f32[324,64]{1,0:T(8,128)} %reshape.264) | copy-start | bytes 248836
  47.5 1.1 copy-start.3
  87.5 2.9 %copy-start.2 = (f32[640,2,64]{2,1,0:T(2,128)}, f32[640,2,64]{2,1,0:T(2,128)S(1)}, u32[]{:S(2)}) copy-start(f32[640,2,64]{2,1,0:T(2,128)S(1)} %reshape.266) | copy-start | bytes 983044
  88.4 2.3 %copy-start.5 = (bf16[18,18,640]{2,1,0:T(8,128)(2,1)S(1)}, bf16[18,18,640]{2,1,0:T(8,128)(2,1)}, u32[]{:S(2)}) copy-start(bf16[18,18,640]{2,1,0:T(8,128)(2,1)} %get-tuple-element.20) | copy-start | bytes 1244164
  95.4 2.0 %copy-start.7 = (bf16[1,16,16,640]{3,2,1,0:T(8,128)(2,1)S(1)}, bf16[1,16,16,640]{3,2,1,0:T(8,128)(2,1)}, u32[]{:S(2)}) copy-start(bf16[1,16,16,640]{3,2,1,0:T(8,128)(2,1)} %fusion.31) | copy-start | bytes 983044
  113.1 4.3 %copy-start = (f32[16,192,128]{2,1,0:T(8,128)S(1)}, f32[16,192,128]{2,1,0:T(8,128)}, u32[]{:S(2)}) copy-start(f32[16,192,128]{2,1,0:T(8,128)} %get-tuple-element.24) | copy-start | bytes 4718596
  115.6 29.3 %collective-permute-start = (f32[4,16,24,128]{3,2,1,0:T(8,128)}, f32[4,16,24,128]{3,2,1,0:T(8,128)}, u32[]{:S(2)}, u32[]{:S(2)}) collective-permute-start(f32[4,16,24,128]{3,2,1,0:T(8,128)} %bitcast.275), channel_id=1, source_target_pairs={{0,4},{4,0},{1,5},{5,1},{2,6},{6,2},{3,7},{7,3},{8,12},{12,8},{9,1... | collective-permute-start | bytes 2359304 | tf_op jit(solution)/shard_map/ppermute | solution.py:335
  117.6 26.1 %collective-permute-start.3 = (f32[2,16,24,128]{3,2,1,0:T(8,128)S(1)}, f32[2,16,24,128]{3,2,1,0:T(8,128)S(1)}, u32[]{:S(2)}, u32[]{:S(2)}) collective-permute-start(f32[2,16,24,128]{3,2,1,0:T(8,128)S(1)} %bitcast.314), channel_id=1, source_target_pairs={{0,3},{1,0},{2,1},{3,2},{4,7},{5,4},{6,5},{7,6},{8,11},{9,8},{10,9... | collective-permute-start | bytes 1179656 | tf_op jit(solution)/shard_map/ppermute | solution.py:335
  118.1 25.6 %collective-permute-start.2 = (f32[2,16,24,128]{3,2,1,0:T(8,128)S(1)}, f32[2,16,24,128]{3,2,1,0:T(8,128)}, u32[]{:S(2)}, u32[]{:S(2)}) collective-permute-start(f32[2,16,24,128]{3,2,1,0:T(8,128)S(1)} %bitcast.315), channel_id=1, source_target_pairs={{0,2},{1,3},{2,0},{3,1},{4,6},{5,7},{6,4},{7,5},{8,10},{9,11},{10,... | collective-permute-start | bytes 1179656 | tf_op jit(solution)/shard_map/ppermute | solution.py:335
  119.1 24.6 %collective-permute-start.1 = (f32[2,16,24,128]{3,2,1,0:T(8,128)S(1)}, f32[2,16,24,128]{3,2,1,0:T(8,128)}, u32[]{:S(2)}, u32[]{:S(2)}) collective-permute-start(f32[2,16,24,128]{3,2,1,0:T(8,128)S(1)} %bitcast.316), channel_id=1, source_target_pairs={{0,1},{1,2},{2,3},{3,0},{4,5},{5,6},{6,7},{7,4},{8,9},{9,10},{10,1... | collective-permute-start | bytes 1179656 | tf_op jit(solution)/shard_map/ppermute | solution.py:335

commit v8 on v7

--- a/solution.py
+++ b/solution.py
@@ -326,12 +326,12 @@
     return out.reshape(shape)
 
 
-def permute_sum(value, axis, sizes):
+def permute_sum(value, axis, sizes, dim):
     n = sizes[axis]
     me = lax.axis_index(axis)
-    total = lax.dynamic_index_in_dim(value, me, 0, keepdims=False)
+    total = lax.dynamic_index_in_dim(value, me, dim, keepdims=False)
     for shift in range(1, n):
-        slab = lax.dynamic_index_in_dim(value, lax.rem(me + shift, n), 0, keepdims=False)
+        slab = lax.dynamic_index_in_dim(value, lax.rem(me + shift, n), dim, keepdims=False)
         total = total + lax.ppermute(slab, axis, [(i, (i + shift) % n) for i in range(n)])
     return total
 
@@ -346,9 +346,8 @@
     padded = jnp.pad(value.reshape(blocks, block_rows, lanes), ((0, 0), (0, piece_rows * group - block_rows), (0, 0)))
     pieces = padded.reshape(blocks, rows_n, cols_n, piece_rows, lanes)
     half = blocks // 2
-    first = pieces[:half].transpose(1, 2, 0, 3, 4)
-    second = pieces[half:].transpose(2, 1, 0, 3, 4)
-    first, second = permute_sum(first, "row", sizes), permute_sum(second, "col", sizes)
+    first = permute_sum(pieces[:half], "row", sizes, 1).transpose(1, 0, 2, 3)
+    second = permute_sum(pieces[half:], "col", sizes, 2).transpose(1, 0, 2, 3)
     first, second = exchange_many([(first, ("col",), False), (second, ("row",), False)], sizes, 5)
     pieces = jnp.concatenate([first.sum(0), second.sum(0)])
     piece = exchange(pieces, ("dp",), sizes, 6).sum(0)

time: 185 us -> 185 us (level)
    dynamic_slice x0 -> x6, local copies, waits for them, and re-layouts: none -> 2.81 us  [the longest x2 1.8 us: permute_sum(): total = lax.dynamic_index_in_dim(value, me, dim, keepdims=False)]
    add x2 -> x0, other arithmetic: 2.4 us -> none  [permute_sum(): total + lax.ppermute(slab, axis, [(i, (i + shift) % n) for i in range(n)])]
    transpose x0 -> x2, other arithmetic: none -> 2.4 us  [the longest x1 1.21 us: block_sum(): first = permute_sum(pieces[:half], 'row', sizes, 1).transpose(1, 0, 2, 3)]
    unnamed x32 -> x28, local copies, waits for them, and re-layouts: 6.21 us -> 5.2 us
where the time goes in v8:
time: 185 us; the launch traced here: 184 us
  Pallas kernels  81.8 us (44%)
  local copies, waits for them, and re-layouts  50.9 us (28%)
  other arithmetic  31.8 us (17%)
  matrix products  14.8 us (8%)
  starting transfers between devices  3.58 us (2%)
    pallas_call x3, Pallas kernels, exchange_many(): pl.pallas_call(functools.partial(exchange_kernel, jobs=tuple(jobs), sizes...  36.8 us
    pallas_call x1, Pallas kernels, all_sum_small(): pl.pallas_call(functools.partial(allsum_kernel, sizes=sizes), out_shape=j...  35.2 us
    another operation x4, other arithmetic, on_device(): lower = jnp.linalg.cholesky(gram)  12.2 us
    another operation x3, other arithmetic, on_device(): lax.linalg.triangular_solve(lower, raw_part.transpose(1, 0, 2), left_side...  9.92 us
    pallas_call x1, Pallas kernels, padded_pair(): pl.pallas_call(functools.partial(halo_kernel, sizes=sizes), out_shape=tup...  9.81 us
    dot_general x8, matrix products, exact_dot(): lax.dot_general(left.astype(jnp.float32), right.astype(jnp.float32), (con...  9.07 us
    transpose x1, local copies, waits for them, and re-layouts, on_device(): rows = rows.transpose(2, 1, 0, 3).reshape(taps * channels, 2, rank)  5.57 us
    slice x1, local copies, waits for them, and re-layouts, on_device(): grad_pad, input_pad = (both_pad[0], both_pad[1])  5.5 us
  transfers between devices with their start and end apart: 4, of which 0 were waited for; matrix products, arithmetic and copies ran while one was open for 14% of the time, Pallas kernels for 0%

profile of v8, /device:TPU:1, one launch (start us, length us, event | category | flops | bytes accessed | tf_op | source)
XLA Modules:
  0.0 184.2 jit_solution(17126876104008769067)
XLA Ops:
  0.6 1.5 copy.122
  2.1 1.5 copy.121
  8.3 9.8 %shard_map.68 = (bf16[2,2,16,640]{3,2,1,0:T(8,128)(2,1)}, bf16[2,2,16,640]{3,2,1,0:T(8,128)(2,1)}, bf16[4,2,640]{2,1,0:T(2,128)(2,1)}) custom-call(bf16[2,2,16,640]{3,2,1,0:T(8,128)(2,1)} %copy.124.refs_0_, bf16[2,2,16,640]{3,2,1,0:T(8,128)(2,1)} %copy.125.refs_1_, bf16[4,2,640]{2,1,0:T(2,128)(2,1)} %pad_maximum_fusion.5.refs_2_), custom_call_target="tpu_custom_call" | custom-call | tf_op jit(solution)/shard_map/pallas_call | solution.py:130
  21.0 2.5 %pad_maximum_fusion = bf16[2,18,18,640]{3,0,2,1:T(2,128)(2,1)S(1)} fusion(bf16[2,1,18,640]{3,0,2,1:T(2,128)(2,1)S(1)} %get-tuple-element.87, bf16[2,16,1,640]{3,0,2,1:T(2,128)(2,1)S(1)} %get-tuple-element.81, bf16[1,16,16,640]{3,0,2,1:T(2,128)(2,1)S(1)} %copy.122, bf16[1,16,16,640]{3,0,2,1:T(2,128)(2,1)S(1)} %copy.121, ...), kind=kLoop, calls=%fused_computation.25 | loop fusion | flops 4976640 | bytes 1658880 | tf_op jit(solution)/shard_map/concatenate | solution.py:154
  23.5 5.5 %slice_reduce_fusion = (bf16[18,18,640]{2,1,0:T(8,128)(2,1)}, bf16[18,18,640]{2,1,0:T(8,128)(2,1)}, bf16[1,18,18,640]{3,0,2,1:T(2,128)(2,1)}, bf16[1,18,18,640]{3,0,2,1:T(2,128)(2,1)}) fusion(bf16[2,18,18,640]{3,0,2,1:T(2,128)(2,1)S(1)} %pad_maximum_fusion), kind=kLoop, calls=%fused_computation.143 | loop fusion | bytes 2488320 | tf_op jit(solution)/shard_map/slice | solution.py:185
  29.0 2.0 %reshape_squeeze.6 = bf16[324,640]{1,0:T(8,128)(2,1)} reshape(bf16[18,18,640]{2,1,0:T(8,128)(2,1)} %get-tuple-element.21) | data formatting | bytes 829440 | tf_op jit(solution)/shard_map/reshape;squeeze | solution.py:195
  31.0 2.6 %reshape.263 = f32[9,640,2,64]{1,0,3,2:T(8,128)} reshape(f32[5760,2,64]{0,2,1:T(8,128)S(1)} %copy-done.1) | data formatting | bytes 5898240 | tf_op jit(solution)/shard_map/reshape | solution.py:197
  33.6 2.9 %fusion.58 = (f32[1,640,9,64]{1,2,3,0:T(8,128)S(1)}, f32[1,640,9,64]{1,2,3,0:T(8,128)S(1)}) fusion(f32[2,640,9,64]{1,2,3,0:T(8,128)} %bitcast.275), kind=kLoop, calls=%fused_computation.145 | loop fusion | bytes 5898240 | tf_op jit(solution)/shard_map/slice | solution.py:199
  36.4 2.0 %fusion = f32[16,16,9,64]{3,1,2,0:T(8,128)S(1)} fusion(f32[1,640,9,64]{1,2,3,0:T(8,128)S(1)} %get-tuple-element.23, bf16[1,16,16,640]{3,2,1,0:T(8,128)(2,1)S(1)} %copy-done.8), kind=kOutput, calls=%fused_computation.3 | convolution fusion | flops 1133445120 | bytes 2392064 | tf_op jit(solution)/shard_map/dot_general | solution.py:163
  41.1 2.9 %fusion.2 = f32[18,18,9,64]{3,1,2,0:T(8,128)S(1)} fusion(f32[1,640,9,64]{1,2,3,0:T(8,128)S(1)} %get-tuple-element.22, bf16[1,18,18,640]{3,0,2,1:T(2,128)(2,1)S(1)} %copy-done.4), kind=kOutput, calls=%fused_computation.5 | convolution fusion | flops 1433272320 | bytes 2635776 | tf_op jit(solution)/shard_map/dot_general | solution.py:163
  50.9 35.2 %shard_map.69 = f32[8,32,320]{2,1,0:T(8,128)} custom-call(f32[8,32,320]{2,1,0:T(8,128)} %reshape.265.p_ref), custom_call_target="tpu_custom_call" | custom-call | tf_op jit(solution)/shard_map/pallas_call | solution.py:309
  86.1 1.4 reshape.266
  95.5 1.6 concatenate.26
  98.4 1.5 convolution_bitcast_fusion.1
  100.0 5.6 %copy.152 = f32[9,640,2,64]{3,2,1,0:T(2,128)} copy(f32[9,640,2,64]{1,3,0,2:T(8,128)S(1)} %maximum_bitcast_fusion) | data formatting | bytes 5898240 | tf_op jit(solution)/shard_map/transpose | solution.py:231
  105.6 5.4 %reshape_reshape.3 = f32[32,180,128]{2,1,0:T(8,128)S(1)} reshape(f32[9,640,2,64]{3,2,1,0:T(2,128)} %copy.152) | data formatting | bytes 5898240 | tf_op jit(solution)/shard_map/reshape;reshape | solution.py:346
  111.1 2.0 %pad_slice_fusion = (f32[16,192,128]{2,1,0:T(8,128)}, f32[16,192,128]{2,1,0:T(8,128)}) fusion(f32[32,180,128]{2,1,0:T(8,128)S(1)} %reshape_reshape.3), kind=kLoop, calls=%fused_computation | loop fusion | bytes 6094848 | tf_op jit(solution)/shard_map/slice | solution.py:350
  113.1 1.6 constant_dynamic-slice_fusion.5
  115.6 1.7 collective-permute-start
  120.1 12.0 %custom-call.9 = f32[2,64,64]{2,1,0:T(8,128)S(1)} custom-call(f32[2,64,64]{2,1,0:T(8,128)S(1)} %fusion.47), custom_call_target="Cholesky" | custom-call | tf_op jit(solution)/shard_map/jit(cholesky)/cholesky | solution.py:237
  132.3 9.8 %custom-call.10 = f32[2,1,64,64]{2,3,1,0:T(8,128)S(1)} custom-call(f32[2,1,64,64]{3,2,1,0:T(8,128)S(1)} %select_bitcast_fusion), custom_call_target="InvertDiagBlocksLowerTriangular" | custom-call | tf_op jit(solution)/shard_map/triangular_solve | solution.py:240
  146.2 13.5 %shard_map.70 = (f32[4,16,24,128]{3,2,1,0:T(8,128)S(1)}, f32[2,16,24,128]{3,2,1,0:T(8,128)S(1)}) custom-call(f32[4,16,24,128]{3,2,1,0:T(8,128)S(1)} %fusion.27.refs_0_, f32[2,16,24,128]{3,2,1,0:T(8,128)S(1)} %fusion.41.refs_1_), custom_call_target="tpu_custom_call" | custom-call | tf_op jit(solution)/shard_map/pallas_call | solution.py:76
  159.8 13.4 %shard_map.71 = f32[32,24,128]{2,1,0:T(8,128)S(1)} custom-call(f32[32,24,128]{2,1,0:T(8,128)S(1)} %pad_maximum_fusion.1.refs_0_), custom_call_target="tpu_custom_call" | custom-call | tf_op jit(solution)/shard_map/pallas_call | solution.py:76
  173.3 9.9 %shard_map.72 = f32[8,24,128]{2,1,0:T(8,128)S(1)} custom-call(f32[24,128]{1,0:T(8,128)S(1)} %reduce_sum.29.refs_0_), custom_call_target="tpu_custom_call" | custom-call | tf_op jit(solution)/shard_map/pallas_call | solution.py:76
  (113 shorter events, 35.1 us)
Async XLA Ops:
  2.1 2.0 %copy-start.8 = (bf16[1,16,16,640]{3,2,1,0:T(8,128)(2,1)S(1)}, bf16[1,16,16,640]{3,2,1,0:T(8,128)(2,1)}, u32[]{:S(2)}) copy-start(bf16[1,16,16,640]{3,2,1,0:T(8,128)(2,1)} %param.6) | copy-start | bytes 983044
  23.5 7.5 %copy-start.1 = (f32[5760,2,64]{0,2,1:T(8,128)S(1)}, f32[5760,2,64]{0,2,1:T(8,128)}, u32[]{:S(2)}) copy-start(f32[5760,2,64]{0,2,1:T(8,128)} %param.9) | copy-start | bytes 8847364
  39.5 1.7 copy-start.4
  39.5 5.2 %slice-start = ((s8[7372800]{0:T(1024)(128)(4,1)}), s8[4194304]{0:T(1024)(128)(4,1)S(1)}, s32[]{:S(2)}) async-start(s8[7372800]{0:T(1024)(128)(4,1)} %bitcast.276), calls=%async_computation | async-start | bytes 8388608
  40.8 3.8 %slice-start.1 = ((s8[7372800]{0:T(1024)(128)(4,1)}), s8[3178496]{0:T(1024)(128)(4,1)S(1)}, s32[]{:S(2)}) async-start(s8[7372800]{0:T(1024)(128)(4,1)} %bitcast.276), calls=%async_computation.1 | async-start | bytes 6356992
  41.1 3.0 %copy-start.6 = (bf16[324,640]{1,0:T(8,128)(2,1)S(1)}, bf16[324,640]{1,0:T(8,128)(2,1)}, u32[]{:S(2)}) copy-start(bf16[324,640]{1,0:T(8,128)(2,1)} %reshape_squeeze.6) | copy-start | bytes 1244164
  41.1 3.0 %copy-start.9 = (f32[324,64]{1,0:T(8,128)S(1)}, f32[324,64]{1,0:T(8,128)}, u32[]{:S(2)}) copy-start(f32[324,64]{1,0:T(8,128)} %reshape.264) | copy-start | bytes 248836
  47.5 1.1 copy-start.3
  87.5 2.9 %copy-start.2 = (f32[640,2,64]{2,1,0:T(2,128)}, f32[640,2,64]{2,1,0:T(2,128)S(1)}, u32[]{:S(2)}) copy-start(f32[640,2,64]{2,1,0:T(2,128)S(1)} %reshape.266) | copy-start | bytes 983044
  88.4 2.3 %copy-start.5 = (bf16[18,18,640]{2,1,0:T(8,128)(2,1)S(1)}, bf16[18,18,640]{2,1,0:T(8,128)(2,1)}, u32[]{:S(2)}) copy-start(bf16[18,18,640]{2,1,0:T(8,128)(2,1)} %get-tuple-element.20) | copy-start | bytes 1244164
  95.4 2.0 %copy-start.7 = (bf16[1,16,16,640]{3,2,1,0:T(8,128)(2,1)S(1)}, bf16[1,16,16,640]{3,2,1,0:T(8,128)(2,1)}, u32[]{:S(2)}) copy-start(bf16[1,16,16,640]{3,2,1,0:T(8,128)(2,1)} %fusion.31) | copy-start | bytes 983044
  113.1 4.3 %copy-start = (f32[16,192,128]{2,1,0:T(8,128)S(1)}, f32[16,192,128]{2,1,0:T(8,128)}, u32[]{:S(2)}) copy-start(f32[16,192,128]{2,1,0:T(8,128)} %get-tuple-element.24) | copy-start | bytes 4718596
  115.6 29.3 %collective-permute-start = (f32[16,4,24,128]{3,2,0,1:T(8,128)}, f32[16,4,24,128]{3,2,0,1:T(8,128)}, u32[]{:S(2)}, u32[]{:S(2)}) collective-permute-start(f32[16,4,24,128]{3,2,0,1:T(8,128)} %bitcast.267), channel_id=1, source_target_pairs={{0,4},{4,0},{1,5},{5,1},{2,6},{6,2},{3,7},{7,3},{8,12},{12,8},{9,1... | collective-permute-start | bytes 2359304 | tf_op jit(solution)/shard_map/ppermute | solution.py:335
  117.6 26.1 %collective-permute-start.3 = (f32[16,2,24,128]{3,2,0,1:T(8,128)S(1)}, f32[16,2,24,128]{3,2,0,1:T(8,128)S(1)}, u32[]{:S(2)}, u32[]{:S(2)}) collective-permute-start(f32[16,2,24,128]{3,2,0,1:T(8,128)S(1)} %bitcast.306), channel_id=1, source_target_pairs={{0,3},{1,0},{2,1},{3,2},{4,7},{5,4},{6,5},{7,6},{8,11},{9,8},{10,9... | collective-permute-start | bytes 1179656 | tf_op jit(solution)/shard_map/ppermute | solution.py:335
  118.2 25.6 %collective-permute-start.2 = (f32[16,2,24,128]{3,2,0,1:T(8,128)S(1)}, f32[16,2,24,128]{3,2,0,1:T(8,128)}, u32[]{:S(2)}, u32[]{:S(2)}) collective-permute-start(f32[16,2,24,128]{3,2,0,1:T(8,128)S(1)} %bitcast.307), channel_id=1, source_target_pairs={{0,2},{1,3},{2,0},{3,1},{4,6},{5,7},{6,4},{7,5},{8,10},{9,11},{10,... | collective-permute-start | bytes 1179656 | tf_op jit(solution)/shard_map/ppermute | solution.py:335
  119.1 24.6 %collective-permute-start.1 = (f32[16,2,24,128]{3,2,0,1:T(8,128)S(1)}, f32[16,2,24,128]{3,2,0,1:T(8,128)}, u32[]{:S(2)}, u32[]{:S(2)}) collective-permute-start(f32[16,2,24,128]{3,2,0,1:T(8,128)S(1)} %bitcast.308), channel_id=1, source_target_pairs={{0,1},{1,2},{2,3},{3,0},{4,5},{5,6},{6,7},{7,4},{8,9},{9,10},{10,1... | collective-permute-start | bytes 1179656 | tf_op jit(solution)/shard_map/ppermute | solution.py:335

commit v9 on v7

--- a/solution.py
+++ b/solution.py
@@ -227,8 +227,13 @@
         axis=1,
     )
     second_rows = exact_dot(hidden, second_spread, ((0,), (0,)))
-    rows = jnp.stack([first_rows, second_rows]).reshape(2, channels, taps, rank)
-    rows = rows.transpose(2, 1, 0, 3).reshape(taps * channels, 2, rank)
+    rows = jnp.concatenate(
+        [
+            first_rows.reshape(channels, taps, rank).transpose(1, 0, 2),
+            second_rows.reshape(channels, taps, rank).transpose(1, 0, 2),
+        ],
+        axis=-1,
+    ).reshape(taps * channels, 2, rank)
     row_block = block_sum(rows, sizes)
 
     gram = jnp.einsum(

time: 185 us -> 179 us (0.968)
  local copies, waits for them, and re-layouts: 50.8 us -> 45.2 us
    transpose x1 -> x0, local copies, waits for them, and re-layouts: 5.57 us -> none  [on_device(): rows = rows.transpose(2, 1, 0, 3).reshape(taps * channels, 2, rank)]
    another operation x1, local copies, waits for them, and re-layouts: 5.45 us -> 2.58 us  [block_sum(): value.reshape(blocks, block_rows, lanes)]
    concatenate x0 -> x1, local copies, waits for them, and re-layouts: none -> 2.74 us  [on_device(): jnp.concatenate([first_rows.reshape(channels, taps, rank).transpose(1, 0,...]
where the time goes in v9:
time: 179 us
  Pallas kernels  81.8 us (46%)
  local copies, waits for them, and re-layouts  45.2 us (25%)
  other arithmetic  31.9 us (18%)
  matrix products  14.8 us (8%)
  starting transfers between devices  3.57 us (2%)
    pallas_call x3, Pallas kernels, exchange_many(): pl.pallas_call(functools.partial(exchange_kernel, jobs=tuple(jobs), sizes...  36.8 us
    pallas_call x1, Pallas kernels, all_sum_small(): pl.pallas_call(functools.partial(allsum_kernel, sizes=sizes), out_shape=j...  35.2 us
    another operation x4, other arithmetic, on_device(): lower = jnp.linalg.cholesky(gram)  12.2 us
    another operation x3, other arithmetic, on_device(): lax.linalg.triangular_solve(lower, raw_part.transpose(1, 0, 2), left_side...  9.92 us
    pallas_call x1, Pallas kernels, padded_pair(): pl.pallas_call(functools.partial(halo_kernel, sizes=sizes), out_shape=tup...  9.81 us
    dot_general x8, matrix products, exact_dot(): lax.dot_general(left.astype(jnp.float32), right.astype(jnp.float32), (con...  9.06 us
    unnamed x32, local copies, waits for them, and re-layouts  6.21 us
    slice x1, local copies, waits for them, and re-layouts, on_device(): grad_pad, input_pad = (both_pad[0], both_pad[1])  5.5 us
  transfers between devices with their start and end apart: 4, of which 0 were waited for; matrix products, arithmetic and copies ran while one was open for 14% of the time, Pallas kernels for 0%

profile of v9, /device:TPU:1, one launch (start us, length us, event | category | flops | bytes accessed | tf_op | source)
XLA Modules:
  0.0 178.5 jit_solution(17041713279623018975)
XLA Ops:
  0.6 1.5 copy.122
  2.1 1.5 copy.121
  8.3 9.8 %shard_map.68 = (bf16[2,2,16,640]{3,2,1,0:T(8,128)(2,1)}, bf16[2,2,16,640]{3,2,1,0:T(8,128)(2,1)}, bf16[4,2,640]{2,1,0:T(2,128)(2,1)}) custom-call(bf16[2,2,16,640]{3,2,1,0:T(8,128)(2,1)} %copy.124.refs_0_, bf16[2,2,16,640]{3,2,1,0:T(8,128)(2,1)} %copy.125.refs_1_, bf16[4,2,640]{2,1,0:T(2,128)(2,1)} %pad_maximum_fusion.6.refs_2_), custom_call_target="tpu_custom_call" | custom-call | tf_op jit(solution)/shard_map/pallas_call | solution.py:130
  21.0 2.5 %pad_maximum_fusion.1 = bf16[2,18,18,640]{3,0,2,1:T(2,128)(2,1)S(1)} fusion(bf16[2,1,18,640]{3,0,2,1:T(2,128)(2,1)S(1)} %get-tuple-element.87, bf16[2,16,1,640]{3,0,2,1:T(2,128)(2,1)S(1)} %get-tuple-element.81, bf16[1,16,16,640]{3,0,2,1:T(2,128)(2,1)S(1)} %copy.122, bf16[1,16,16,640]{3,0,2,1:T(2,128)(2,1)S(1)} %copy.121, ...), kind=kLoop, calls=%fused_computation.25 | loop fusion | flops 4976640 | bytes 1658880 | tf_op jit(solution)/shard_map/concatenate | solution.py:154
  23.5 5.5 %slice_reduce_fusion = (bf16[18,18,640]{2,1,0:T(8,128)(2,1)}, bf16[18,18,640]{2,1,0:T(8,128)(2,1)}, bf16[1,18,18,640]{3,0,2,1:T(2,128)(2,1)}, bf16[1,18,18,640]{3,0,2,1:T(2,128)(2,1)}) fusion(bf16[2,18,18,640]{3,0,2,1:T(2,128)(2,1)S(1)} %pad_maximum_fusion.1), kind=kLoop, calls=%fused_computation.143 | loop fusion | bytes 2488320 | tf_op jit(solution)/shard_map/slice | solution.py:185
  29.0 2.0 %reshape_squeeze.6 = bf16[324,640]{1,0:T(8,128)(2,1)} reshape(bf16[18,18,640]{2,1,0:T(8,128)(2,1)} %get-tuple-element.21) | data formatting | bytes 829440 | tf_op jit(solution)/shard_map/reshape;squeeze | solution.py:195
  31.0 2.6 %reshape.252 = f32[9,640,2,64]{1,0,3,2:T(8,128)} reshape(f32[5760,2,64]{0,2,1:T(8,128)S(1)} %copy-done.1) | data formatting | bytes 5898240 | tf_op jit(solution)/shard_map/reshape | solution.py:197
  33.6 2.9 %fusion.58 = (f32[1,640,9,64]{1,2,3,0:T(8,128)S(1)}, f32[1,640,9,64]{1,2,3,0:T(8,128)S(1)}) fusion(f32[2,640,9,64]{1,2,3,0:T(8,128)} %bitcast.281), kind=kLoop, calls=%fused_computation.145 | loop fusion | bytes 5898240 | tf_op jit(solution)/shard_map/slice | solution.py:199
  36.4 2.0 %fusion = f32[16,16,9,64]{3,1,2,0:T(8,128)S(1)} fusion(f32[1,640,9,64]{1,2,3,0:T(8,128)S(1)} %get-tuple-element.23, bf16[1,16,16,640]{3,2,1,0:T(8,128)(2,1)S(1)} %copy-done.8), kind=kOutput, calls=%fused_computation.3 | convolution fusion | flops 1133445120 | bytes 2392064 | tf_op jit(solution)/shard_map/dot_general | solution.py:163
  41.1 2.9 %fusion.2 = f32[18,18,9,64]{3,1,2,0:T(8,128)S(1)} fusion(f32[1,640,9,64]{1,2,3,0:T(8,128)S(1)} %get-tuple-element.22, bf16[1,18,18,640]{3,0,2,1:T(2,128)(2,1)S(1)} %copy-done.4), kind=kOutput, calls=%fused_computation.5 | convolution fusion | flops 1433272320 | bytes 2635776 | tf_op jit(solution)/shard_map/dot_general | solution.py:163
  50.9 35.2 %shard_map.69 = f32[8,32,320]{2,1,0:T(8,128)} custom-call(f32[8,32,320]{2,1,0:T(8,128)} %reshape.254.p_ref), custom_call_target="tpu_custom_call" | custom-call | tf_op jit(solution)/shard_map/pallas_call | solution.py:314
  86.1 1.4 reshape.255
  95.5 1.6 concatenate.28
  98.4 1.5 convolution_bitcast_fusion.1
  100.1 2.7 %copy.152 = f32[9,640,128]{2,1,0:T(8,128)} copy(f32[9,640,128]{1,2,0:T(8,128)S(1)} %pad_maximum_fusion) | data formatting | bytes 5898240 | tf_op jit(solution)/shard_map/concatenate | solution.py:230
  102.8 2.6 %reshape_reshape.3 = f32[32,180,128]{2,1,0:T(8,128)S(1)} reshape(f32[9,640,128]{2,1,0:T(8,128)} %copy.152) | data formatting | bytes 5898240 | tf_op jit(solution)/shard_map/reshape;reshape | solution.py:351
  105.4 2.0 %pad_slice_fusion = (f32[16,192,128]{2,1,0:T(8,128)}, f32[16,192,128]{2,1,0:T(8,128)}) fusion(f32[32,180,128]{2,1,0:T(8,128)S(1)} %reshape_reshape.3), kind=kLoop, calls=%fused_computation | loop fusion | bytes 6094848 | tf_op jit(solution)/shard_map/slice | solution.py:355
  107.4 1.6 constant_dynamic-slice_fusion.5
  110.0 1.7 collective-permute-start
  114.4 12.0 %custom-call.9 = f32[2,64,64]{2,1,0:T(8,128)S(1)} custom-call(f32[2,64,64]{2,1,0:T(8,128)S(1)} %fusion.47), custom_call_target="Cholesky" | custom-call | tf_op jit(solution)/shard_map/jit(cholesky)/cholesky | solution.py:242
  126.6 9.8 %custom-call.10 = f32[2,1,64,64]{2,3,1,0:T(8,128)S(1)} custom-call(f32[2,1,64,64]{3,2,1,0:T(8,128)S(1)} %select_bitcast_fusion), custom_call_target="InvertDiagBlocksLowerTriangular" | custom-call | tf_op jit(solution)/shard_map/triangular_solve | solution.py:245
  140.5 13.5 %shard_map.70 = (f32[4,16,24,128]{3,2,1,0:T(8,128)S(1)}, f32[2,16,24,128]{3,2,1,0:T(8,128)S(1)}) custom-call(f32[4,16,24,128]{3,2,1,0:T(8,128)S(1)} %fusion.27.refs_0_, f32[2,16,24,128]{3,2,1,0:T(8,128)S(1)} %fusion.41.refs_1_), custom_call_target="tpu_custom_call" | custom-call | tf_op jit(solution)/shard_map/pallas_call | solution.py:76
  154.1 13.4 %shard_map.71 = f32[32,24,128]{2,1,0:T(8,128)S(1)} custom-call(f32[32,24,128]{2,1,0:T(8,128)S(1)} %pad_maximum_fusion.2.refs_0_), custom_call_target="tpu_custom_call" | custom-call | tf_op jit(solution)/shard_map/pallas_call | solution.py:76
  167.6 9.9 %shard_map.72 = f32[8,24,128]{2,1,0:T(8,128)S(1)} custom-call(f32[24,128]{1,0:T(8,128)S(1)} %reduce_sum.29.refs_0_), custom_call_target="tpu_custom_call" | custom-call | tf_op jit(solution)/shard_map/pallas_call | solution.py:76
  (113 shorter events, 35.1 us)
Async XLA Ops:
  2.1 2.0 %copy-start.8 = (bf16[1,16,16,640]{3,2,1,0:T(8,128)(2,1)S(1)}, bf16[1,16,16,640]{3,2,1,0:T(8,128)(2,1)}, u32[]{:S(2)}) copy-start(bf16[1,16,16,640]{3,2,1,0:T(8,128)(2,1)} %param.6) | copy-start | bytes 983044
  23.5 7.5 %copy-start.1 = (f32[5760,2,64]{0,2,1:T(8,128)S(1)}, f32[5760,2,64]{0,2,1:T(8,128)}, u32[]{:S(2)}) copy-start(f32[5760,2,64]{0,2,1:T(8,128)} %param.9) | copy-start | bytes 8847364
  39.5 1.7 copy-start.4
  39.5 5.2 %slice-start = ((s8[7372800]{0:T(1024)(128)(4,1)}), s8[4194304]{0:T(1024)(128)(4,1)S(1)}, s32[]{:S(2)}) async-start(s8[7372800]{0:T(1024)(128)(4,1)} %bitcast.282), calls=%async_computation | async-start | bytes 8388608
  40.8 3.8 %slice-start.1 = ((s8[7372800]{0:T(1024)(128)(4,1)}), s8[3178496]{0:T(1024)(128)(4,1)S(1)}, s32[]{:S(2)}) async-start(s8[7372800]{0:T(1024)(128)(4,1)} %bitcast.282), calls=%async_computation.1 | async-start | bytes 6356992
  41.1 3.0 %copy-start.6 = (bf16[324,640]{1,0:T(8,128)(2,1)S(1)}, bf16[324,640]{1,0:T(8,128)(2,1)}, u32[]{:S(2)}) copy-start(bf16[324,640]{1,0:T(8,128)(2,1)} %reshape_squeeze.6) | copy-start | bytes 1244164
  41.1 3.0 %copy-start.9 = (f32[324,64]{1,0:T(8,128)S(1)}, f32[324,64]{1,0:T(8,128)}, u32[]{:S(2)}) copy-start(f32[324,64]{1,0:T(8,128)} %reshape.253) | copy-start | bytes 248836
  47.5 1.1 copy-start.3
  87.5 2.9 %copy-start.2 = (f32[640,2,64]{2,1,0:T(2,128)}, f32[640,2,64]{2,1,0:T(2,128)S(1)}, u32[]{:S(2)}) copy-start(f32[640,2,64]{2,1,0:T(2,128)S(1)} %reshape.255) | copy-start | bytes 983044
  88.4 2.3 %copy-start.5 = (bf16[18,18,640]{2,1,0:T(8,128)(2,1)S(1)}, bf16[18,18,640]{2,1,0:T(8,128)(2,1)}, u32[]{:S(2)}) copy-start(bf16[18,18,640]{2,1,0:T(8,128)(2,1)} %get-tuple-element.20) | copy-start | bytes 1244164
  95.5 2.0 %copy-start.7 = (bf16[1,16,16,640]{3,2,1,0:T(8,128)(2,1)S(1)}, bf16[1,16,16,640]{3,2,1,0:T(8,128)(2,1)}, u32[]{:S(2)}) copy-start(bf16[1,16,16,640]{3,2,1,0:T(8,128)(2,1)} %fusion.31) | copy-start | bytes 983044
  107.4 4.3 %copy-start = (f32[16,192,128]{2,1,0:T(8,128)S(1)}, f32[16,192,128]{2,1,0:T(8,128)}, u32[]{:S(2)}) copy-start(f32[16,192,128]{2,1,0:T(8,128)} %get-tuple-element.24) | copy-start | bytes 4718596
  110.0 29.3 %collective-permute-start = (f32[4,16,24,128]{3,2,1,0:T(8,128)}, f32[4,16,24,128]{3,2,1,0:T(8,128)}, u32[]{:S(2)}, u32[]{:S(2)}) collective-permute-start(f32[4,16,24,128]{3,2,1,0:T(8,128)} %bitcast.273), channel_id=1, source_target_pairs={{0,4},{4,0},{1,5},{5,1},{2,6},{6,2},{3,7},{7,3},{8,12},{12,8},{9,1... | collective-permute-start | bytes 2359304 | tf_op jit(solution)/shard_map/ppermute | solution.py:340
  111.9 26.1 %collective-permute-start.3 = (f32[2,16,24,128]{3,2,1,0:T(8,128)S(1)}, f32[2,16,24,128]{3,2,1,0:T(8,128)S(1)}, u32[]{:S(2)}, u32[]{:S(2)}) collective-permute-start(f32[2,16,24,128]{3,2,1,0:T(8,128)S(1)} %bitcast.312), channel_id=1, source_target_pairs={{0,3},{1,0},{2,1},{3,2},{4,7},{5,4},{6,5},{7,6},{8,11},{9,8},{10,9... | collective-permute-start | bytes 1179656 | tf_op jit(solution)/shard_map/ppermute | solution.py:340
  112.5 25.6 %collective-permute-start.2 = (f32[2,16,24,128]{3,2,1,0:T(8,128)S(1)}, f32[2,16,24,128]{3,2,1,0:T(8,128)}, u32[]{:S(2)}, u32[]{:S(2)}) collective-permute-start(f32[2,16,24,128]{3,2,1,0:T(8,128)S(1)} %bitcast.313), channel_id=1, source_target_pairs={{0,2},{1,3},{2,0},{3,1},{4,6},{5,7},{6,4},{7,5},{8,10},{9,11},{10,... | collective-permute-start | bytes 1179656 | tf_op jit(solution)/shard_map/ppermute | solution.py:340
  113.4 24.6 %collective-permute-start.1 = (f32[2,16,24,128]{3,2,1,0:T(8,128)S(1)}, f32[2,16,24,128]{3,2,1,0:T(8,128)}, u32[]{:S(2)}, u32[]{:S(2)}) collective-permute-start(f32[2,16,24,128]{3,2,1,0:T(8,128)S(1)} %bitcast.314), channel_id=1, source_target_pairs={{0,1},{1,2},{2,3},{3,0},{4,5},{5,6},{6,7},{7,4},{8,9},{9,10},{10,1... | collective-permute-start | bytes 1179656 | tf_op jit(solution)/shard_map/ppermute | solution.py:340

commit v10 on v9

--- a/solution.py
+++ b/solution.py
@@ -196,14 +196,16 @@
     input_flat = input_pad.reshape(-1, channels)
     q_taps = q_prev.reshape(taps, channels, 2, rank).transpose(2, 1, 0, 3).reshape(2, channels, taps * rank)
 
-    first_terms = exact_dot(input_flat, q_taps[0], ((1,), (0,))).reshape(grid + (taps, rank))
+    first_terms = exact_dot(input_flat, q_taps[0], ((1,), (0,))).reshape(grid + (taps * rank,))
     first_sum = sum(
-        first_terms[1 + a : 1 + a + height, 1 + b : 1 + b + breadth, k] for k, (a, b) in enumerate(TAPS)
+        first_terms[1 + a : 1 + a + height, 1 + b : 1 + b + breadth, k * rank : (k + 1) * rank]
+        for k, (a, b) in enumerate(TAPS)
     ).reshape(pixels, rank)
     first_raw = exact_dot(pre_grad, first_sum, ((0,), (0,)))
-    second_terms = exact_dot(hidden, q_taps[1], ((1,), (0,))).reshape(height, breadth, taps, rank)
+    second_terms = exact_dot(hidden, q_taps[1], ((1,), (0,))).reshape(height, breadth, taps * rank)
     second_sum = sum(
-        jnp.pad(second_terms[:, :, k], ((1 - a, 1 + a), (1 - b, 1 + b), (0, 0))) for k, (a, b) in enumerate(TAPS)
+        jnp.pad(second_terms[:, :, k * rank : (k + 1) * rank], ((1 - a, 1 + a), (1 - b, 1 + b), (0, 0)))
+        for k, (a, b) in enumerate(TAPS)
     ).reshape(-1, rank)
     second_raw = exact_dot(grad_flat, second_sum, ((0,), (0,)))
 

time: 179 us -> 178 us (level)
  matrix products: 14.8 us -> 12.9 us
    dot_general x8, matrix products: 9.06 us -> 7.08 us  [exact_dot(): lax.dot_general(left.astype(jnp.float32), right.astype(jnp.float32), (con...]
    unnamed x32 -> x34, local copies, waits for them, and re-layouts: 6.21 us -> 7.34 us
where the time goes in v10:
time: 178 us
  Pallas kernels  81.7 us (46%)
  local copies, waits for them, and re-layouts  46.2 us (26%)
  other arithmetic  32 us (18%)
  matrix products  12.9 us (7%)
  starting transfers between devices  3.58 us (2%)
    pallas_call x3, Pallas kernels, exchange_many(): pl.pallas_call(functools.partial(exchange_kernel, jobs=tuple(jobs), sizes...  36.8 us
    pallas_call x1, Pallas kernels, all_sum_small(): pl.pallas_call(functools.partial(allsum_kernel, sizes=sizes), out_shape=j...  35.2 us
    another operation x4, other arithmetic, on_device(): lower = jnp.linalg.cholesky(gram)  12.2 us
    another operation x3, other arithmetic, on_device(): lax.linalg.triangular_solve(lower, raw_part.transpose(1, 0, 2), left_side...  9.92 us
    pallas_call x1, Pallas kernels, padded_pair(): pl.pallas_call(functools.partial(halo_kernel, sizes=sizes), out_shape=tup...  9.81 us
    unnamed x34, local copies, waits for them, and re-layouts  7.34 us
    dot_general x8, matrix products, exact_dot(): lax.dot_general(left.astype(jnp.float32), right.astype(jnp.float32), (con...  7.08 us
    slice x1, local copies, waits for them, and re-layouts, on_device(): grad_pad, input_pad = (both_pad[0], both_pad[1])  5.33 us
  transfers between devices with their start and end apart: 4, of which 0 were waited for; matrix products, arithmetic and copies ran while one was open for 14% of the time, Pallas kernels for 0%

profile of v10, /device:TPU:1, one launch (start us, length us, event | category | flops | bytes accessed | tf_op | source)
XLA Modules:
  0.0 177.7 jit_solution(16092076405091905520)
XLA Ops:
  0.6 1.5 copy.66
  2.1 1.5 copy.65
  8.3 9.8 %shard_map.68 = (bf16[2,2,16,640]{3,2,1,0:T(8,128)(2,1)}, bf16[2,2,16,640]{3,2,1,0:T(8,128)(2,1)}, bf16[4,2,640]{2,1,0:T(2,128)(2,1)}) custom-call(bf16[2,2,16,640]{3,2,1,0:T(8,128)(2,1)} %copy.68.refs_0_, bf16[2,2,16,640]{3,2,1,0:T(8,128)(2,1)} %copy.69.refs_1_, bf16[4,2,640]{2,1,0:T(2,128)(2,1)} %pad_maximum_fusion.6.refs_2_), custom_call_target="tpu_custom_call" | custom-call | tf_op jit(solution)/shard_map/pallas_call | solution.py:130
  21.0 2.5 %pad_maximum_fusion.1 = bf16[2,18,18,640]{3,0,2,1:T(2,128)(2,1)S(1)} fusion(bf16[2,1,18,640]{3,0,2,1:T(2,128)(2,1)S(1)} %get-tuple-element.85, bf16[2,16,1,640]{3,0,2,1:T(2,128)(2,1)S(1)} %get-tuple-element.79, bf16[1,16,16,640]{3,0,2,1:T(2,128)(2,1)S(1)} %copy.66, bf16[1,16,16,640]{3,0,2,1:T(2,128)(2,1)S(1)} %copy.65, ...), kind=kLoop, calls=%fused_computation.19 | loop fusion | flops 4976640 | bytes 1658880 | tf_op jit(solution)/shard_map/concatenate | solution.py:154
  23.5 5.3 %slice_reduce_fusion = (bf16[18,18,640]{2,1,0:T(8,128)(2,1)}, bf16[18,18,640]{2,1,0:T(8,128)(2,1)S(1)}, bf16[1,18,18,640]{3,0,2,1:T(2,128)(2,1)}, bf16[1,18,18,640]{3,0,2,1:T(2,128)(2,1)}) fusion(bf16[2,18,18,640]{3,0,2,1:T(2,128)(2,1)S(1)} %pad_maximum_fusion.1), kind=kLoop, calls=%fused_computation.130 | loop fusion | bytes 2488320 | tf_op jit(solution)/shard_map/slice | solution.py:185
  29.8 2.6 %reshape.239 = f32[9,640,2,64]{1,0,3,2:T(8,128)} reshape(f32[5760,2,64]{0,2,1:T(8,128)S(1)} %copy-done.1) | data formatting | bytes 5898240 | tf_op jit(solution)/shard_map/reshape | solution.py:197
  32.3 2.9 %fusion.54 = (f32[1,640,9,64]{1,2,3,0:T(8,128)S(1)}, f32[1,640,9,64]{1,2,3,0:T(8,128)S(1)}) fusion(f32[2,640,9,64]{1,2,3,0:T(8,128)} %bitcast.232), kind=kLoop, calls=%fused_computation.132 | loop fusion | bytes 5898240 | tf_op jit(solution)/shard_map/slice | solution.py:199
  36.2 1.3 fusion.37
  41.4 1.7 fusion.31
  48.8 1.3 reshape.242.p_ref
  50.1 35.2 %shard_map.69 = f32[8,32,320]{2,1,0:T(8,128)} custom-call(f32[8,32,320]{2,1,0:T(8,128)} %reshape.242.p_ref), custom_call_target="tpu_custom_call" | custom-call | tf_op jit(solution)/shard_map/pallas_call | solution.py:316
  85.2 1.4 reshape.243
  94.7 1.6 concatenate.28
  97.5 1.5 convolution_bitcast_fusion.1
  99.2 2.7 %copy.88 = f32[9,640,128]{2,1,0:T(8,128)} copy(f32[9,640,128]{1,2,0:T(8,128)S(1)} %pad_maximum_fusion) | data formatting | bytes 5898240 | tf_op jit(solution)/shard_map/concatenate | solution.py:232
  102.0 2.6 %reshape_reshape.3 = f32[32,180,128]{2,1,0:T(8,128)S(1)} reshape(f32[9,640,128]{2,1,0:T(8,128)} %copy.88) | data formatting | bytes 5898240 | tf_op jit(solution)/shard_map/reshape;reshape | solution.py:353
  104.5 2.0 %pad_slice_fusion = (f32[16,192,128]{2,1,0:T(8,128)}, f32[16,192,128]{2,1,0:T(8,128)}) fusion(f32[32,180,128]{2,1,0:T(8,128)S(1)} %reshape_reshape.3), kind=kLoop, calls=%fused_computation | loop fusion | bytes 6094848 | tf_op jit(solution)/shard_map/slice | solution.py:357
  106.6 1.6 constant_dynamic-slice_fusion.5
  109.1 1.7 collective-permute-start
  113.6 12.0 %custom-call.9 = f32[2,64,64]{2,1,0:T(8,128)S(1)} custom-call(f32[2,64,64]{2,1,0:T(8,128)S(1)} %fusion.43), custom_call_target="Cholesky" | custom-call | tf_op jit(solution)/shard_map/jit(cholesky)/cholesky | solution.py:244
  125.8 9.8 %custom-call.10 = f32[2,1,64,64]{2,3,1,0:T(8,128)S(1)} custom-call(f32[2,1,64,64]{3,2,1,0:T(8,128)S(1)} %select_bitcast_fusion), custom_call_target="InvertDiagBlocksLowerTriangular" | custom-call | tf_op jit(solution)/shard_map/triangular_solve | solution.py:247
  139.6 13.5 %shard_map.70 = (f32[4,16,24,128]{3,2,1,0:T(8,128)S(1)}, f32[2,16,24,128]{3,2,1,0:T(8,128)S(1)}) custom-call(f32[4,16,24,128]{3,2,1,0:T(8,128)S(1)} %fusion.21.refs_0_, f32[2,16,24,128]{3,2,1,0:T(8,128)S(1)} %fusion.36.refs_1_), custom_call_target="tpu_custom_call" | custom-call | tf_op jit(solution)/shard_map/pallas_call | solution.py:76
  153.2 13.3 %shard_map.71 = f32[32,24,128]{2,1,0:T(8,128)S(1)} custom-call(f32[32,24,128]{2,1,0:T(8,128)S(1)} %pad_maximum_fusion.2.refs_0_), custom_call_target="tpu_custom_call" | custom-call | tf_op jit(solution)/shard_map/pallas_call | solution.py:76
  166.6 9.9 %shard_map.72 = f32[8,24,128]{2,1,0:T(8,128)S(1)} custom-call(f32[24,128]{1,0:T(8,128)S(1)} %reduce_sum.29.refs_0_), custom_call_target="tpu_custom_call" | custom-call | tf_op jit(solution)/shard_map/pallas_call | solution.py:76
  (117 shorter events, 37.1 us)
Async XLA Ops:
  2.1 2.0 %copy-start.8 = (bf16[1,16,16,640]{3,2,1,0:T(8,128)(2,1)S(1)}, bf16[1,16,16,640]{3,2,1,0:T(8,128)(2,1)}, u32[]{:S(2)}) copy-start(bf16[1,16,16,640]{3,2,1,0:T(8,128)(2,1)} %param.6) | copy-start | bytes 983044
  23.5 6.3 %copy-start.1 = (f32[5760,2,64]{0,2,1:T(8,128)S(1)}, f32[5760,2,64]{0,2,1:T(8,128)}, u32[]{:S(2)}) copy-start(f32[5760,2,64]{0,2,1:T(8,128)} %param.9) | copy-start | bytes 8847364
  35.2 1.0 copy-start.9
  39.8 4.0 %slice-start = ((s8[7372800]{0:T(1024)(128)(4,1)}), s8[3178496]{0:T(1024)(128)(4,1)S(1)}, s32[]{:S(2)}) async-start(s8[7372800]{0:T(1024)(128)(4,1)} %bitcast.233), calls=%async_computation | async-start | bytes 6356992
  40.1 1.3 copy-start.4
  40.1 3.7 %slice-start.1 = ((s8[7372800]{0:T(1024)(128)(4,1)}), s8[4194304]{0:T(1024)(128)(4,1)S(1)}, s32[]{:S(2)}) async-start(s8[7372800]{0:T(1024)(128)(4,1)} %bitcast.233), calls=%async_computation.1 | async-start | bytes 8388608
  40.6 2.7 %copy-start.6 = (bf16[324,640]{1,0:T(8,128)(2,1)S(1)}, bf16[324,640]{1,0:T(8,128)(2,1)}, u32[]{:S(2)}) copy-start(bf16[324,640]{1,0:T(8,128)(2,1)} %reshape_squeeze.6) | copy-start | bytes 1244164
  40.6 2.7 %copy-start.10 = (f32[324,64]{1,0:T(8,128)S(1)}, f32[324,64]{1,0:T(8,128)}, u32[]{:S(2)}) copy-start(f32[324,64]{1,0:T(8,128)} %reshape.241) | copy-start | bytes 248836
  46.6 1.1 copy-start.3
  86.7 2.9 %copy-start.2 = (f32[640,2,64]{2,1,0:T(2,128)}, f32[640,2,64]{2,1,0:T(2,128)S(1)}, u32[]{:S(2)}) copy-start(f32[640,2,64]{2,1,0:T(2,128)S(1)} %reshape.243) | copy-start | bytes 983044
  87.5 2.3 %copy-start.5 = (bf16[18,18,640]{2,1,0:T(8,128)(2,1)S(1)}, bf16[18,18,640]{2,1,0:T(8,128)(2,1)}, u32[]{:S(2)}) copy-start(bf16[18,18,640]{2,1,0:T(8,128)(2,1)} %get-tuple-element.18) | copy-start | bytes 1244164
  94.6 2.0 %copy-start.7 = (bf16[1,16,16,640]{3,2,1,0:T(8,128)(2,1)S(1)}, bf16[1,16,16,640]{3,2,1,0:T(8,128)(2,1)}, u32[]{:S(2)}) copy-start(bf16[1,16,16,640]{3,2,1,0:T(8,128)(2,1)} %fusion.25) | copy-start | bytes 983044
  106.6 4.3 %copy-start = (f32[16,192,128]{2,1,0:T(8,128)S(1)}, f32[16,192,128]{2,1,0:T(8,128)}, u32[]{:S(2)}) copy-start(f32[16,192,128]{2,1,0:T(8,128)} %get-tuple-element.22) | copy-start | bytes 4718596
  109.1 29.3 %collective-permute-start = (f32[4,16,24,128]{3,2,1,0:T(8,128)}, f32[4,16,24,128]{3,2,1,0:T(8,128)}, u32[]{:S(2)}, u32[]{:S(2)}) collective-permute-start(f32[4,16,24,128]{3,2,1,0:T(8,128)} %bitcast.224), channel_id=1, source_target_pairs={{0,4},{4,0},{1,5},{5,1},{2,6},{6,2},{3,7},{7,3},{8,12},{12,8},{9,1... | collective-permute-start | bytes 2359304 | tf_op jit(solution)/shard_map/ppermute | solution.py:342
  111.1 26.1 %collective-permute-start.3 = (f32[2,16,24,128]{3,2,1,0:T(8,128)S(1)}, f32[2,16,24,128]{3,2,1,0:T(8,128)S(1)}, u32[]{:S(2)}, u32[]{:S(2)}) collective-permute-start(f32[2,16,24,128]{3,2,1,0:T(8,128)S(1)} %bitcast.265), channel_id=1, source_target_pairs={{0,3},{1,0},{2,1},{3,2},{4,7},{5,4},{6,5},{7,6},{8,11},{9,8},{10,9... | collective-permute-start | bytes 1179656 | tf_op jit(solution)/shard_map/ppermute | solution.py:342
  111.6 25.6 %collective-permute-start.2 = (f32[2,16,24,128]{3,2,1,0:T(8,128)S(1)}, f32[2,16,24,128]{3,2,1,0:T(8,128)}, u32[]{:S(2)}, u32[]{:S(2)}) collective-permute-start(f32[2,16,24,128]{3,2,1,0:T(8,128)S(1)} %bitcast.266), channel_id=1, source_target_pairs={{0,2},{1,3},{2,0},{3,1},{4,6},{5,7},{6,4},{7,5},{8,10},{9,11},{10,... | collective-permute-start | bytes 1179656 | tf_op jit(solution)/shard_map/ppermute | solution.py:342
  112.6 24.6 %collective-permute-start.1 = (f32[2,16,24,128]{3,2,1,0:T(8,128)S(1)}, f32[2,16,24,128]{3,2,1,0:T(8,128)}, u32[]{:S(2)}, u32[]{:S(2)}) collective-permute-start(f32[2,16,24,128]{3,2,1,0:T(8,128)S(1)} %bitcast.267), channel_id=1, source_target_pairs={{0,1},{1,2},{2,3},{3,0},{4,5},{5,6},{6,7},{7,4},{8,9},{9,10},{10,1... | collective-permute-start | bytes 1179656 | tf_op jit(solution)/shard_map/ppermute | solution.py:342

commit v11 on v10

--- a/solution.py
+++ b/solution.py
@@ -148,10 +148,13 @@
     top_right = jnp.where(up & right, corners_in[1], zero)
     bottom_left = jnp.where(down & left, corners_in[2], zero)
     bottom_right = jnp.where(down & right, corners_in[3], zero)
-    first = jnp.concatenate([top_left[:, None], top, top_right[:, None]], axis=1)
-    middle = jnp.concatenate([west[:, :, None], tiles, east[:, :, None]], axis=2)
-    last = jnp.concatenate([bottom_left[:, None], bottom, bottom_right[:, None]], axis=1)
-    return jnp.concatenate([first[:, None], middle, last[:, None]], axis=1)
+    padded = []
+    for k in range(tiles.shape[0]):
+        first = jnp.concatenate([top_left[k, None], top[k], top_right[k, None]], axis=0)
+        middle = jnp.concatenate([west[k, :, None], tiles[k], east[k, :, None]], axis=1)
+        last = jnp.concatenate([bottom_left[k, None], bottom[k], bottom_right[k, None]], axis=0)
+        padded.append(jnp.concatenate([first[None], middle, last[None]], axis=0))
+    return padded
 
 
 def silu_slope(pre_float):
@@ -182,7 +185,7 @@
     both_pad = padded_pair(
         jnp.stack([out_grad.reshape(height, breadth, channels), x_input.reshape(height, breadth, channels)]), sizes
     )
-    grad_pad, input_pad = both_pad[0], both_pad[1]
+    grad_pad, input_pad = both_pad
     back_grad = jnp.zeros((pixels, channels), jnp.float32)
     for a, b in TAPS:
         window = grad_pad[1 - a : 1 - a + height, 1 - b : 1 - b + breadth].reshape(pixels, channels)

time: 178 us -> 174 us (0.978)
  local copies, waits for them, and re-layouts: 46.2 us -> 39.3 us
    slice x1 -> x2, local copies, waits for them, and re-layouts: 5.33 us -> 0.02 us  [the longest x1 0.01 us: padded_pair(): bottom_right[k, None]]
    pallas_call x2 -> x0, local copies, waits for them, and re-layouts: 1.9 us -> none  [padded_pair(): pl.pallas_call(functools.partial(halo_kernel, sizes=sizes), out_shape=tup...]
    unnamed x34 -> x57, local copies, waits for them, and re-layouts: 7.34 us -> 7.73 us
  transfers between devices with their start and end apart: 4 -> 4, of which waited for: 0 -> 0; matrix products, arithmetic and copies ran while one was open for 14% -> 15% of each run, Pallas kernels for 0% -> 0%
where the time goes in v11:
time: 174 us; the launch traced here: 173 us
  Pallas kernels  81.8 us (47%)
  local copies, waits for them, and re-layouts  39.3 us (23%)
  other arithmetic  31.7 us (18%)
  matrix products  14.3 us (8%)
  starting transfers between devices  4.33 us (2%)
    pallas_call x3, Pallas kernels, exchange_many(): pl.pallas_call(functools.partial(exchange_kernel, jobs=tuple(jobs), sizes...  36.8 us
    pallas_call x1, Pallas kernels, all_sum_small(): pl.pallas_call(functools.partial(allsum_kernel, sizes=sizes), out_shape=j...  35.2 us
    another operation x4, other arithmetic, on_device(): lower = jnp.linalg.cholesky(gram)  12.2 us
    another operation x3, other arithmetic, on_device(): lax.linalg.triangular_solve(lower, raw_part.transpose(1, 0, 2), left_side...  9.92 us
    pallas_call x1, Pallas kernels, padded_pair(): pl.pallas_call(functools.partial(halo_kernel, sizes=sizes), out_shape=tup...  9.81 us
    dot_general x8, matrix products, exact_dot(): lax.dot_general(left.astype(jnp.float32), right.astype(jnp.float32), (con...  8.51 us
    unnamed x57, local copies, waits for them, and re-layouts  7.73 us
    ppermute x4, starting transfers between devices, permute_sum(): lax.ppermute(slab, axis, [(i, (i + shift) % n) for i in range(n)])  4.33 us
  transfers between devices with their start and end apart: 4, of which 0 were waited for; matrix products, arithmetic and copies ran while one was open for 15% of the time, Pallas kernels for 0%

profile of v11, /device:TPU:1, one launch (start us, length us, event | category | flops | bytes accessed | tf_op | source)
XLA Modules:
  0.0 172.8 jit_solution(11967109807541639040)
XLA Ops:
  0.6 1.5 copy.66
  2.1 1.5 copy.65
  6.8 2.6 %reshape.201 = f32[9,640,2,64]{1,0,3,2:T(8,128)} reshape(f32[5760,2,64]{0,2,1:T(8,128)S(1)} %copy-done.3) | data formatting | bytes 5898240 | tf_op jit(solution)/shard_map/reshape | solution.py:200
  9.4 2.9 %fusion.64 = (f32[1,640,9,64]{1,2,3,0:T(8,128)S(1)}, f32[1,640,9,64]{1,2,3,0:T(8,128)S(1)}) fusion(f32[2,640,9,64]{1,2,3,0:T(8,128)} %bitcast.240), kind=kLoop, calls=%fused_computation.161 | loop fusion | bytes 5898240 | tf_op jit(solution)/shard_map/slice | solution.py:202
  12.7 1.3 fusion.34
  17.3 9.8 %shard_map.68 = (bf16[2,2,16,640]{3,2,1,0:T(8,128)(2,1)}, bf16[2,2,16,640]{3,2,1,0:T(8,128)(2,1)}, bf16[4,2,640]{2,1,0:T(2,128)(2,1)}) custom-call(bf16[2,2,16,640]{3,2,1,0:T(8,128)(2,1)} %copy.68.refs_0_, bf16[2,2,16,640]{3,2,1,0:T(8,128)(2,1)} %copy.69.refs_1_, bf16[4,2,640]{2,1,0:T(2,128)(2,1)} %pad_maximum_fusion.10.refs_2_), custom_call_target="tpu_custom_call" | custom-call | tf_op jit(solution)/shard_map/pallas_call | solution.py:130
  32.1 1.8 %fusion.63 = f32[18,18,576]{2,1,0:T(8,128)S(1)} fusion(f32[640,576,1]{0,1,2:T(8,128)S(1)} %bitcast.255, bf16[1,18,640]{2,1,0:T(8,128)(2,1)S(1)} %maximum_bitcast_fusion.7, bf16[16,1,640]{2,1,0:T(2,128)(2,1)S(1)} %copy.75, bf16[16,16,640]{2,1,0:T(8,128)(2,1)S(1)} %bitcast.261, bf16[16,1,640]{2,1,0:T(2,128)(2,1)S(1)} %copy.74, ...), kind=kOutput, calls=%fused_computation.160 | convolution fusion | flops 1435345920 | bytes 2635776 | tf_op jit(solution)/shard_map/dot_general | solution.py:166
  40.9 1.5 reshape.203.p_ref
  42.4 35.2 %shard_map.69 = f32[8,32,320]{2,1,0:T(8,128)} custom-call(f32[8,32,320]{2,1,0:T(8,128)} %reshape.203.p_ref), custom_call_target="tpu_custom_call" | custom-call | tf_op jit(solution)/shard_map/pallas_call | solution.py:319
  77.5 1.4 reshape.204
  86.2 1.9 %concatenate.64 = f32[324,576]{1,0:T(8,128)S(1)} concatenate(f32[324,64]{1,0:T(8,128)S(1)} %reshape.206, f32[324,64]{1,0:T(8,128)S(1)} %copy-done.11, f32[324,64]{1,0:T(8,128)S(1)} %copy-done.12, f32[324,64]{1,0:T(8,128)S(1)} %copy-done.13, f32[324,64]{1,0:T(8,128)} %reshape.210, f32[324,64]{1,0:T(8,128)} %reshape.211, f32[324,64]{1,0:T(8,128)S(1)} %reshape.212, ...), dimensions={1} | concatenate | bytes 1492992 | tf_op jit(solution)/shard_map/concatenate | solution.py:218
  88.4 1.9 %convolution_bitcast_fusion = f32[9,640,64]{1,2,0:T(8,128)S(1)} fusion(bf16[256,640,1]{1,0,2:T(8,128)(2,1)} %bitcast.257, f32[9,64,256]{2,1,0:T(8,128)S(1)} %bitcast.254), kind=kOutput, calls=%fused_computation.3 | convolution fusion | flops 1132462080 | bytes 2392064 | tf_op jit(solution)/shard_map/dot_general | solution.py:166
  90.4 1.5 convolution_bitcast_fusion.1
  92.1 2.8 %copy.88 = f32[9,640,128]{2,1,0:T(8,128)} copy(f32[9,640,128]{1,2,0:T(8,128)S(1)} %pad_maximum_fusion) | data formatting | bytes 5898240 | tf_op jit(solution)/shard_map/concatenate | solution.py:235
  94.8 2.6 %reshape_reshape.3 = f32[32,180,128]{2,1,0:T(8,128)S(1)} reshape(f32[9,640,128]{2,1,0:T(8,128)} %copy.88) | data formatting | bytes 5898240 | tf_op jit(solution)/shard_map/reshape;reshape | solution.py:356
  97.4 2.0 %pad_slice_fusion = (f32[16,192,128]{2,1,0:T(8,128)}, f32[16,192,128]{2,1,0:T(8,128)}) fusion(f32[32,180,128]{2,1,0:T(8,128)S(1)} %reshape_reshape.3), kind=kLoop, calls=%fused_computation | loop fusion | bytes 6094848 | tf_op jit(solution)/shard_map/slice | solution.py:360
  99.4 2.4 %constant_dynamic-slice_fusion.5 = (f32[16,1,4,24,128]{4,3,2,1,0:T(8,128)}, f32[16,1,4,24,128]{4,3,2,1,0:T(8,128)S(1)}) fusion(f32[16,2,4,24,128]{4,3,2,1,0:T(8,128)} %bitcast.243, s32[]{:T(128)S(6)} %select_n.105, s32[]{:T(128)S(6)} %select_n.106), kind=kLoop, calls=%fused_computation.155 | loop fusion | bytes 3145736 | tf_op jit(solution)/shard_map/dynamic-slice
  102.7 1.7 %collective-permute-start = (f32[4,16,24,128]{3,2,1,0:T(8,128)}, f32[4,16,24,128]{3,2,1,0:T(8,128)}, u32[]{:S(2)}, u32[]{:S(2)}) collective-permute-start(f32[4,16,24,128]{3,2,1,0:T(8,128)} %bitcast.235), channel_id=1, source_target_pairs={{0,4},{4,0},{1,5},{5,1},{2,6},{6,2},{3,7},{7,3},{8,12},{12,8},{9,1... | collective-permute-start | bytes 2359304 | tf_op jit(solution)/shard_map/ppermute | solution.py:345
  105.4 1.3 collective-permute-start.3
  108.7 12.0 %custom-call.9 = f32[2,64,64]{2,1,0:T(8,128)S(1)} custom-call(f32[2,64,64]{2,1,0:T(8,128)S(1)} %fusion.57), custom_call_target="Cholesky" | custom-call | tf_op jit(solution)/shard_map/jit(cholesky)/cholesky | solution.py:247
  120.9 9.8 %custom-call.10 = f32[2,1,64,64]{2,3,1,0:T(8,128)S(1)} custom-call(f32[2,1,64,64]{3,2,1,0:T(8,128)S(1)} %select_bitcast_fusion), custom_call_target="InvertDiagBlocksLowerTriangular" | custom-call | tf_op jit(solution)/shard_map/triangular_solve | solution.py:250
  134.8 13.7 %shard_map.70 = (f32[4,16,24,128]{3,2,1,0:T(8,128)S(1)}, f32[2,16,24,128]{3,2,1,0:T(8,128)S(1)}) custom-call(f32[4,16,24,128]{3,2,1,0:T(8,128)S(1)} %fusion.21.refs_0_, f32[2,16,24,128]{3,2,1,0:T(8,128)S(1)} %fusion.33.refs_1_), custom_call_target="tpu_custom_call" | custom-call | tf_op jit(solution)/shard_map/pallas_call | solution.py:76
  148.6 14.6 %shard_map.71 = f32[32,24,128]{2,1,0:T(8,128)S(1)} custom-call(f32[32,24,128]{2,1,0:T(8,128)S(1)} %pad_maximum_fusion.4.refs_0_), custom_call_target="tpu_custom_call" | custom-call | tf_op jit(solution)/shard_map/pallas_call | solution.py:76
  163.2 8.5 %shard_map.72 = f32[8,24,128]{2,1,0:T(8,128)S(1)} custom-call(f32[24,128]{1,0:T(8,128)S(1)} %reduce_sum.29.refs_0_), custom_call_target="tpu_custom_call" | custom-call | tf_op jit(solution)/shard_map/pallas_call | solution.py:76
  (149 shorter events, 35.4 us)
Async XLA Ops:
  4.0 2.8 %copy-start.3 = (f32[5760,2,64]{0,2,1:T(8,128)S(1)}, f32[5760,2,64]{0,2,1:T(8,128)}, u32[]{:S(2)}) copy-start(f32[5760,2,64]{0,2,1:T(8,128)} %param.9) | copy-start | bytes 8847364
  15.1 13.8 %copy-start.1 = (bf16[1,16,16,640]{3,2,1,0:T(8,128)(2,1)S(1)}, bf16[1,16,16,640]{3,2,1,0:T(8,128)(2,1)}, u32[]{:S(2)}) copy-start(bf16[1,16,16,640]{3,2,1,0:T(8,128)(2,1)} %param.7) | copy-start | bytes 983044
  29.5 4.6 %slice-start = ((s8[7372800]{0:T(1024)(128)(4,1)}), s8[4194304]{0:T(1024)(128)(4,1)S(1)}, s32[]{:S(2)}) async-start(s8[7372800]{0:T(1024)(128)(4,1)} %bitcast.241), calls=%async_computation | async-start | bytes 8388608
  29.9 1.2 copy-start.10
  29.9 4.2 %slice-start.1 = ((s8[7372800]{0:T(1024)(128)(4,1)}), s8[3178496]{0:T(1024)(128)(4,1)S(1)}, s32[]{:S(2)}) async-start(s8[7372800]{0:T(1024)(128)(4,1)} %bitcast.241), calls=%async_computation.1 | async-start | bytes 6356992
  37.4 1.1 copy-start.5
  38.5 1.0 copy-start.16
  38.5 1.1 copy-start.17
  38.5 1.2 copy-start.18
  38.5 1.2 copy-start.19
  38.6 1.2 copy-start.20
  38.6 1.2 copy-start.21
  38.6 1.3 copy-start.22
  79.9 1.1 copy-start.6
  83.9 2.1 %copy-start.11 = (f32[324,64]{1,0:T(8,128)S(1)}, f32[324,64]{1,0:T(8,128)}, u32[]{:S(2)}) copy-start(f32[324,64]{1,0:T(8,128)} %reshape.207) | copy-start | bytes 248836
  84.6 1.5 copy-start.12
  88.4 1.9 %copy-start.7 = (bf16[324,640,1]{1,0,2:T(8,128)(2,1)S(1)}, bf16[324,640,1]{1,0,2:T(8,128)(2,1)}, u32[]{:S(2)}) copy-start(bf16[324,640,1]{1,0,2:T(8,128)(2,1)} %reshape.231) | copy-start | bytes 1244164
  101.8 2.7 %copy-start = (f32[16,192,128]{2,1,0:T(8,128)S(1)}, f32[16,192,128]{2,1,0:T(8,128)}, u32[]{:S(2)}) copy-start(f32[16,192,128]{2,1,0:T(8,128)} %get-tuple-element.20) | copy-start | bytes 4718596
  102.7 30.8 %collective-permute-start = (f32[4,16,24,128]{3,2,1,0:T(8,128)}, f32[4,16,24,128]{3,2,1,0:T(8,128)}, u32[]{:S(2)}, u32[]{:S(2)}) collective-permute-start(f32[4,16,24,128]{3,2,1,0:T(8,128)} %bitcast.235), channel_id=1, source_target_pairs={{0,4},{4,0},{1,5},{5,1},{2,6},{6,2},{3,7},{7,3},{8,12},{12,8},{9,1... | collective-permute-start | bytes 2359304 | tf_op jit(solution)/shard_map/ppermute | solution.py:345
  105.4 26.9 %collective-permute-start.3 = (f32[2,16,24,128]{3,2,1,0:T(8,128)S(1)}, f32[2,16,24,128]{3,2,1,0:T(8,128)}, u32[]{:S(2)}, u32[]{:S(2)}) collective-permute-start(f32[2,16,24,128]{3,2,1,0:T(8,128)S(1)} %bitcast.279), channel_id=1, source_target_pairs={{0,3},{1,0},{2,1},{3,2},{4,7},{5,4},{6,5},{7,6},{8,11},{9,8},{10,9... | collective-permute-start | bytes 1179656 | tf_op jit(solution)/shard_map/ppermute | solution.py:345
  106.7 25.6 %copy-start.8 = (f32[16,2,1,24,128]{4,3,2,1,0:T(8,128)S(1)}, f32[16,2,1,24,128]{4,3,2,1,0:T(8,128)}, u32[]{:S(2)}) copy-start(f32[16,2,1,24,128]{4,3,2,1,0:T(8,128)} %get-tuple-element.22) | copy-start | bytes 1179652
  106.7 25.6 %collective-permute-start.2 = (f32[2,16,24,128]{3,2,1,0:T(8,128)S(1)}, f32[2,16,24,128]{3,2,1,0:T(8,128)}, u32[]{:S(2)}, u32[]{:S(2)}) collective-permute-start(f32[2,16,24,128]{3,2,1,0:T(8,128)S(1)} %bitcast.280), channel_id=1, source_target_pairs={{0,2},{1,3},{2,0},{3,1},{4,6},{5,7},{6,4},{7,5},{8,10},{9,11},{10,... | collective-permute-start | bytes 1179656 | tf_op jit(solution)/shard_map/ppermute | solution.py:345
  107.2 25.1 %collective-permute-start.1 = (f32[2,16,24,128]{3,2,1,0:T(8,128)S(1)}, f32[2,16,24,128]{3,2,1,0:T(8,128)S(1)}, u32[]{:S(2)}, u32[]{:S(2)}) collective-permute-start(f32[2,16,24,128]{3,2,1,0:T(8,128)S(1)} %bitcast.281), channel_id=1, source_target_pairs={{0,1},{1,2},{2,3},{3,0},{4,5},{5,6},{6,7},{7,4},{8,9},{9,10},{10,1... | collective-permute-start | bytes 1179656 | tf_op jit(solution)/shard_map/ppermute | solution.py:345
  108.5 25.0 %copy-start.2 = (f32[16,1,4,24,128]{4,3,2,1,0:T(8,128)S(1)}, f32[16,1,4,24,128]{4,3,2,1,0:T(8,128)}, u32[]{:S(2)}) copy-start(f32[16,1,4,24,128]{4,3,2,1,0:T(8,128)} %get-tuple-element.26) | copy-start | bytes 2359300
  (5 other events, 4.7 us)

commit v12 on v11

--- a/solution.py
+++ b/solution.py
@@ -355,7 +355,7 @@
     lanes = math.prod(shape[1:])
     padded = jnp.pad(value.reshape(blocks, block_rows, lanes), ((0, 0), (0, piece_rows * group - block_rows), (0, 0)))
     pieces = padded.reshape(blocks, rows_n, cols_n, piece_rows, lanes)
-    half = blocks // 2
+    half = blocks * 3 // 8
     first = pieces[:half].transpose(1, 2, 0, 3, 4)
     second = pieces[half:].transpose(2, 1, 0, 3, 4)
     first, second = permute_sum(first, "row", sizes), permute_sum(second, "col", sizes)

time: 174 us -> 166 us (0.954)
  other arithmetic: 31.7 us -> 29.6 us
  Pallas kernels: 81.8 us -> 79.7 us
    reshape x9, local copies, waits for them, and re-layouts: 3.51 us -> 0.15 us  [on_device(): jnp.pad(first_image, ((1 + a, 1 - a), (1 + b, 1 - b), (0, 0)))]
    pallas_call x3, Pallas kernels: 36.8 us -> 34.7 us  [exchange_many(): pl.pallas_call(functools.partial(exchange_kernel, jobs=tuple(jobs), sizes...]
    unnamed x57 -> x51, local copies, waits for them, and re-layouts: 7.73 us -> 8.55 us
  transfers between devices with their start and end apart: 4 -> 4, of which waited for: 0 -> 0; matrix products, arithmetic and copies ran while one was open for 15% -> 18% of each run, Pallas kernels for 0% -> 0%
where the time goes in v12:
time: 166 us; the launch traced here: 165 us
  Pallas kernels  79.7 us (48%)
  local copies, waits for them, and re-layouts  37.8 us (23%)
  other arithmetic  29.6 us (18%)
  matrix products  13.3 us (8%)
  starting transfers between devices  3.4 us (2%)
    pallas_call x1, Pallas kernels, all_sum_small(): pl.pallas_call(functools.partial(allsum_kernel, sizes=sizes), out_shape=j...  35.1 us
    pallas_call x3, Pallas kernels, exchange_many(): pl.pallas_call(functools.partial(exchange_kernel, jobs=tuple(jobs), sizes...  34.7 us
    another operation x4, other arithmetic, on_device(): lower = jnp.linalg.cholesky(gram)  12.2 us
    another operation x3, other arithmetic, on_device(): lax.linalg.triangular_solve(lower, raw_part.transpose(1, 0, 2), left_side...  9.92 us
    pallas_call x1, Pallas kernels, padded_pair(): pl.pallas_call(functools.partial(halo_kernel, sizes=sizes), out_shape=tup...  9.81 us
    unnamed x51, local copies, waits for them, and re-layouts  8.55 us
    dot_general x8, matrix products, exact_dot(): lax.dot_general(left.astype(jnp.float32), right.astype(jnp.float32), (con...  7.47 us
    dot_general x9, matrix products, on_device(): lax.dot_general(window, conv_weight[a + 1, b + 1], (((1,), (1,)), ((), ()...  4.2 us
  transfers between devices with their start and end apart: 4, of which 0 were waited for; matrix products, arithmetic and copies ran while one was open for 18% of the time, Pallas kernels for 0%

profile of v12, /device:TPU:1, one launch (start us, length us, event | category | flops | bytes accessed | tf_op | source)
XLA Modules:
  0.0 165.3 jit_solution(16294519038584299890)
XLA Ops:
  0.6 1.5 copy.66
  2.1 1.5 copy.65
  6.8 2.6 %reshape.201 = f32[9,640,2,64]{1,0,3,2:T(8,128)} reshape(f32[5760,2,64]{0,2,1:T(8,128)S(1)} %copy-done.3) | data formatting | bytes 5898240 | tf_op jit(solution)/shard_map/reshape | solution.py:200
  9.3 2.9 %fusion.64 = (f32[1,640,9,64]{1,2,3,0:T(8,128)S(1)}, f32[1,640,9,64]{1,2,3,0:T(8,128)S(1)}) fusion(f32[2,640,9,64]{1,2,3,0:T(8,128)} %bitcast.240), kind=kLoop, calls=%fused_computation.161 | loop fusion | bytes 5898240 | tf_op jit(solution)/shard_map/slice | solution.py:202
  12.7 1.3 fusion.34
  17.2 9.8 %shard_map.68 = (bf16[2,2,16,640]{3,2,1,0:T(8,128)(2,1)}, bf16[2,2,16,640]{3,2,1,0:T(8,128)(2,1)}, bf16[4,2,640]{2,1,0:T(2,128)(2,1)}) custom-call(bf16[2,2,16,640]{3,2,1,0:T(8,128)(2,1)} %copy.68.refs_0_, bf16[2,2,16,640]{3,2,1,0:T(8,128)(2,1)} %copy.69.refs_1_, bf16[4,2,640]{2,1,0:T(2,128)(2,1)} %pad_maximum_fusion.10.refs_2_), custom_call_target="tpu_custom_call" | custom-call | tf_op jit(solution)/shard_map/pallas_call | solution.py:130
  31.2 1.8 %fusion.63 = f32[18,18,576]{2,1,0:T(8,128)S(1)} fusion(f32[640,576,1]{0,1,2:T(8,128)S(1)} %bitcast.255, bf16[1,18,640]{2,1,0:T(8,128)(2,1)S(1)} %maximum_bitcast_fusion.7, bf16[16,1,640]{2,1,0:T(2,128)(2,1)S(1)} %copy.75, bf16[16,16,640]{2,1,0:T(8,128)(2,1)S(1)} %bitcast.261, bf16[16,1,640]{2,1,0:T(2,128)(2,1)S(1)} %copy.74, ...), kind=kOutput, calls=%fused_computation.160 | convolution fusion | flops 1435345920 | bytes 2635776 | tf_op jit(solution)/shard_map/dot_general | solution.py:166
  40.0 1.5 reshape.203.p_ref
  41.5 35.1 %shard_map.69 = f32[8,32,320]{2,1,0:T(8,128)} custom-call(f32[8,32,320]{2,1,0:T(8,128)} %reshape.203.p_ref), custom_call_target="tpu_custom_call" | custom-call | tf_op jit(solution)/shard_map/pallas_call | solution.py:319
  76.7 1.4 reshape.204
  81.2 1.9 %concatenate.64 = f32[324,576]{1,0:T(8,128)S(1)} concatenate(f32[324,64]{1,0:T(8,128)S(1)} %reshape.206, f32[324,64]{1,0:T(8,128)S(1)} %reshape.207, f32[324,64]{1,0:T(8,128)S(1)} %reshape.208, f32[324,64]{1,0:T(8,128)S(1)} %reshape.209, f32[324,64]{1,0:T(8,128)S(1)} %reshape.210, f32[324,64]{1,0:T(8,128)S(1)} %reshape.211, f32[324,64]{1,0:T(8,128)S(1)} %reshape.212, ...), dimensions={1} | concatenate | bytes 1492992 | tf_op jit(solution)/shard_map/concatenate | solution.py:218
  84.4 1.4 convolution_bitcast_fusion.1
  86.1 2.8 %copy.88 = f32[9,640,128]{2,1,0:T(8,128)} copy(f32[9,640,128]{1,2,0:T(8,128)S(1)} %pad_maximum_fusion) | data formatting | bytes 5898240 | tf_op jit(solution)/shard_map/concatenate | solution.py:235
  88.9 2.6 %reshape_reshape.3 = f32[32,180,128]{2,1,0:T(8,128)S(1)} reshape(f32[9,640,128]{2,1,0:T(8,128)} %copy.88) | data formatting | bytes 5898240 | tf_op jit(solution)/shard_map/reshape;reshape | solution.py:356
  91.4 1.1 pad_slice_fusion.1
  92.6 2.2 %constant_dynamic-slice_fusion.5 = (f32[12,1,4,24,128]{4,3,2,1,0:T(8,128)}, f32[12,1,4,24,128]{4,3,2,1,0:T(8,128)S(1)}) fusion(f32[12,2,4,24,128]{4,3,2,1,0:T(8,128)} %bitcast.249, s32[]{:T(128)S(6)} %select_n.105, s32[]{:T(128)S(6)} %select_n.106), kind=kLoop, calls=%fused_computation.155 | loop fusion | bytes 2359304 | tf_op jit(solution)/shard_map/dynamic-slice
  95.6 1.7 %collective-permute-start = (f32[4,12,24,128]{3,2,1,0:T(8,128)}, f32[4,12,24,128]{3,2,1,0:T(8,128)}, u32[]{:S(2)}, u32[]{:S(2)}) collective-permute-start(f32[4,12,24,128]{3,2,1,0:T(8,128)} %bitcast.235), channel_id=1, source_target_pairs={{0,4},{4,0},{1,5},{5,1},{2,6},{6,2},{3,7},{7,3},{8,12},{12,8},{9,1... | collective-permute-start | bytes 1769480 | tf_op jit(solution)/shard_map/ppermute | solution.py:345
  97.3 1.5 pad_slice_fusion
  98.8 1.6 constant_dynamic-slice_fusion.3
  104.4 12.0 %custom-call.9 = f32[2,64,64]{2,1,0:T(8,128)S(1)} custom-call(f32[2,64,64]{2,1,0:T(8,128)S(1)} %fusion.57), custom_call_target="Cholesky" | custom-call | tf_op jit(solution)/shard_map/jit(cholesky)/cholesky | solution.py:247
  116.7 9.8 %custom-call.10 = f32[2,1,64,64]{2,3,1,0:T(8,128)S(1)} custom-call(f32[2,1,64,64]{3,2,1,0:T(8,128)S(1)} %select_bitcast_fusion), custom_call_target="InvertDiagBlocksLowerTriangular" | custom-call | tf_op jit(solution)/shard_map/triangular_solve | solution.py:250
  129.3 11.4 %shard_map.70 = (f32[4,12,24,128]{3,2,1,0:T(8,128)S(1)}, f32[2,20,24,128]{3,2,1,0:T(8,128)S(1)}) custom-call(f32[4,12,24,128]{3,2,1,0:T(8,128)S(1)} %fusion.30.refs_0_, f32[2,20,24,128]{3,2,1,0:T(8,128)S(1)} %fusion.33.refs_1_), custom_call_target="tpu_custom_call" | custom-call | tf_op jit(solution)/shard_map/pallas_call | solution.py:76
  140.9 13.4 %shard_map.71 = f32[32,24,128]{2,1,0:T(8,128)S(1)} custom-call(f32[32,24,128]{2,1,0:T(8,128)S(1)} %pad_maximum_fusion.4.refs_0_), custom_call_target="tpu_custom_call" | custom-call | tf_op jit(solution)/shard_map/pallas_call | solution.py:76
  154.3 9.9 %shard_map.72 = f32[8,24,128]{2,1,0:T(8,128)S(1)} custom-call(f32[24,128]{1,0:T(8,128)S(1)} %reduce_sum.29.refs_0_), custom_call_target="tpu_custom_call" | custom-call | tf_op jit(solution)/shard_map/pallas_call | solution.py:76
  (144 shorter events, 31.1 us)
Async XLA Ops:
  3.8 1.0 copy-start.9
  4.0 2.8 %copy-start.3 = (f32[5760,2,64]{0,2,1:T(8,128)S(1)}, f32[5760,2,64]{0,2,1:T(8,128)}, u32[]{:S(2)}) copy-start(f32[5760,2,64]{0,2,1:T(8,128)} %param.9) | copy-start | bytes 8847364
  15.1 13.8 %copy-start = (bf16[1,16,16,640]{3,2,1,0:T(8,128)(2,1)S(1)}, bf16[1,16,16,640]{3,2,1,0:T(8,128)(2,1)}, u32[]{:S(2)}) copy-start(bf16[1,16,16,640]{3,2,1,0:T(8,128)(2,1)} %param.7) | copy-start | bytes 983044
  29.5 3.8 %slice-start = ((s8[7372800]{0:T(1024)(128)(4,1)}), s8[4194304]{0:T(1024)(128)(4,1)S(1)}, s32[]{:S(2)}) async-start(s8[7372800]{0:T(1024)(128)(4,1)} %bitcast.242), calls=%async_computation | async-start | bytes 8388608
  29.9 1.2 copy-start.10
  29.9 3.4 %slice-start.1 = ((s8[7372800]{0:T(1024)(128)(4,1)}), s8[3178496]{0:T(1024)(128)(4,1)S(1)}, s32[]{:S(2)}) async-start(s8[7372800]{0:T(1024)(128)(4,1)} %bitcast.242), calls=%async_computation.1 | async-start | bytes 6356992
  36.6 1.1 copy-start.5
  37.7 1.0 copy-start.12
  37.7 1.0 copy-start.13
  37.7 1.1 copy-start.14
  37.7 1.2 copy-start.15
  37.7 1.2 copy-start.16
  37.7 1.2 copy-start.17
  37.7 1.2 copy-start.18
  37.7 1.3 copy-start.19
  78.3 2.1 %copy-start.1 = (f32[640,2,64]{0,2,1:T(8,128)}, f32[640,2,64]{0,2,1:T(8,128)S(1)}, u32[]{:S(2)}) copy-start(f32[640,2,64]{0,2,1:T(8,128)S(1)} %copy.80) | copy-start | bytes 983044
  81.2 2.2 %copy-start.8 = (bf16[1,16,16,640]{3,2,1,0:T(8,128)(2,1)S(1)}, bf16[1,16,16,640]{3,2,1,0:T(8,128)(2,1)}, u32[]{:S(2)}) copy-start(bf16[1,16,16,640]{3,2,1,0:T(8,128)(2,1)} %fusion.24) | copy-start | bytes 983044
  83.4 1.0 copy-start.7
  95.6 32.6 %collective-permute-start = (f32[4,12,24,128]{3,2,1,0:T(8,128)}, f32[4,12,24,128]{3,2,1,0:T(8,128)}, u32[]{:S(2)}, u32[]{:S(2)}) collective-permute-start(f32[4,12,24,128]{3,2,1,0:T(8,128)} %bitcast.235), channel_id=1, source_target_pairs={{0,4},{4,0},{1,5},{5,1},{2,6},{6,2},{3,7},{7,3},{8,12},{12,8},{9,1... | collective-permute-start | bytes 1769480 | tf_op jit(solution)/shard_map/ppermute | solution.py:345
  100.5 3.4 %copy-start.2 = (f32[640,2,64]{0,2,1:T(8,128)S(1)}, f32[640,2,64]{0,2,1:T(8,128)}, u32[]{:S(2)}) copy-start(f32[640,2,64]{0,2,1:T(8,128)} %copy-done.1) | copy-start | bytes 983044
  100.5 27.6 %collective-permute-start.3 = (f32[2,20,24,128]{3,2,1,0:T(8,128)S(1)}, f32[2,20,24,128]{3,2,1,0:T(8,128)S(1)}, u32[]{:S(2)}, u32[]{:S(2)}) collective-permute-start(f32[2,20,24,128]{3,2,1,0:T(8,128)S(1)} %bitcast.279), channel_id=1, source_target_pairs={{0,3},{1,0},{2,1},{3,2},{4,7},{5,4},{6,5},{7,6},{8,11},{9,8},{10,9... | collective-permute-start | bytes 1474568 | tf_op jit(solution)/shard_map/ppermute | solution.py:345
  101.9 26.2 %collective-permute-start.2 = (f32[2,20,24,128]{3,2,1,0:T(8,128)}, f32[2,20,24,128]{3,2,1,0:T(8,128)S(1)}, u32[]{:S(2)}, u32[]{:S(2)}) collective-permute-start(f32[2,20,24,128]{3,2,1,0:T(8,128)} %bitcast.237), channel_id=1, source_target_pairs={{0,2},{1,3},{2,0},{3,1},{4,6},{5,7},{6,4},{7,5},{8,10},{9,11},{10,... | collective-permute-start | bytes 1474568 | tf_op jit(solution)/shard_map/ppermute | solution.py:345
  103.6 24.5 %collective-permute-start.1 = (f32[2,20,24,128]{3,2,1,0:T(8,128)}, f32[2,20,24,128]{3,2,1,0:T(8,128)S(1)}, u32[]{:S(2)}, u32[]{:S(2)}) collective-permute-start(f32[2,20,24,128]{3,2,1,0:T(8,128)} %bitcast.238), channel_id=1, source_target_pairs={{0,1},{1,2},{2,3},{3,0},{4,5},{5,6},{6,7},{7,4},{8,9},{9,10},{10,1... | collective-permute-start | bytes 1474568 | tf_op jit(solution)/shard_map/ppermute | solution.py:345
  104.4 23.8 %copy-start.6 = (f32[12,1,4,24,128]{4,3,2,1,0:T(8,128)S(1)}, f32[12,1,4,24,128]{4,3,2,1,0:T(8,128)}, u32[]{:S(2)}) copy-start(f32[12,1,4,24,128]{4,3,2,1,0:T(8,128)} %get-tuple-element.32) | copy-start | bytes 1769476
  (2 other events, 1.8 us)

commit v13 on v12

--- a/solution.py
+++ b/solution.py
@@ -355,7 +355,7 @@
     lanes = math.prod(shape[1:])
     padded = jnp.pad(value.reshape(blocks, block_rows, lanes), ((0, 0), (0, piece_rows * group - block_rows), (0, 0)))
     pieces = padded.reshape(blocks, rows_n, cols_n, piece_rows, lanes)
-    half = blocks * 3 // 8
+    half = blocks // 4
     first = pieces[:half].transpose(1, 2, 0, 3, 4)
     second = pieces[half:].transpose(2, 1, 0, 3, 4)
     first, second = permute_sum(first, "row", sizes), permute_sum(second, "col", sizes)

time: 166 us -> 171 us (1.030)
  Pallas kernels: 79.7 us -> 76 us
  waiting for transfers between devices: 0.01 us -> 2.94 us
  local copies, waits for them, and re-layouts: 37.8 us -> 40.1 us
  other arithmetic: 29.6 us -> 31.7 us
    pallas_call x3, Pallas kernels: 34.7 us -> 31 us  [exchange_many(): pl.pallas_call(functools.partial(exchange_kernel, jobs=tuple(jobs), sizes...]
    reshape x9, local copies, waits for them, and re-layouts: 0.15 us -> 3.46 us  [on_device(): jnp.pad(first_image, ((1 + a, 1 - a), (1 + b, 1 - b), (0, 0)))]
    ppermute x4, waiting for transfers between devices: 0.01 us -> 2.94 us  [permute_sum(): lax.ppermute(slab, axis, [(i, (i + shift) % n) for i in range(n)])]
    unnamed x51 -> x53, local copies, waits for them, and re-layouts: 8.55 us -> 7.58 us
  transfers between devices with their start and end apart: 4 -> 4, of which waited for: 0 -> 1; matrix products, arithmetic and copies ran while one was open for 18% -> 17% of each run, Pallas kernels for 0% -> 0%
where the time goes in v13:
time: 171 us; the launch traced here: 170 us
  Pallas kernels  76 us (44%)
  local copies, waits for them, and re-layouts  40.1 us (23%)
  other arithmetic  31.7 us (19%)
  matrix products  14.3 us (8%)
  starting transfers between devices  3.57 us (2%)
  waiting for transfers between devices  2.94 us (2%)
    pallas_call x1, Pallas kernels, all_sum_small(): pl.pallas_call(functools.partial(allsum_kernel, sizes=sizes), out_shape=j...  35.2 us
    pallas_call x3, Pallas kernels, exchange_many(): pl.pallas_call(functools.partial(exchange_kernel, jobs=tuple(jobs), sizes...  31 us
    another operation x4, other arithmetic, on_device(): lower = jnp.linalg.cholesky(gram)  12.2 us
    another operation x3, other arithmetic, on_device(): lax.linalg.triangular_solve(lower, raw_part.transpose(1, 0, 2), left_side...  9.92 us
    pallas_call x1, Pallas kernels, padded_pair(): pl.pallas_call(functools.partial(halo_kernel, sizes=sizes), out_shape=tup...  9.81 us
    dot_general x8, matrix products, exact_dot(): lax.dot_general(left.astype(jnp.float32), right.astype(jnp.float32), (con...  8.51 us
    unnamed x53, local copies, waits for them, and re-layouts  7.58 us
    dot_general x9, matrix products, on_device(): lax.dot_general(window, conv_weight[a + 1, b + 1], (((1,), (1,)), ((), ()...  4.19 us
  transfers between devices with their start and end apart: 4, of which 1 were waited for; matrix products, arithmetic and copies ran while one was open for 17% of the time, Pallas kernels for 0%

profile of v13, /device:TPU:1, one launch (start us, length us, event | category | flops | bytes accessed | tf_op | source)
XLA Modules:
  0.0 170.1 jit_solution(4403785497142091748)
XLA Ops:
  0.6 1.5 copy.66
  2.1 1.5 copy.65
  6.8 2.6 %reshape.201 = f32[9,640,2,64]{1,0,3,2:T(8,128)} reshape(f32[5760,2,64]{0,2,1:T(8,128)S(1)} %copy-done.1) | data formatting | bytes 5898240 | tf_op jit(solution)/shard_map/reshape | solution.py:200
  9.3 2.9 %fusion.64 = (f32[1,640,9,64]{1,2,3,0:T(8,128)S(1)}, f32[1,640,9,64]{1,2,3,0:T(8,128)S(1)}) fusion(f32[2,640,9,64]{1,2,3,0:T(8,128)} %bitcast.240), kind=kLoop, calls=%fused_computation.161 | loop fusion | bytes 5898240 | tf_op jit(solution)/shard_map/slice | solution.py:202
  17.2 9.8 %shard_map.68 = (bf16[2,2,16,640]{3,2,1,0:T(8,128)(2,1)}, bf16[2,2,16,640]{3,2,1,0:T(8,128)(2,1)}, bf16[4,2,640]{2,1,0:T(2,128)(2,1)}) custom-call(bf16[2,2,16,640]{3,2,1,0:T(8,128)(2,1)} %copy.68.refs_0_, bf16[2,2,16,640]{3,2,1,0:T(8,128)(2,1)} %copy.69.refs_1_, bf16[4,2,640]{2,1,0:T(2,128)(2,1)} %pad_maximum_fusion.10.refs_2_), custom_call_target="tpu_custom_call" | custom-call | tf_op jit(solution)/shard_map/pallas_call | solution.py:130
  32.0 1.8 %fusion.63 = f32[18,18,576]{2,1,0:T(8,128)S(1)} fusion(f32[640,576,1]{0,1,2:T(8,128)S(1)} %bitcast.255, bf16[1,18,640]{2,1,0:T(8,128)(2,1)S(1)} %maximum_bitcast_fusion.7, bf16[16,1,640]{2,1,0:T(2,128)(2,1)S(1)} %copy.75, bf16[16,16,640]{2,1,0:T(8,128)(2,1)S(1)} %bitcast.261, bf16[16,1,640]{2,1,0:T(2,128)(2,1)S(1)} %copy.74, ...), kind=kOutput, calls=%fused_computation.160 | convolution fusion | flops 1435345920 | bytes 2635776 | tf_op jit(solution)/shard_map/dot_general | solution.py:166
  40.8 1.5 reshape.203.p_ref
  42.3 35.2 %shard_map.69 = f32[8,32,320]{2,1,0:T(8,128)} custom-call(f32[8,32,320]{2,1,0:T(8,128)} %reshape.203.p_ref), custom_call_target="tpu_custom_call" | custom-call | tf_op jit(solution)/shard_map/pallas_call | solution.py:319
  86.1 1.9 %concatenate.64 = f32[324,576]{1,0:T(8,128)S(1)} concatenate(f32[324,64]{1,0:T(8,128)S(1)} %reshape.206, f32[324,64]{1,0:T(8,128)S(1)} %copy-done.9, f32[324,64]{1,0:T(8,128)S(1)} %copy-done.10, f32[324,64]{1,0:T(8,128)S(1)} %copy-done.11, f32[324,64]{1,0:T(8,128)} %reshape.210, f32[324,64]{1,0:T(8,128)} %reshape.211, f32[324,64]{1,0:T(8,128)S(1)} %reshape.212, ...), dimensions={1} | concatenate | bytes 1492992 | tf_op jit(solution)/shard_map/concatenate | solution.py:218
  88.3 1.9 %convolution_bitcast_fusion = f32[9,640,64]{1,2,0:T(8,128)S(1)} fusion(bf16[256,640,1]{1,0,2:T(8,128)(2,1)} %bitcast.257, f32[9,64,256]{2,1,0:T(8,128)S(1)} %bitcast.254), kind=kOutput, calls=%fused_computation.3 | convolution fusion | flops 1132462080 | bytes 2392064 | tf_op jit(solution)/shard_map/dot_general | solution.py:166
  90.2 1.5 convolution_bitcast_fusion.1
  91.9 2.7 %copy.88 = f32[9,640,128]{2,1,0:T(8,128)} copy(f32[9,640,128]{1,2,0:T(8,128)S(1)} %pad_maximum_fusion) | data formatting | bytes 5898240 | tf_op jit(solution)/shard_map/concatenate | solution.py:235
  94.7 2.6 %reshape_reshape.3 = f32[32,180,128]{2,1,0:T(8,128)S(1)} reshape(f32[9,640,128]{2,1,0:T(8,128)} %copy.88) | data formatting | bytes 5898240 | tf_op jit(solution)/shard_map/reshape;reshape | solution.py:356
  98.2 1.9 %constant_dynamic-slice_fusion.5 = (f32[8,1,4,24,128]{4,3,2,1,0:T(8,128)}, f32[8,1,4,24,128]{4,3,2,1,0:T(8,128)S(1)}) fusion(f32[8,2,4,24,128]{4,3,2,1,0:T(8,128)} %bitcast.251, s32[]{:T(128)S(6)} %select_n.105, s32[]{:T(128)S(6)} %select_n.106), kind=kLoop, calls=%fused_computation.155 | loop fusion | bytes 1572872 | tf_op jit(solution)/shard_map/dynamic-slice
  100.9 1.7 %collective-permute-start = (f32[4,8,24,128]{3,2,1,0:T(8,128)}, f32[4,8,24,128]{3,2,1,0:T(8,128)}, u32[]{:S(2)}, u32[]{:S(2)}) collective-permute-start(f32[4,8,24,128]{3,2,1,0:T(8,128)} %bitcast.238), channel_id=1, source_target_pairs={{0,4},{4,0},{1,5},{5,1},{2,6},{6,2},{3,7},{7,3},{8,12},{12,8},{9,1... | collective-permute-start | bytes 1179656 | tf_op jit(solution)/shard_map/ppermute | solution.py:345
  102.6 1.7 pad_slice_fusion
  104.3 1.8 %constant_dynamic-slice_fusion.3 = (f32[24,2,1,24,128]{4,3,2,1,0:T(8,128)S(1)}, f32[24,2,1,24,128]{4,3,2,1,0:T(8,128)S(1)}, f32[24,2,1,24,128]{4,3,2,1,0:T(8,128)S(1)}, f32[24,2,1,24,128]{4,3,2,1,0:T(8,128)S(1)}) fusion(f32[24,2,4,24,128]{4,3,2,1,0:T(8,128)} %bitcast.241, s32[]{:T(128)S(6)} %select_n.107, s32[]{:T(128)S(6)} %select_n.109, ...), kind=kLoop, calls=%fused_computation.153 | loop fusion | bytes 4718608 | tf_op jit(solution)/shard_map/dynamic-slice.2
  108.7 12.0 %custom-call.9 = f32[2,64,64]{2,1,0:T(8,128)S(1)} custom-call(f32[2,64,64]{2,1,0:T(8,128)S(1)} %fusion.57), custom_call_target="Cholesky" | custom-call | tf_op jit(solution)/shard_map/jit(cholesky)/cholesky | solution.py:247
  120.9 9.8 %custom-call.10 = f32[2,1,64,64]{2,3,1,0:T(8,128)S(1)} custom-call(f32[2,1,64,64]{3,2,1,0:T(8,128)S(1)} %select_bitcast_fusion), custom_call_target="InvertDiagBlocksLowerTriangular" | custom-call | tf_op jit(solution)/shard_map/triangular_solve | solution.py:250
  133.4 2.9 %collective-permute-done.1 = f32[2,24,24,128]{3,2,1,0:T(8,128)} collective-permute-done((f32[2,24,24,128]{3,2,1,0:T(8,128)S(1)}, f32[2,24,24,128]{3,2,1,0:T(8,128)}, u32[]{:S(2)}, u32[]{:S(2)}) %collective-permute-start.1) | collective-permute-done | bytes 589856 | tf_op jit(solution)/shard_map/ppermute | solution.py:345
  136.3 1.5 fusion.32.refs_1_
  137.8 7.8 %shard_map.70 = (f32[4,8,24,128]{3,2,1,0:T(8,128)S(1)}, f32[2,24,24,128]{3,2,1,0:T(8,128)S(1)}) custom-call(f32[4,8,24,128]{3,2,1,0:T(8,128)S(1)} %fusion.33.refs_0_, f32[2,24,24,128]{3,2,1,0:T(8,128)S(1)} %fusion.32.refs_1_), custom_call_target="tpu_custom_call" | custom-call | tf_op jit(solution)/shard_map/pallas_call | solution.py:76
  145.7 12.9 %shard_map.71 = f32[32,24,128]{2,1,0:T(8,128)S(1)} custom-call(f32[32,24,128]{2,1,0:T(8,128)S(1)} %pad_maximum_fusion.4.refs_0_), custom_call_target="tpu_custom_call" | custom-call | tf_op jit(solution)/shard_map/pallas_call | solution.py:76
  158.7 10.3 %shard_map.72 = f32[8,24,128]{2,1,0:T(8,128)S(1)} custom-call(f32[24,128]{1,0:T(8,128)S(1)} %reduce_sum.29.refs_0_), custom_call_target="tpu_custom_call" | custom-call | tf_op jit(solution)/shard_map/pallas_call | solution.py:76
  (146 shorter events, 37.0 us)
Async XLA Ops:
  3.8 1.0 copy-start.7
  4.0 2.8 %copy-start.1 = (f32[5760,2,64]{0,2,1:T(8,128)S(1)}, f32[5760,2,64]{0,2,1:T(8,128)}, u32[]{:S(2)}) copy-start(f32[5760,2,64]{0,2,1:T(8,128)} %param.9) | copy-start | bytes 8847364
  15.1 13.8 %copy-start = (bf16[1,16,16,640]{3,2,1,0:T(8,128)(2,1)S(1)}, bf16[1,16,16,640]{3,2,1,0:T(8,128)(2,1)}, u32[]{:S(2)}) copy-start(bf16[1,16,16,640]{3,2,1,0:T(8,128)(2,1)} %param.7) | copy-start | bytes 983044
  29.5 4.5 %slice-start = ((s8[7372800]{0:T(1024)(128)(4,1)}), s8[4194304]{0:T(1024)(128)(4,1)S(1)}, s32[]{:S(2)}) async-start(s8[7372800]{0:T(1024)(128)(4,1)} %bitcast.242), calls=%async_computation | async-start | bytes 8388608
  29.8 1.2 copy-start.8
  29.9 4.2 %slice-start.1 = ((s8[7372800]{0:T(1024)(128)(4,1)}), s8[3178496]{0:T(1024)(128)(4,1)S(1)}, s32[]{:S(2)}) async-start(s8[7372800]{0:T(1024)(128)(4,1)} %bitcast.242), calls=%async_computation.1 | async-start | bytes 6356992
  37.4 1.1 copy-start.3
  38.5 1.0 copy-start.14
  38.5 1.1 copy-start.15
  38.5 1.2 copy-start.16
  38.5 1.2 copy-start.17
  38.5 1.2 copy-start.18
  38.5 1.2 copy-start.19
  38.5 1.3 copy-start.20
  79.9 1.1 copy-start.4
  83.8 2.1 %copy-start.9 = (f32[324,64]{1,0:T(8,128)S(1)}, f32[324,64]{1,0:T(8,128)}, u32[]{:S(2)}) copy-start(f32[324,64]{1,0:T(8,128)} %reshape.207) | copy-start | bytes 248836
  84.4 1.4 copy-start.10
  85.1 1.0 copy-start.11
  88.3 1.9 %copy-start.5 = (bf16[324,640,1]{1,0,2:T(8,128)(2,1)S(1)}, bf16[324,640,1]{1,0,2:T(8,128)(2,1)}, u32[]{:S(2)}) copy-start(bf16[324,640,1]{1,0,2:T(8,128)(2,1)} %reshape.231) | copy-start | bytes 1244164
  100.9 31.4 %collective-permute-start = (f32[4,8,24,128]{3,2,1,0:T(8,128)}, f32[4,8,24,128]{3,2,1,0:T(8,128)}, u32[]{:S(2)}, u32[]{:S(2)}) collective-permute-start(f32[4,8,24,128]{3,2,1,0:T(8,128)} %bitcast.238), channel_id=1, source_target_pairs={{0,4},{4,0},{1,5},{5,1},{2,6},{6,2},{3,7},{7,3},{8,12},{12,8},{9,1... | collective-permute-start | bytes 1179656 | tf_op jit(solution)/shard_map/ppermute | solution.py:345
  106.1 27.2 %collective-permute-start.3 = (f32[2,24,24,128]{3,2,1,0:T(8,128)S(1)}, f32[2,24,24,128]{3,2,1,0:T(8,128)}, u32[]{:S(2)}, u32[]{:S(2)}) collective-permute-start(f32[2,24,24,128]{3,2,1,0:T(8,128)S(1)} %bitcast.268), channel_id=1, source_target_pairs={{0,3},{1,0},{2,1},{3,2},{4,7},{5,4},{6,5},{7,6},{8,11},{9,8},{10,9... | collective-permute-start | bytes 1769480 | tf_op jit(solution)/shard_map/ppermute | solution.py:345
  106.7 25.6 %copy-start.6 = (f32[8,1,4,24,128]{4,3,2,1,0:T(8,128)S(1)}, f32[8,1,4,24,128]{4,3,2,1,0:T(8,128)}, u32[]{:S(2)}) copy-start(f32[8,1,4,24,128]{4,3,2,1,0:T(8,128)} %get-tuple-element.32) | copy-start | bytes 1179652
  106.7 26.6 %collective-permute-start.2 = (f32[2,24,24,128]{3,2,1,0:T(8,128)S(1)}, f32[2,24,24,128]{3,2,1,0:T(8,128)}, u32[]{:S(2)}, u32[]{:S(2)}) collective-permute-start(f32[2,24,24,128]{3,2,1,0:T(8,128)S(1)} %bitcast.269), channel_id=1, source_target_pairs={{0,2},{1,3},{2,0},{3,1},{4,6},{5,7},{6,4},{7,5},{8,10},{9,11},{10,... | collective-permute-start | bytes 1769480 | tf_op jit(solution)/shard_map/ppermute | solution.py:345
  107.7 28.6 %collective-permute-start.1 = (f32[2,24,24,128]{3,2,1,0:T(8,128)S(1)}, f32[2,24,24,128]{3,2,1,0:T(8,128)}, u32[]{:S(2)}, u32[]{:S(2)}) collective-permute-start(f32[2,24,24,128]{3,2,1,0:T(8,128)S(1)} %bitcast.270), channel_id=1, source_target_pairs={{0,1},{1,2},{2,3},{3,0},{4,5},{5,6},{6,7},{7,4},{8,9},{9,10},{10,1... | collective-permute-start | bytes 1769480 | tf_op jit(solution)/shard_map/ppermute | solution.py:345
  (3 other events, 2.7 us)

commit v14 on v13

--- a/solution.py
+++ b/solution.py
@@ -355,7 +355,7 @@
     lanes = math.prod(shape[1:])
     padded = jnp.pad(value.reshape(blocks, block_rows, lanes), ((0, 0), (0, piece_rows * group - block_rows), (0, 0)))
     pieces = padded.reshape(blocks, rows_n, cols_n, piece_rows, lanes)
-    half = blocks // 4
+    half = blocks * 5 // 16
     first = pieces[:half].transpose(1, 2, 0, 3, 4)
     second = pieces[half:].transpose(2, 1, 0, 3, 4)
     first, second = permute_sum(first, "row", sizes), permute_sum(second, "col", sizes)

time: 171 us -> 171 us (level)
  waiting for transfers between devices: 2.94 us -> 0.81 us
  Pallas kernels: 76 us -> 77.8 us
    ppermute x4, waiting for transfers between devices: 2.94 us -> 0.81 us  [permute_sum(): lax.ppermute(slab, axis, [(i, (i + shift) % n) for i in range(n)])]
    pallas_call x3, Pallas kernels: 31 us -> 32.9 us  [exchange_many(): pl.pallas_call(functools.partial(exchange_kernel, jobs=tuple(jobs), sizes...]
where the time goes in v14:
time: 171 us; the launch traced here: 170 us
  Pallas kernels  77.8 us (45%)
  local copies, waits for them, and re-layouts  40.2 us (24%)
  other arithmetic  31.7 us (19%)
  matrix products  14.3 us (8%)
  starting transfers between devices  3.57 us (2%)
    pallas_call x1, Pallas kernels, all_sum_small(): pl.pallas_call(functools.partial(allsum_kernel, sizes=sizes), out_shape=j...  35.2 us
    pallas_call x3, Pallas kernels, exchange_many(): pl.pallas_call(functools.partial(exchange_kernel, jobs=tuple(jobs), sizes...  32.9 us
    another operation x4, other arithmetic, on_device(): lower = jnp.linalg.cholesky(gram)  12.2 us
    another operation x3, other arithmetic, on_device(): lax.linalg.triangular_solve(lower, raw_part.transpose(1, 0, 2), left_side...  9.9 us
    pallas_call x1, Pallas kernels, padded_pair(): pl.pallas_call(functools.partial(halo_kernel, sizes=sizes), out_shape=tup...  9.81 us
    dot_general x8, matrix products, exact_dot(): lax.dot_general(left.astype(jnp.float32), right.astype(jnp.float32), (con...  8.51 us
    unnamed x53, local copies, waits for them, and re-layouts  7.63 us
    dot_general x9, matrix products, on_device(): lax.dot_general(window, conv_weight[a + 1, b + 1], (((1,), (1,)), ((), ()...  4.19 us
  transfers between devices with their start and end apart: 4, of which 1 were waited for; matrix products, arithmetic and copies ran while one was open for 17% of the time, Pallas kernels for 0%

profile of v14, /device:TPU:1, one launch (start us, length us, event | category | flops | bytes accessed | tf_op | source)
XLA Modules:
  0.0 169.9 jit_solution(5134284990541219483)
XLA Ops:
  0.6 1.5 copy.66
  2.1 1.5 copy.65
  6.8 2.6 %reshape.201 = f32[9,640,2,64]{1,0,3,2:T(8,128)} reshape(f32[5760,2,64]{0,2,1:T(8,128)S(1)} %copy-done.1) | data formatting | bytes 5898240 | tf_op jit(solution)/shard_map/reshape | solution.py:200
  9.3 2.9 %fusion.64 = (f32[1,640,9,64]{1,2,3,0:T(8,128)S(1)}, f32[1,640,9,64]{1,2,3,0:T(8,128)S(1)}) fusion(f32[2,640,9,64]{1,2,3,0:T(8,128)} %bitcast.240), kind=kLoop, calls=%fused_computation.161 | loop fusion | bytes 5898240 | tf_op jit(solution)/shard_map/slice | solution.py:202
  17.2 9.8 %shard_map.68 = (bf16[2,2,16,640]{3,2,1,0:T(8,128)(2,1)}, bf16[2,2,16,640]{3,2,1,0:T(8,128)(2,1)}, bf16[4,2,640]{2,1,0:T(2,128)(2,1)}) custom-call(bf16[2,2,16,640]{3,2,1,0:T(8,128)(2,1)} %copy.68.refs_0_, bf16[2,2,16,640]{3,2,1,0:T(8,128)(2,1)} %copy.69.refs_1_, bf16[4,2,640]{2,1,0:T(2,128)(2,1)} %pad_maximum_fusion.10.refs_2_), custom_call_target="tpu_custom_call" | custom-call | tf_op jit(solution)/shard_map/pallas_call | solution.py:130
  32.0 1.8 %fusion.63 = f32[18,18,576]{2,1,0:T(8,128)S(1)} fusion(f32[640,576,1]{0,1,2:T(8,128)S(1)} %bitcast.255, bf16[1,18,640]{2,1,0:T(8,128)(2,1)S(1)} %maximum_bitcast_fusion.7, bf16[16,1,640]{2,1,0:T(2,128)(2,1)S(1)} %copy.75, bf16[16,16,640]{2,1,0:T(8,128)(2,1)S(1)} %bitcast.261, bf16[16,1,640]{2,1,0:T(2,128)(2,1)S(1)} %copy.74, ...), kind=kOutput, calls=%fused_computation.160 | convolution fusion | flops 1435345920 | bytes 2635776 | tf_op jit(solution)/shard_map/dot_general | solution.py:166
  40.8 1.5 reshape.203.p_ref
  42.3 35.2 %shard_map.69 = f32[8,32,320]{2,1,0:T(8,128)} custom-call(f32[8,32,320]{2,1,0:T(8,128)} %reshape.203.p_ref), custom_call_target="tpu_custom_call" | custom-call | tf_op jit(solution)/shard_map/pallas_call | solution.py:319
  77.5 1.4 reshape.204
  86.1 1.9 %concatenate.64 = f32[324,576]{1,0:T(8,128)S(1)} concatenate(f32[324,64]{1,0:T(8,128)S(1)} %reshape.206, f32[324,64]{1,0:T(8,128)S(1)} %copy-done.9, f32[324,64]{1,0:T(8,128)S(1)} %copy-done.10, f32[324,64]{1,0:T(8,128)S(1)} %copy-done.11, f32[324,64]{1,0:T(8,128)} %reshape.210, f32[324,64]{1,0:T(8,128)} %reshape.211, f32[324,64]{1,0:T(8,128)S(1)} %reshape.212, ...), dimensions={1} | concatenate | bytes 1492992 | tf_op jit(solution)/shard_map/concatenate | solution.py:218
  88.3 1.9 %convolution_bitcast_fusion = f32[9,640,64]{1,2,0:T(8,128)S(1)} fusion(bf16[256,640,1]{1,0,2:T(8,128)(2,1)} %bitcast.257, f32[9,64,256]{2,1,0:T(8,128)S(1)} %bitcast.254), kind=kOutput, calls=%fused_computation.3 | convolution fusion | flops 1132462080 | bytes 2392064 | tf_op jit(solution)/shard_map/dot_general | solution.py:166
  90.2 1.5 convolution_bitcast_fusion.1
  91.9 2.7 %copy.88 = f32[9,640,128]{2,1,0:T(8,128)} copy(f32[9,640,128]{1,2,0:T(8,128)S(1)} %pad_maximum_fusion) | data formatting | bytes 5898240 | tf_op jit(solution)/shard_map/concatenate | solution.py:235
  94.7 2.6 %reshape_reshape.3 = f32[32,180,128]{2,1,0:T(8,128)S(1)} reshape(f32[9,640,128]{2,1,0:T(8,128)} %copy.88) | data formatting | bytes 5898240 | tf_op jit(solution)/shard_map/reshape;reshape | solution.py:356
  98.3 2.0 %constant_dynamic-slice_fusion.5 = (f32[10,1,4,24,128]{4,3,2,1,0:T(8,128)}, f32[10,1,4,24,128]{4,3,2,1,0:T(8,128)S(1)}) fusion(f32[10,2,4,24,128]{4,3,2,1,0:T(8,128)} %bitcast.249, s32[]{:T(128)S(6)} %select_n.105, s32[]{:T(128)S(6)} %select_n.106), kind=kLoop, calls=%fused_computation.155 | loop fusion | bytes 1966088 | tf_op jit(solution)/shard_map/dynamic-slice
  101.2 1.7 %collective-permute-start = (f32[4,10,24,128]{3,2,1,0:T(8,128)}, f32[4,10,24,128]{3,2,1,0:T(8,128)}, u32[]{:S(2)}, u32[]{:S(2)}) collective-permute-start(f32[4,10,24,128]{3,2,1,0:T(8,128)} %bitcast.238), channel_id=1, source_target_pairs={{0,4},{4,0},{1,5},{5,1},{2,6},{6,2},{3,7},{7,3},{8,12},{12,8},{9,1... | collective-permute-start | bytes 1474568 | tf_op jit(solution)/shard_map/ppermute | solution.py:345
  102.9 1.6 pad_slice_fusion
  104.5 1.7 constant_dynamic-slice_fusion.3
  108.8 12.0 %custom-call.9 = f32[2,64,64]{2,1,0:T(8,128)S(1)} custom-call(f32[2,64,64]{2,1,0:T(8,128)S(1)} %fusion.57), custom_call_target="Cholesky" | custom-call | tf_op jit(solution)/shard_map/jit(cholesky)/cholesky | solution.py:247
  121.8 9.8 %custom-call.10 = f32[2,1,64,64]{2,3,1,0:T(8,128)S(1)} custom-call(f32[2,1,64,64]{3,2,1,0:T(8,128)S(1)} %select_bitcast_fusion), custom_call_target="InvertDiagBlocksLowerTriangular" | custom-call | tf_op jit(solution)/shard_map/triangular_solve | solution.py:250
  134.3 1.5 fusion.32.refs_1_
  135.8 9.6 %shard_map.70 = (f32[4,10,24,128]{3,2,1,0:T(8,128)S(1)}, f32[2,22,24,128]{3,2,1,0:T(8,128)S(1)}) custom-call(f32[4,10,24,128]{3,2,1,0:T(8,128)S(1)} %fusion.33.refs_0_, f32[2,22,24,128]{3,2,1,0:T(8,128)S(1)} %fusion.32.refs_1_), custom_call_target="tpu_custom_call" | custom-call | tf_op jit(solution)/shard_map/pallas_call | solution.py:76
  145.5 13.1 %shard_map.71 = f32[32,24,128]{2,1,0:T(8,128)S(1)} custom-call(f32[32,24,128]{2,1,0:T(8,128)S(1)} %pad_maximum_fusion.4.refs_0_), custom_call_target="tpu_custom_call" | custom-call | tf_op jit(solution)/shard_map/pallas_call | solution.py:76
  158.7 10.1 %shard_map.72 = f32[8,24,128]{2,1,0:T(8,128)S(1)} custom-call(f32[24,128]{1,0:T(8,128)S(1)} %reduce_sum.29.refs_0_), custom_call_target="tpu_custom_call" | custom-call | tf_op jit(solution)/shard_map/pallas_call | solution.py:76
  (146 shorter events, 36.6 us)
Async XLA Ops:
  3.8 1.0 copy-start.7
  4.0 2.8 %copy-start.1 = (f32[5760,2,64]{0,2,1:T(8,128)S(1)}, f32[5760,2,64]{0,2,1:T(8,128)}, u32[]{:S(2)}) copy-start(f32[5760,2,64]{0,2,1:T(8,128)} %param.9) | copy-start | bytes 8847364
  15.1 13.8 %copy-start = (bf16[1,16,16,640]{3,2,1,0:T(8,128)(2,1)S(1)}, bf16[1,16,16,640]{3,2,1,0:T(8,128)(2,1)}, u32[]{:S(2)}) copy-start(bf16[1,16,16,640]{3,2,1,0:T(8,128)(2,1)} %param.7) | copy-start | bytes 983044
  29.5 4.5 %slice-start = ((s8[7372800]{0:T(1024)(128)(4,1)}), s8[4194304]{0:T(1024)(128)(4,1)S(1)}, s32[]{:S(2)}) async-start(s8[7372800]{0:T(1024)(128)(4,1)} %bitcast.242), calls=%async_computation | async-start | bytes 8388608
  29.8 1.2 copy-start.8
  29.9 4.2 %slice-start.1 = ((s8[7372800]{0:T(1024)(128)(4,1)}), s8[3178496]{0:T(1024)(128)(4,1)S(1)}, s32[]{:S(2)}) async-start(s8[7372800]{0:T(1024)(128)(4,1)} %bitcast.242), calls=%async_computation.1 | async-start | bytes 6356992
  37.4 1.1 copy-start.3
  38.5 1.0 copy-start.14
  38.5 1.1 copy-start.15
  38.5 1.2 copy-start.16
  38.5 1.2 copy-start.17
  38.5 1.2 copy-start.18
  38.5 1.2 copy-start.19
  38.5 1.3 copy-start.20
  79.9 1.1 copy-start.4
  83.8 2.1 %copy-start.9 = (f32[324,64]{1,0:T(8,128)S(1)}, f32[324,64]{1,0:T(8,128)}, u32[]{:S(2)}) copy-start(f32[324,64]{1,0:T(8,128)} %reshape.207) | copy-start | bytes 248836
  84.4 1.4 copy-start.10
  85.1 1.0 copy-start.11
  88.3 1.9 %copy-start.6 = (bf16[324,640,1]{1,0,2:T(8,128)(2,1)S(1)}, bf16[324,640,1]{1,0,2:T(8,128)(2,1)}, u32[]{:S(2)}) copy-start(bf16[324,640,1]{1,0,2:T(8,128)(2,1)} %reshape.231) | copy-start | bytes 1244164
  101.2 31.2 %collective-permute-start = (f32[4,10,24,128]{3,2,1,0:T(8,128)}, f32[4,10,24,128]{3,2,1,0:T(8,128)}, u32[]{:S(2)}, u32[]{:S(2)}) collective-permute-start(f32[4,10,24,128]{3,2,1,0:T(8,128)} %bitcast.238), channel_id=1, source_target_pairs={{0,4},{4,0},{1,5},{5,1},{2,6},{6,2},{3,7},{7,3},{8,12},{12,8},{9,1... | collective-permute-start | bytes 1474568 | tf_op jit(solution)/shard_map/ppermute | solution.py:345
  106.3 27.2 %collective-permute-start.3 = (f32[2,22,24,128]{3,2,1,0:T(8,128)S(1)}, f32[2,22,24,128]{3,2,1,0:T(8,128)}, u32[]{:S(2)}, u32[]{:S(2)}) collective-permute-start(f32[2,22,24,128]{3,2,1,0:T(8,128)S(1)} %bitcast.268), channel_id=1, source_target_pairs={{0,3},{1,0},{2,1},{3,2},{4,7},{5,4},{6,5},{7,6},{8,11},{9,8},{10,9... | collective-permute-start | bytes 1622024 | tf_op jit(solution)/shard_map/ppermute | solution.py:345
  106.8 25.6 %copy-start.5 = (f32[10,1,4,24,128]{4,3,2,1,0:T(8,128)S(1)}, f32[10,1,4,24,128]{4,3,2,1,0:T(8,128)}, u32[]{:S(2)}) copy-start(f32[10,1,4,24,128]{4,3,2,1,0:T(8,128)} %get-tuple-element.32) | copy-start | bytes 1474564
  106.8 26.7 %collective-permute-start.2 = (f32[2,22,24,128]{3,2,1,0:T(8,128)S(1)}, f32[2,22,24,128]{3,2,1,0:T(8,128)}, u32[]{:S(2)}, u32[]{:S(2)}) collective-permute-start(f32[2,22,24,128]{3,2,1,0:T(8,128)S(1)} %bitcast.269), channel_id=1, source_target_pairs={{0,2},{1,3},{2,0},{3,1},{4,6},{5,7},{6,4},{7,5},{8,10},{9,11},{10,... | collective-permute-start | bytes 1622024 | tf_op jit(solution)/shard_map/ppermute | solution.py:345
  107.8 26.5 %collective-permute-start.1 = (f32[2,22,24,128]{3,2,1,0:T(8,128)S(1)}, f32[2,22,24,128]{3,2,1,0:T(8,128)}, u32[]{:S(2)}, u32[]{:S(2)}) collective-permute-start(f32[2,22,24,128]{3,2,1,0:T(8,128)S(1)} %bitcast.270), channel_id=1, source_target_pairs={{0,1},{1,2},{2,3},{3,0},{4,5},{5,6},{6,7},{7,4},{8,9},{9,10},{10,1... | collective-permute-start | bytes 1622024 | tf_op jit(solution)/shard_map/ppermute | solution.py:345
  (3 other events, 2.7 us)
